TPU v7x, 256 devices: a whole 4x4x8 slice. The times are simulated.
256 devices in a mesh: mesh: 16 (over x_hi, y, core), tm: 16 (over z, x_lo).
Axes of the slice: x: 4 (x_hi: 2, x_lo: 2; x = x_hi * 2 + x_lo), y: 4, z: 8, core: 2. Of those that a mesh axis runs over, the one named last changes fastest.
Arguments:
- slice_start: float32 [16, 64, 128, 128], P('tm', 'mesh'), may hold values from -4 to 4
- conductivity: float32 [64, 128, 128], P('mesh'), may hold values from 0.5 to 2
- coil_current: float32 [64, 128, 128], P('mesh'), may hold values from -6 to 6
- switching: int32 [64], P('tm'), may hold values from -1 to 1
- loss_coeffs: float32 [3, 64, 128, 128], P(None, 'mesh', 'tm'), may hold values from 0.5 to 2
Outputs:
- next_start: float32 [16, 64, 128, 128], P('tm', 'mesh')
- loss_density: float32 [64, 128, 128], P('mesh', 'tm')
All inputs are finite; a program needn't handle non-finite values.
Results may differ from a plain program's by a relative error of at most 0.000086.
Values sent between devices are 32-bit elements; how exact they have to be, the bound alone decides.
No kernel may reach another device: no remote copies, remote signals or barrier semaphores. Data moves between devices by JAX's collectives and lax.ppermute only.
A program may use at most 128 MiB of HBM per device.

v0:
```python
import jax
import jax.numpy as jnp
from jax import lax
from jax.sharding import PartitionSpec as P

STEPS = 4
SWEEPS = 5
CSWEEPS = 2


time_step = 0.25


def with_halo(block, sides, width):
    for axis, dim in sides:
        count = lax.axis_size(axis)
        forward = [(i, i + 1) for i in range(count - 1)]
        backward = [(target, source) for source, target in forward]
        low = lax.ppermute(
            lax.slice_in_dim(block, block.shape[dim] - width, None, axis=dim), axis, forward
        )
        high = lax.ppermute(lax.slice_in_dim(block, 0, width, axis=dim), axis, backward)
        block = jnp.concatenate([low, block, high], axis=dim)
    return block


def from_behind(block, axis, distance):
    devices = range(lax.axis_size(axis))
    route = [((i - distance) % len(devices), i) for i in devices]
    return lax.ppermute(block, axis, route)


def passed_along(value, axis, steps):
    count = lax.axis_size(axis)
    leading, last = (max(0, -steps), min(count, count - steps))
    return lax.ppermute(value, axis, [(source, source + steps) for source in range(leading, last)])


def chebyshev(apply_op, rhs, scale, sweeps):
    upper = 2.0 + 12.0 * scale
    center = (upper + 0.5) / 2.0
    radius = (upper - 0.5) / 2.0
    ratio = center / radius
    weight = 1.0 / ratio
    update = rhs / center
    result = update
    residual = rhs
    for sweep_index in range(sweeps):
        residual = residual - apply_op(update, scale)
        weight_next = 1.0 / (2.0 * ratio - weight)
        update = weight_next * weight * update + 2.0 * weight_next / radius * residual
        result = result + update
        weight = weight_next
    return result


def z_difference(field):
    inner = field[..., 1:] - field[..., :-1]
    return jnp.concatenate([inner, jnp.zeros_like(field[..., :1])], axis=-1)


def dft_table(sample_times, total, harmonics):
    orders = jnp.arange(1, harmonics + 1, dtype=jnp.int32)
    product = orders[:, None] * sample_times[None, :] % total
    angle = 2.0 * jnp.pi / total * product.astype(jnp.float32)
    return jnp.concatenate([jnp.cos(angle), -jnp.sin(angle)], axis=0)


def core_loss(spectrum, loss_coeffs, total):
    harmonics = total // 2
    real_part = spectrum[:harmonics]
    imag_part = spectrum[harmonics:]
    power = (real_part * real_part + imag_part * imag_part) * (2.0 / total) ** 2
    freq = (jnp.arange(1, harmonics + 1, dtype=jnp.int32).astype(jnp.float32) / harmonics).reshape(
        -1, 1, 1, 1
    )
    terms = loss_coeffs[0] * freq * power + loss_coeffs[1] * (freq * freq) * power
    terms = terms + loss_coeffs[2] * freq**1.5 * power**0.75
    return jnp.sum(terms, axis=0)


def on_device(slice_start, conductivity, coil_current, switching, loss_coeffs):

    def apply_op(field, scale):
        padded = with_halo(field, (("mesh", 0),), 1)
        padded = jnp.pad(padded, ((0, 0), (1, 1), (1, 1)))
        beside = padded[2:, 1:-1, 1:-1] + padded[:-2, 1:-1, 1:-1]
        beside = beside + padded[1:-1, 2:, 1:-1] + padded[1:-1, :-2, 1:-1]
        beside = beside + padded[1:-1, 1:-1, 2:] + padded[1:-1, 1:-1, :-2]
        return conductivity * field + scale * (6.0 * field - beside)

    def coarse(field):
        return chebyshev(apply_op, conductivity * field, 4.0 * time_step, CSWEEPS)

    slice_count = lax.axis_size("tm")
    slice_index = lax.axis_index("tm")
    total = STEPS * slice_count
    initial = slice_start[0]
    state = initial
    fluxes = []
    for step_index in range(STEPS):
        level = switching[step_index].astype(jnp.float32)
        rhs = conductivity * state + time_step * level * coil_current
        state = chebyshev(apply_op, rhs, time_step, SWEEPS)
        fluxes.append(z_difference(state))
    jump = state - coarse(initial)
    outgoing = jnp.where(slice_index == slice_count - 1, state, jump)
    entry = from_behind(outgoing, "tm", 1)

    def one_turn(turn_index, current):
        moved = passed_along(current, "tm", 1)
        return entry + coarse(moved)

    current = lax.fori_loop(0, slice_count - 1, one_turn, entry)
    next_start = current[None]
    flux = jnp.stack(fluxes, axis=0)
    gathered = lax.all_to_all(flux, "tm", split_axis=2, concat_axis=0, tiled=True)
    table = dft_table(jnp.arange(total, dtype=jnp.int32), total, total // 2)
    spectrum = jnp.einsum("kt,txyz->kxyz", table, gathered, precision=lax.Precision.HIGHEST)
    loss_density = core_loss(spectrum, loss_coeffs, total)
    return (next_start, loss_density)


def solution(mesh):
    placed = (
        P("tm", "mesh", None, None),
        P("mesh", None, None),
        P("mesh", None, None),
        P("tm"),
        P(None, "mesh", "tm", None),
    )
    return jax.shard_map(
        on_device,
        mesh=mesh,
        in_specs=placed,
        out_specs=(P("tm", "mesh", None, None), P("mesh", "tm", None)),
        check_vma=False,
    )
```

profile of v0, /device:TPU:132, one launch (start us, length us, event | category | flops | bytes accessed | tf_op | source)
XLA Modules:
  0.0 847.8 jit_solution(6531851841816018939)
XLA Ops:
  291.1 8.9 %all-to-all-start = ((f32[4,4,128,128]{3,1,0,2:T(4,128)}), f32[4,4,128,128]{3,1,0,2:T(4,128)S(1)}, u32[]{:S(2)}, u32[]{:S(2)}) async-start(f32[4,4,128,128]{3,1,0,2:T(4,128)} %pad_maximum_fusion.4), calls=%async_computation | async-start | bytes 2097152 | tf_op jit(solution)/shard_map/all_to_all | solution.py:117
  301.7 22.8 %collective-permute-done.49 = f32[4,128,128]{2,0,1:T(4,128)S(1)} collective-permute-done((f32[4,128,128]{2,0,1:T(4,128)S(1)}, f32[4,128,128]{2,0,1:T(4,128)S(1)}, u32[]{:S(2)}, u32[]{:S(2)}) %collective-permute-start.49) | collective-permute-done | bytes 262176 | tf_op jit(solution)/shard_map/ppermute | solution.py:30
  327.1 519.8 %while.12 = (s32[]{:T(128)}, f32[4,128,128]{2,1,0:T(8,128)S(1)}, f32[4,128,128]{2,1,0:T(8,128)S(1)}, f32[4,128,128]{2,1,0:T(8,128)S(1)}, s32[]{:T(128)}) while((s32[]{:T(128)}, f32[4,128,128]{2,1,0:T(8,128)S(1)}, f32[4,128,128]{2,1,0:T(8,128)S(1)}, f32[4,128,128]{2,1,0:T(8,128)S(1)}, s32[]{:T(128)}) %tuple.104), condition=%wide.region_1.2_spmd, body=%wide.region_0.1_spmd.sunk | while | flops 5401298 | bytes 10510789 | solution.py:114
  329.0 8.4 collective-permute-done
  353.7 7.5 collective-permute-done.4
  363.8 8.4 collective-permute-done
  388.4 7.5 collective-permute-done.4
  398.4 8.4 collective-permute-done
  423.1 7.5 collective-permute-done.4
  433.1 8.4 collective-permute-done
  457.8 7.5 collective-permute-done.4
  467.8 8.4 collective-permute-done
  492.5 7.5 collective-permute-done.4
  502.5 8.4 collective-permute-done
  527.2 7.5 collective-permute-done.4
  537.2 8.4 collective-permute-done
  561.9 7.5 collective-permute-done.4
  571.9 8.4 collective-permute-done
  596.6 7.5 collective-permute-done.4
  606.6 8.4 collective-permute-done
  631.3 7.5 collective-permute-done.4
  641.3 8.4 collective-permute-done
  666.0 7.5 collective-permute-done.4
  676.0 8.4 collective-permute-done
  700.7 7.5 collective-permute-done.4
  710.7 8.4 collective-permute-done
  735.3 7.5 collective-permute-done.4
  745.4 8.4 collective-permute-done
  770.0 7.5 collective-permute-done.4
  780.1 8.4 collective-permute-done
  804.7 7.5 collective-permute-done.4
  814.8 8.4 collective-permute-done
  (410 shorter events, 578.6 us)
Async XLA Ops:
  203.9 13.2 %collective-permute-start.33 = (f32[1,128,128]{2,0,1:T(1,128)S(1)}, f32[1,128,128]{2,0,1:T(1,128)S(1)}, u32[]{:S(2)}, u32[]{:S(2)}) collective-permute-start(f32[1,128,128]{2,0,1:T(1,128)S(1)} %get-tuple-element.138), channel_id=1, source_target_pairs={{16,0},{32,16},{48,32},{64,48},{80,64},{96,80},{112,96},{128,112},... | collective-permute-start | bytes 196616 | tf_op jit(solution)/shard_map/ppermute | solution.py:22
  205.8 11.2 %collective-permute-start.34 = (f32[1,128,128]{2,0,1:T(1,128)S(1)}, f32[1,128,128]{2,0,1:T(1,128)S(1)}, u32[]{:S(2)}, u32[]{:S(2)}) collective-permute-start(f32[1,128,128]{2,0,1:T(1,128)S(1)} %get-tuple-element.137), channel_id=1, source_target_pairs={{0,16},{16,32},{32,48},{48,64},{64,80},{80,96},{96,112},{112,128},... | collective-permute-start | bytes 196616 | tf_op jit(solution)/shard_map/ppermute | solution.py:19
  208.4 20.4 %collective-permute-start.47 = (f32[1,128,128]{2,0,1:T(1,128)S(1)}, f32[1,128,128]{2,0,1:T(1,128)S(1)}, u32[]{:S(2)}, u32[]{:S(2)}) collective-permute-start(f32[1,128,128]{2,0,1:T(1,128)S(1)} %get-tuple-element.168), channel_id=1, source_target_pairs={{16,0},{32,16},{48,32},{64,48},{80,64},{96,80},{112,96},{128,112},... | collective-permute-start | bytes 196616 | tf_op jit(solution)/shard_map/ppermute | solution.py:22
  215.1 13.6 %collective-permute-start.48 = (f32[1,128,128]{2,0,1:T(1,128)S(1)}, f32[1,128,128]{2,0,1:T(1,128)S(1)}, u32[]{:S(2)}, u32[]{:S(2)}) collective-permute-start(f32[1,128,128]{2,0,1:T(1,128)S(1)} %get-tuple-element.167), channel_id=1, source_target_pairs={{0,16},{16,32},{32,48},{48,64},{64,80},{80,96},{96,112},{112,128},... | collective-permute-start | bytes 196616 | tf_op jit(solution)/shard_map/ppermute | solution.py:19
  219.1 10.5 %collective-permute-start.35 = (f32[1,128,128]{2,0,1:T(1,128)S(1)}, f32[1,128,128]{2,0,1:T(1,128)S(1)}, u32[]{:S(2)}, u32[]{:S(2)}) collective-permute-start(f32[1,128,128]{2,0,1:T(1,128)S(1)} %get-tuple-element.136), channel_id=1, source_target_pairs={{16,0},{32,16},{48,32},{64,48},{80,64},{96,80},{112,96},{128,112},... | collective-permute-start | bytes 196616 | tf_op jit(solution)/shard_map/ppermute | solution.py:22
  291.1 33.5 %all-to-all-start = ((f32[4,4,128,128]{3,1,0,2:T(4,128)}), f32[4,4,128,128]{3,1,0,2:T(4,128)S(1)}, u32[]{:S(2)}, u32[]{:S(2)}) async-start(f32[4,4,128,128]{3,1,0,2:T(4,128)} %pad_maximum_fusion.4), calls=%async_computation | async-start | bytes 2097152 | tf_op jit(solution)/shard_map/all_to_all | solution.py:117
  300.1 24.4 %collective-permute-start.49 = (f32[4,128,128]{2,0,1:T(4,128)S(1)}, f32[4,128,128]{2,0,1:T(4,128)S(1)}, u32[]{:S(2)}, u32[]{:S(2)}) collective-permute-start(f32[4,128,128]{2,0,1:T(4,128)S(1)} %get-tuple-element.74), channel_id=1, source_target_pairs={{15,0},{0,1},{1,2},{2,3},{3,4},{4,5},{5,6},{6,7},{7,8},{8,9},{9,10... | collective-permute-start | bytes 786440 | tf_op jit(solution)/shard_map/ppermute | solution.py:30
  327.1 10.4 %collective-permute-start = (f32[4,128,128]{2,1,0:T(8,128)S(1)}, f32[4,128,128]{2,1,0:T(8,128)S(1)}, u32[]{:S(2)}, u32[]{:S(2)}) collective-permute-start(f32[4,128,128]{2,1,0:T(8,128)S(1)} %get-tuple-element.233), channel_id=1, source_target_pairs={{0,1},{1,2},{2,3},{3,4},{4,5},{5,6},{6,7},{7,8},{8,9},{9,10},{10,1... | collective-permute-start | bytes 786440 | tf_op jit(solution)/shard_map/while/body/eval_jaxpr/ppermute | solution.py:36
  351.3 9.9 %collective-permute-start.4 = (f32[1,128,128]{2,1,0:T(8,128)S(1)}, f32[1,128,128]{2,1,0:T(8,128)S(1)}, u32[]{:S(2)}, u32[]{:S(2)}) collective-permute-start(f32[1,128,128]{2,1,0:T(8,128)S(1)} %get-tuple-element.226), channel_id=1, source_target_pairs={{0,16},{16,32},{32,48},{48,64},{64,80},{80,96},{96,112},{112,128},... | collective-permute-start | bytes 196616 | tf_op jit(solution)/shard_map/while/body/eval_jaxpr/ppermute | solution.py:19
  361.8 10.4 %collective-permute-start = (f32[4,128,128]{2,1,0:T(8,128)S(1)}, f32[4,128,128]{2,1,0:T(8,128)S(1)}, u32[]{:S(2)}, u32[]{:S(2)}) collective-permute-start(f32[4,128,128]{2,1,0:T(8,128)S(1)} %get-tuple-element.233), channel_id=1, source_target_pairs={{0,1},{1,2},{2,3},{3,4},{4,5},{5,6},{6,7},{7,8},{8,9},{9,10},{10,1... | collective-permute-start | bytes 786440 | tf_op jit(solution)/shard_map/while/body/eval_jaxpr/ppermute | solution.py:36
  386.0 9.9 %collective-permute-start.4 = (f32[1,128,128]{2,1,0:T(8,128)S(1)}, f32[1,128,128]{2,1,0:T(8,128)S(1)}, u32[]{:S(2)}, u32[]{:S(2)}) collective-permute-start(f32[1,128,128]{2,1,0:T(8,128)S(1)} %get-tuple-element.226), channel_id=1, source_target_pairs={{0,16},{16,32},{32,48},{48,64},{64,80},{80,96},{96,112},{112,128},... | collective-permute-start | bytes 196616 | tf_op jit(solution)/shard_map/while/body/eval_jaxpr/ppermute | solution.py:19
  396.5 10.4 %collective-permute-start = (f32[4,128,128]{2,1,0:T(8,128)S(1)}, f32[4,128,128]{2,1,0:T(8,128)S(1)}, u32[]{:S(2)}, u32[]{:S(2)}) collective-permute-start(f32[4,128,128]{2,1,0:T(8,128)S(1)} %get-tuple-element.233), channel_id=1, source_target_pairs={{0,1},{1,2},{2,3},{3,4},{4,5},{5,6},{6,7},{7,8},{8,9},{9,10},{10,1... | collective-permute-start | bytes 786440 | tf_op jit(solution)/shard_map/while/body/eval_jaxpr/ppermute | solution.py:36
  420.7 9.9 %collective-permute-start.4 = (f32[1,128,128]{2,1,0:T(8,128)S(1)}, f32[1,128,128]{2,1,0:T(8,128)S(1)}, u32[]{:S(2)}, u32[]{:S(2)}) collective-permute-start(f32[1,128,128]{2,1,0:T(8,128)S(1)} %get-tuple-element.226), channel_id=1, source_target_pairs={{0,16},{16,32},{32,48},{48,64},{64,80},{80,96},{96,112},{112,128},... | collective-permute-start | bytes 196616 | tf_op jit(solution)/shard_map/while/body/eval_jaxpr/ppermute | solution.py:19
  431.2 10.4 %collective-permute-start = (f32[4,128,128]{2,1,0:T(8,128)S(1)}, f32[4,128,128]{2,1,0:T(8,128)S(1)}, u32[]{:S(2)}, u32[]{:S(2)}) collective-permute-start(f32[4,128,128]{2,1,0:T(8,128)S(1)} %get-tuple-element.233), channel_id=1, source_target_pairs={{0,1},{1,2},{2,3},{3,4},{4,5},{5,6},{6,7},{7,8},{8,9},{9,10},{10,1... | collective-permute-start | bytes 786440 | tf_op jit(solution)/shard_map/while/body/eval_jaxpr/ppermute | solution.py:36
  455.4 9.9 %collective-permute-start.4 = (f32[1,128,128]{2,1,0:T(8,128)S(1)}, f32[1,128,128]{2,1,0:T(8,128)S(1)}, u32[]{:S(2)}, u32[]{:S(2)}) collective-permute-start(f32[1,128,128]{2,1,0:T(8,128)S(1)} %get-tuple-element.226), channel_id=1, source_target_pairs={{0,16},{16,32},{32,48},{48,64},{64,80},{80,96},{96,112},{112,128},... | collective-permute-start | bytes 196616 | tf_op jit(solution)/shard_map/while/body/eval_jaxpr/ppermute | solution.py:19
  465.9 10.4 %collective-permute-start = (f32[4,128,128]{2,1,0:T(8,128)S(1)}, f32[4,128,128]{2,1,0:T(8,128)S(1)}, u32[]{:S(2)}, u32[]{:S(2)}) collective-permute-start(f32[4,128,128]{2,1,0:T(8,128)S(1)} %get-tuple-element.233), channel_id=1, source_target_pairs={{0,1},{1,2},{2,3},{3,4},{4,5},{5,6},{6,7},{7,8},{8,9},{9,10},{10,1... | collective-permute-start | bytes 786440 | tf_op jit(solution)/shard_map/while/body/eval_jaxpr/ppermute | solution.py:36
  490.1 9.9 %collective-permute-start.4 = (f32[1,128,128]{2,1,0:T(8,128)S(1)}, f32[1,128,128]{2,1,0:T(8,128)S(1)}, u32[]{:S(2)}, u32[]{:S(2)}) collective-permute-start(f32[1,128,128]{2,1,0:T(8,128)S(1)} %get-tuple-element.226), channel_id=1, source_target_pairs={{0,16},{16,32},{32,48},{48,64},{64,80},{80,96},{96,112},{112,128},... | collective-permute-start | bytes 196616 | tf_op jit(solution)/shard_map/while/body/eval_jaxpr/ppermute | solution.py:19
  500.6 10.4 %collective-permute-start = (f32[4,128,128]{2,1,0:T(8,128)S(1)}, f32[4,128,128]{2,1,0:T(8,128)S(1)}, u32[]{:S(2)}, u32[]{:S(2)}) collective-permute-start(f32[4,128,128]{2,1,0:T(8,128)S(1)} %get-tuple-element.233), channel_id=1, source_target_pairs={{0,1},{1,2},{2,3},{3,4},{4,5},{5,6},{6,7},{7,8},{8,9},{9,10},{10,1... | collective-permute-start | bytes 786440 | tf_op jit(solution)/shard_map/while/body/eval_jaxpr/ppermute | solution.py:36
  524.7 9.9 %collective-permute-start.4 = (f32[1,128,128]{2,1,0:T(8,128)S(1)}, f32[1,128,128]{2,1,0:T(8,128)S(1)}, u32[]{:S(2)}, u32[]{:S(2)}) collective-permute-start(f32[1,128,128]{2,1,0:T(8,128)S(1)} %get-tuple-element.226), channel_id=1, source_target_pairs={{0,16},{16,32},{32,48},{48,64},{64,80},{80,96},{96,112},{112,128},... | collective-permute-start | bytes 196616 | tf_op jit(solution)/shard_map/while/body/eval_jaxpr/ppermute | solution.py:19
  535.3 10.4 %collective-permute-start = (f32[4,128,128]{2,1,0:T(8,128)S(1)}, f32[4,128,128]{2,1,0:T(8,128)S(1)}, u32[]{:S(2)}, u32[]{:S(2)}) collective-permute-start(f32[4,128,128]{2,1,0:T(8,128)S(1)} %get-tuple-element.233), channel_id=1, source_target_pairs={{0,1},{1,2},{2,3},{3,4},{4,5},{5,6},{6,7},{7,8},{8,9},{9,10},{10,1... | collective-permute-start | bytes 786440 | tf_op jit(solution)/shard_map/while/body/eval_jaxpr/ppermute | solution.py:36
  559.4 9.9 %collective-permute-start.4 = (f32[1,128,128]{2,1,0:T(8,128)S(1)}, f32[1,128,128]{2,1,0:T(8,128)S(1)}, u32[]{:S(2)}, u32[]{:S(2)}) collective-permute-start(f32[1,128,128]{2,1,0:T(8,128)S(1)} %get-tuple-element.226), channel_id=1, source_target_pairs={{0,16},{16,32},{32,48},{48,64},{64,80},{80,96},{96,112},{112,128},... | collective-permute-start | bytes 196616 | tf_op jit(solution)/shard_map/while/body/eval_jaxpr/ppermute | solution.py:19
  570.0 10.4 %collective-permute-start = (f32[4,128,128]{2,1,0:T(8,128)S(1)}, f32[4,128,128]{2,1,0:T(8,128)S(1)}, u32[]{:S(2)}, u32[]{:S(2)}) collective-permute-start(f32[4,128,128]{2,1,0:T(8,128)S(1)} %get-tuple-element.233), channel_id=1, source_target_pairs={{0,1},{1,2},{2,3},{3,4},{4,5},{5,6},{6,7},{7,8},{8,9},{9,10},{10,1... | collective-permute-start | bytes 786440 | tf_op jit(solution)/shard_map/while/body/eval_jaxpr/ppermute | solution.py:36
  594.1 9.9 %collective-permute-start.4 = (f32[1,128,128]{2,1,0:T(8,128)S(1)}, f32[1,128,128]{2,1,0:T(8,128)S(1)}, u32[]{:S(2)}, u32[]{:S(2)}) collective-permute-start(f32[1,128,128]{2,1,0:T(8,128)S(1)} %get-tuple-element.226), channel_id=1, source_target_pairs={{0,16},{16,32},{32,48},{48,64},{64,80},{80,96},{96,112},{112,128},... | collective-permute-start | bytes 196616 | tf_op jit(solution)/shard_map/while/body/eval_jaxpr/ppermute | solution.py:19
  604.7 10.4 %collective-permute-start = (f32[4,128,128]{2,1,0:T(8,128)S(1)}, f32[4,128,128]{2,1,0:T(8,128)S(1)}, u32[]{:S(2)}, u32[]{:S(2)}) collective-permute-start(f32[4,128,128]{2,1,0:T(8,128)S(1)} %get-tuple-element.233), channel_id=1, source_target_pairs={{0,1},{1,2},{2,3},{3,4},{4,5},{5,6},{6,7},{7,8},{8,9},{9,10},{10,1... | collective-permute-start | bytes 786440 | tf_op jit(solution)/shard_map/while/body/eval_jaxpr/ppermute | solution.py:36
  628.8 9.9 %collective-permute-start.4 = (f32[1,128,128]{2,1,0:T(8,128)S(1)}, f32[1,128,128]{2,1,0:T(8,128)S(1)}, u32[]{:S(2)}, u32[]{:S(2)}) collective-permute-start(f32[1,128,128]{2,1,0:T(8,128)S(1)} %get-tuple-element.226), channel_id=1, source_target_pairs={{0,16},{16,32},{32,48},{48,64},{64,80},{80,96},{96,112},{112,128},... | collective-permute-start | bytes 196616 | tf_op jit(solution)/shard_map/while/body/eval_jaxpr/ppermute | solution.py:19
  639.4 10.4 %collective-permute-start = (f32[4,128,128]{2,1,0:T(8,128)S(1)}, f32[4,128,128]{2,1,0:T(8,128)S(1)}, u32[]{:S(2)}, u32[]{:S(2)}) collective-permute-start(f32[4,128,128]{2,1,0:T(8,128)S(1)} %get-tuple-element.233), channel_id=1, source_target_pairs={{0,1},{1,2},{2,3},{3,4},{4,5},{5,6},{6,7},{7,8},{8,9},{9,10},{10,1... | collective-permute-start | bytes 786440 | tf_op jit(solution)/shard_map/while/body/eval_jaxpr/ppermute | solution.py:36
  674.1 10.4 %collective-permute-start = (f32[4,128,128]{2,1,0:T(8,128)S(1)}, f32[4,128,128]{2,1,0:T(8,128)S(1)}, u32[]{:S(2)}, u32[]{:S(2)}) collective-permute-start(f32[4,128,128]{2,1,0:T(8,128)S(1)} %get-tuple-element.233), channel_id=1, source_target_pairs={{0,1},{1,2},{2,3},{3,4},{4,5},{5,6},{6,7},{7,8},{8,9},{9,10},{10,1... | collective-permute-start | bytes 786440 | tf_op jit(solution)/shard_map/while/body/eval_jaxpr/ppermute | solution.py:36
  708.8 10.4 %collective-permute-start = (f32[4,128,128]{2,1,0:T(8,128)S(1)}, f32[4,128,128]{2,1,0:T(8,128)S(1)}, u32[]{:S(2)}, u32[]{:S(2)}) collective-permute-start(f32[4,128,128]{2,1,0:T(8,128)S(1)} %get-tuple-element.233), channel_id=1, source_target_pairs={{0,1},{1,2},{2,3},{3,4},{4,5},{5,6},{6,7},{7,8},{8,9},{9,10},{10,1... | collective-permute-start | bytes 786440 | tf_op jit(solution)/shard_map/while/body/eval_jaxpr/ppermute | solution.py:36
  743.5 10.4 %collective-permute-start = (f32[4,128,128]{2,1,0:T(8,128)S(1)}, f32[4,128,128]{2,1,0:T(8,128)S(1)}, u32[]{:S(2)}, u32[]{:S(2)}) collective-permute-start(f32[4,128,128]{2,1,0:T(8,128)S(1)} %get-tuple-element.233), channel_id=1, source_target_pairs={{0,1},{1,2},{2,3},{3,4},{4,5},{5,6},{6,7},{7,8},{8,9},{9,10},{10,1... | collective-permute-start | bytes 786440 | tf_op jit(solution)/shard_map/while/body/eval_jaxpr/ppermute | solution.py:36
  778.2 10.4 %collective-permute-start = (f32[4,128,128]{2,1,0:T(8,128)S(1)}, f32[4,128,128]{2,1,0:T(8,128)S(1)}, u32[]{:S(2)}, u32[]{:S(2)}) collective-permute-start(f32[4,128,128]{2,1,0:T(8,128)S(1)} %get-tuple-element.233), channel_id=1, source_target_pairs={{0,1},{1,2},{2,3},{3,4},{4,5},{5,6},{6,7},{7,8},{8,9},{9,10},{10,1... | collective-permute-start | bytes 786440 | tf_op jit(solution)/shard_map/while/body/eval_jaxpr/ppermute | solution.py:36
  802.3 9.9 %collective-permute-start.4 = (f32[1,128,128]{2,1,0:T(8,128)S(1)}, f32[1,128,128]{2,1,0:T(8,128)S(1)}, u32[]{:S(2)}, u32[]{:S(2)}) collective-permute-start(f32[1,128,128]{2,1,0:T(8,128)S(1)} %get-tuple-element.226), channel_id=1, source_target_pairs={{0,16},{16,32},{32,48},{48,64},{64,80},{80,96},{96,112},{112,128},... | collective-permute-start | bytes 196616 | tf_op jit(solution)/shard_map/while/body/eval_jaxpr/ppermute | solution.py:19
  812.9 10.4 %collective-permute-start = (f32[4,128,128]{2,1,0:T(8,128)S(1)}, f32[4,128,128]{2,1,0:T(8,128)S(1)}, u32[]{:S(2)}, u32[]{:S(2)}) collective-permute-start(f32[4,128,128]{2,1,0:T(8,128)S(1)} %get-tuple-element.233), channel_id=1, source_target_pairs={{0,1},{1,2},{2,3},{3,4},{4,5},{5,6},{6,7},{7,8},{8,9},{9,10},{10,1... | collective-permute-start | bytes 786440 | tf_op jit(solution)/shard_map/while/body/eval_jaxpr/ppermute | solution.py:36
  (94 other events, 660.1 us)
where the time goes:
time: 861 us; the launch traced here: 848 us
  waiting for transfers between devices  488 us (57%)
  starting transfers between devices  286 us (33%)
  other arithmetic  60.7 us (7%)
    ppermute x52, waiting for transfers between devices, with_halo(): lax.ppermute(lax.slice_in_dim(block, block.shape[dim] - width, None, axis...  337 us
    ppermute x15, waiting for transfers between devices, passed_along(): lax.ppermute(value, axis, [(source, source + steps) for source in range(l...  127 us
    ppermute x52, starting transfers between devices, with_halo(): lax.ppermute(lax.slice_in_dim(block, 0, width, axis=dim), axis, backward)  123 us
    ppermute x52, starting transfers between devices, with_halo(): lax.ppermute(lax.slice_in_dim(block, block.shape[dim] - width, None, axis...  123 us
    ppermute x15, starting transfers between devices, passed_along(): lax.ppermute(value, axis, [(source, source + steps) for source in range(l...  28.8 us
    concatenate x52, other arithmetic, with_halo(): block = jnp.concatenate([low, block, high], axis=dim)  27.8 us
    ppermute x1, waiting for transfers between devices, from_behind(): return lax.ppermute(block, axis, route)  22.8 us
  transfers between devices with their start and end apart: 121, of which 66 were waited for; matrix products, arithmetic and copies ran while one was open for 1% of the time, Pallas kernels for 0%

commit v1 on v0

v1 whole, which is shorter than its diff:
```python
import functools

import jax
import jax.numpy as jnp
import numpy as np
from jax import lax
from jax.experimental import pallas as pl
from jax.experimental.pallas import tpu as pltpu
from jax.sharding import PartitionSpec as P

STEPS = 4
SWEEPS = 5
CSWEEPS = 2
TAU = 0.25
LINE = 16
ROWS = 8
NX = 64
CZ = 128
FINE_HALO = 5
S_HALO = 8

CHIP = [c if c < 4 else 11 - c for c in range(8)]
BLOCK_OF = [2 * CHIP[m // 2] + m % 2 for m in range(LINE)]
HOLDER = [BLOCK_OF.index(q) for q in range(LINE)]


def sweep_constants(scale, sweeps):
    upper = 2.0 + 12.0 * scale
    center = (upper + 0.5) / 2.0
    radius = (upper - 0.5) / 2.0
    ratio = center / radius
    weight = 1.0 / ratio
    pairs = []
    for _ in range(sweeps):
        weight_next = 1.0 / (2.0 * ratio - weight)
        pairs.append((weight_next * weight, 2.0 * weight_next / radius))
        weight = weight_next
    return 1.0 / center, pairs


def inside(block, row):
    place = block * ROWS + row
    return jnp.logical_and(place >= 0, place < LINE * ROWS)


def sweep(block, first_row, lo, hi, cond_at, rhs, old, now, scale, pair, first):
    alpha, beta = pair
    row_id = lax.broadcasted_iota(jnp.int32, (NX, CZ), 0)
    lane_id = lax.broadcasted_iota(jnp.int32, (NX, CZ), 1)
    own = 1.0 + alpha - 6.0 * scale * beta

    def body(row, carry):
        x = now[row]
        near = now[row - 1] + now[row + 1]
        near = near + jnp.where(row_id == 0, 0.0, pltpu.roll(x, 1, 0))
        near = near + jnp.where(row_id == NX - 1, 0.0, pltpu.roll(x, NX - 1, 0))
        near = near + jnp.where(lane_id == 0, 0.0, pltpu.roll(x, 1, 1))
        near = near + jnp.where(lane_id == CZ - 1, 0.0, pltpu.roll(x, CZ - 1, 1))
        gain = jnp.where(inside(block, first_row + row), beta * scale, 0.0)
        new = x * (own - beta * cond_at(row)) + beta * rhs[row] + gain * near
        if not first:
            new = new - alpha * old[row]
        old[row] = new
        return carry

    lax.fori_loop(lo, hi, body, 0)


def solve(block, first_row, lo, hi, cond_at, rhs, a, b, scale, sweeps):
    _, pairs = sweep_constants(scale, sweeps)
    old, now = b, a
    for k, pair in enumerate(pairs):
        sweep(block, first_row, lo + k + 1, hi - k - 1, cond_at, rhs, old, now, scale, pair, k == 0)
        old, now = now, old
    return now


def write_edges(parity, source, at, height, out_i, out_x):
    top = ROWS - height
    from_i = jnp.where(parity == 0, top, 0)
    out_i[...] = source[pl.ds(at + from_i, height)]
    out_x[...] = source[pl.ds(at + top - from_i, height)]


def spread(parity, target, height, own, halo_i, halo_x):
    far = height + ROWS
    place_i = jnp.where(parity == 0, far, 0)
    target[pl.ds(height, ROWS)] = own
    target[pl.ds(place_i, height)] = halo_i
    target[pl.ds(far - place_i, height)] = halo_x


def unpack_kernel(info, packed, cond, coil, start, edge_i, edge_x):
    for row in range(ROWS):
        for place, out in enumerate((cond, coil, start)):
            out[row] = packed[pl.ds(place * ROWS + row, NX, stride=3 * ROWS), :]
    parity = info[1]
    at = 0
    for out, height in ((cond, S_HALO), (coil, FINE_HALO), (start, FINE_HALO)):
        write_edges(parity, out, 0, height, edge_i.at[pl.ds(at, height)], edge_x.at[pl.ds(at, height)])
        at += height


def gather_kernel(info, cond, coil, halo_i, halo_x, cond_all, coil_all):
    parity = info[1]
    spread(parity, cond_all, S_HALO, cond[...], halo_i[pl.ds(0, S_HALO)], halo_x[pl.ds(0, S_HALO)])
    spread(
        parity,
        coil_all,
        FINE_HALO,
        coil[...],
        halo_i[pl.ds(S_HALO, FINE_HALO)],
        halo_x[pl.ds(S_HALO, FINE_HALO)],
    )


def fine_kernel(halo_at, step, info, cond, coil, own, halo_i, halo_x, state, sample, edge_i, edge_x, a, b, rhs):
    block, parity = info[0], info[1]
    height = FINE_HALO
    total = ROWS + 2 * height
    spread(parity, b, height, own[...], halo_i[pl.ds(halo_at, height)], halo_x[pl.ds(halo_at, height)])
    drive = TAU * info[3 + step].astype(jnp.float32)
    inverse, _ = sweep_constants(TAU, SWEEPS)
    shift = S_HALO - height

    def cond_at(row):
        return cond[row + shift]

    def start(row, carry):
        value = cond_at(row) * b[row] + drive * coil[row]
        rhs[row] = value
        a[row] = value * inverse
        return carry

    lax.fori_loop(0, total, start, 0)
    result = solve(block, -height, 0, total, cond_at, rhs, a, b, TAU, SWEEPS)
    for row in range(ROWS):
        value = result[height + row]
        state[row] = value
        sample[pl.ds(row, NX, stride=ROWS), :] = value
    write_edges(parity, result, height, height, edge_i, edge_x)


def coarse_kernel(power, info, cond, own, halo_i, halo_x, *rest):
    height = 2 * power
    outs, (a, b, rhs) = rest[:-3], rest[-3:]
    block, parity = info[0], info[1]
    total = ROWS + 2 * height
    spread(parity, a, height, own[...], halo_i[...], halo_x[...])
    scale = 4.0 * TAU
    inverse, _ = sweep_constants(scale, CSWEEPS)
    shift = S_HALO - height

    def cond_at(row):
        return cond[row + shift]

    lo, hi = 0, total
    value_in, spare = a, b
    for _ in range(power):

        def start(row, carry):
            value = cond_at(row) * value_in[row]
            rhs[row] = value
            value_in[row] = value * inverse
            return carry

        lax.fori_loop(lo, hi, start, 0)
        result = solve(block, -height, lo, hi, cond_at, rhs, value_in, spare, scale, CSWEEPS)
        spare = spare if result is value_in else value_in
        value_in = result
        lo, hi = lo + CSWEEPS, hi - CSWEEPS
    outs[0][...] = value_in[pl.ds(height, ROWS)]
    if len(outs) > 1:
        write_edges(parity, value_in, height, ROWS, outs[1], outs[2])


def combine_kernel(height, sign, info, left, right, out, edge_i, edge_x):
    out[...] = left[...] + sign * right[...]
    write_edges(info[1], out, 0, height, edge_i, edge_x)


def final_kernel(info, left, right, start, out):
    for row in range(ROWS):
        value = left[row] + right[row] + start[row]
        out[pl.ds(row, NX, stride=ROWS), :] = value


def shape(*dims):
    return jax.ShapeDtypeStruct(dims, jnp.float32)


def tile(rows=ROWS):
    return shape(rows, NX, CZ)


def call(kernel, name, outs, scratch, flops, *args):
    size = sum(int(np.prod(o.shape)) for o in outs) + sum(int(np.prod(a.shape)) for a in args[1:])
    return pl.pallas_call(
        kernel,
        out_shape=outs,
        in_specs=[pl.BlockSpec(memory_space=pltpu.SMEM)] + [pl.BlockSpec(memory_space=pltpu.VMEM)] * (len(args) - 1),
        out_specs=[pl.BlockSpec(memory_space=pltpu.VMEM)] * len(outs),
        scratch_shapes=[pltpu.VMEM((rows, NX, CZ), jnp.float32) for rows in scratch],
        cost_estimate=pl.CostEstimate(flops=flops, bytes_accessed=4 * size, transcendentals=0),
        compiler_params=pltpu.CompilerParams(vmem_limit_bytes=24 << 20),
        name=name,
    )(*args)


def swap_halos(edge_i, edge_x):
    inner = [(m, m ^ 1) for m in range(LINE)]
    outer = []
    for q in range(1, LINE - 1, 2):
        outer += [(HOLDER[q], HOLDER[q + 1]), (HOLDER[q + 1], HOLDER[q])]
    return lax.ppermute(edge_i, "mesh", inner), lax.ppermute(edge_x, "mesh", outer)


def later(value, distance, cyclic=False):
    route = [(n, (n + distance) % LINE) for n in range(LINE) if cyclic or n + distance < LINE]
    return lax.ppermute(value, "tm", route)


def dft_table(sample_times, total, harmonics):
    orders = jnp.arange(1, harmonics + 1, dtype=jnp.int32)
    product = orders[:, None] * sample_times[None, :] % total
    angle = 2.0 * jnp.pi / total * product.astype(jnp.float32)
    return jnp.concatenate([jnp.cos(angle), -jnp.sin(angle)], axis=0)


def z_difference(field):
    inner = field[..., 1:] - field[..., :-1]
    return jnp.concatenate([inner, jnp.zeros_like(field[..., :1])], axis=-1)


def core_loss(spectrum, loss_coeffs, total):
    harmonics = total // 2
    real_part = spectrum[:harmonics]
    imag_part = spectrum[harmonics:]
    power = (real_part * real_part + imag_part * imag_part) * (2.0 / total) ** 2
    freq = (jnp.arange(1, harmonics + 1, dtype=jnp.int32).astype(jnp.float32) / harmonics).reshape(-1, 1, 1, 1)
    root = jnp.sqrt(power)
    terms = loss_coeffs[0] * freq * power + loss_coeffs[1] * (freq * freq) * power
    terms = terms + loss_coeffs[2] * freq**1.5 * (root * jnp.sqrt(root))
    return jnp.sum(terms, axis=0)


def on_device(slice_start, conductivity, coil_current, switching, loss_coeffs):
    total = STEPS * LINE
    block = jnp.asarray(BLOCK_OF, jnp.int32)[lax.axis_index("mesh")]
    info = jnp.concatenate([jnp.stack([block, block % 2, block]), switching]).astype(jnp.int32)

    fields = jnp.stack([conductivity, coil_current, slice_start[0]], axis=1)
    fields = fields.reshape(4, 3, LINE, ROWS, CZ)
    fields = jnp.stack([fields[:, :, q] for q in BLOCK_OF], axis=0)
    packed = lax.all_to_all(fields, "mesh", 0, 0, tiled=True).reshape(LINE * 4 * 3 * ROWS, CZ)

    to_spectrum = [(m * LINE + t, HOLDER[t] * LINE + m) for m in range(LINE) for t in range(LINE)]
    back = [(target, source) for source, target in to_spectrum]
    coeffs = lax.ppermute(loss_coeffs, ("mesh", "tm"), to_spectrum)

    edge_rows = S_HALO + 2 * FINE_HALO
    cond, coil, start, edge_i, edge_x = call(
        unpack_kernel, "unpack", [tile(), tile(), tile(), tile(edge_rows), tile(edge_rows)], [], 0, info, packed
    )
    halo_i, halo_x = swap_halos(edge_i, edge_x)
    cond_all, coil_all = call(
        gather_kernel,
        "gather",
        [tile(ROWS + 2 * S_HALO), tile(ROWS + 2 * FINE_HALO)],
        [],
        0,
        info,
        cond,
        coil,
        halo_i,
        halo_x,
    )
    state, samples = start, []
    rows = ROWS + 2 * FINE_HALO
    for step in range(STEPS):
        state, sample, edge_i, edge_x = call(
            functools.partial(fine_kernel, S_HALO + FINE_HALO if step == 0 else 0, step),
            "fine",
            [tile(), shape(NX * ROWS, CZ), tile(FINE_HALO), tile(FINE_HALO)],
            [rows] * 3,
            20 * SWEEPS * rows * NX * CZ,
            info,
            cond_all,
            coil_all,
            state,
            halo_i,
            halo_x,
        )
        samples.append(sample.reshape(LINE, 4, ROWS, CZ))
        if step + 1 < STEPS:
            halo_i, halo_x = swap_halos(edge_i, edge_x)

    arrived = later(state, 1, cyclic=True)
    other, sign = start, -1.0
    value = arrived
    for power in (1, 2, 4, 8):
        height = min(2 * power, S_HALO)
        value, edge_i, edge_x = call(
            functools.partial(combine_kernel, height, sign),
            "combine",
            [tile(), tile(height), tile(height)],
            [],
            0,
            info,
            value,
            other,
        )
        sign = 1.0
        moved = value
        halves = max(1, power // 4)
        for half in range(halves):
            halo_i, halo_x = swap_halos(edge_i, edge_x)
            own_power = power // halves
            more = half + 1 < halves
            rows = ROWS + 2 * height
            result = call(
                functools.partial(coarse_kernel, own_power),
                "coarse",
                [tile()] + ([tile(), tile()] if more else []),
                [rows] * 3,
                20 * CSWEEPS * own_power * rows * NX * CZ,
                info,
                cond_all,
                moved,
                halo_i,
                halo_x,
            )
            moved = result[0]
            if more:
                edge_i, edge_x = result[1], result[2]
        other = later(moved, power)
    (out,) = call(final_kernel, "final", [shape(NX * ROWS, CZ)], [], 0, info, value, other, start)
    out = lax.all_to_all(out.reshape(LINE, 4, ROWS, CZ), "mesh", 0, 0, tiled=True)
    next_start = jnp.stack([out[m] for m in HOLDER], axis=1).reshape(1, 4, LINE * ROWS, CZ)

    gathered = jnp.stack(samples, axis=1)
    gathered = lax.all_to_all(gathered, "tm", 0, 0, tiled=True).reshape(total, 4, ROWS, CZ)
    table = dft_table(jnp.arange(total, dtype=jnp.int32), total, total // 2)
    spectrum = jnp.einsum("kt,txyz->kxyz", table, z_difference(gathered), precision=lax.Precision.HIGHEST)
    loss = core_loss(spectrum, coeffs, total)
    loss_density = lax.ppermute(loss, ("mesh", "tm"), back)
    return next_start, loss_density


def solution(mesh):
    placed = (
        P("tm", "mesh", None, None),
        P("mesh", None, None),
        P("mesh", None, None),
        P("tm"),
        P(None, "mesh", "tm", None),
    )
    return jax.shard_map(
        on_device,
        mesh=mesh,
        in_specs=placed,
        out_specs=(P("tm", "mesh", None, None), P("mesh", "tm", None)),
        check_vma=False,
    )
```

time: 861 us -> 283 us (0.33)
  the two profiles are of different devices: /device:TPU:132 before, /device:TPU:160 now
where the time goes in v1:
time: 283 us; the launch traced here: 282 us
  starting transfers between devices  127 us (45%)
  Pallas kernels  72.8 us (26%)
  waiting for transfers between devices  58.8 us (21%)
  local copies, waits for them, and re-layouts  15.2 us (5%)
  other arithmetic  4.01 us (1%)
  between operations  3.09 us (1%)
    pallas_call x16, Pallas kernels, call(): pl.pallas_call(kernel, out_shape=outs, in_specs=[pl.BlockSpec(memory_spac...  72.8 us
    ppermute x9, starting transfers between devices, swap_halos(): lax.ppermute(edge_i, 'mesh', inner)  51.7 us
    ppermute x5, waiting for transfers between devices, later(): return lax.ppermute(value, 'tm', route)  33.6 us
    all_to_all x1, starting transfers between devices, on_device(): lax.all_to_all(out.reshape(LINE, 4, ROWS, CZ), 'mesh', 0, 0, tiled=True)  19.7 us
    ppermute x1, starting transfers between devices, on_device(): coeffs = lax.ppermute(loss_coeffs, ('mesh', 'tm'), to_spectrum)  19.3 us
    unnamed x37, local copies, waits for them, and re-layouts  11.2 us
    ppermute x5, starting transfers between devices, later(): return lax.ppermute(value, 'tm', route)  11 us
    all_to_all x1, waiting for transfers between devices, on_device(): lax.all_to_all(fields, 'mesh', 0, 0, tiled=True)  10.6 us
  transfers between devices with their start and end apart: 28, of which 13 were waited for; matrix products, arithmetic and copies ran while one was open for 2% of the time, Pallas kernels for 12%

profile of v1, /device:TPU:160, one launch (start us, length us, event | category | flops | bytes accessed | tf_op | source)
XLA Modules:
  0.0 281.6 jit_solution(3202099733610857177)
XLA Ops:
  11.8 7.0 %all-to-all-start = ((f32[16,4,3,8,128]{4,3,2,1,0:T(8,128)}), f32[16,4,3,8,128]{4,3,2,1,0:T(8,128)S(1)}, u32[]{:S(2)}, u32[]{:S(2)}) async-start(f32[16,4,3,8,128]{4,3,2,1,0:T(8,128)} %constant_dynamic-update-slice_fusion), calls=%async_computation | async-start | bytes 1572864 | tf_op jit(solution)/shard_map/all_to_all | solution.py:255
  23.4 10.6 %all-to-all-done = f32[16,4,3,8,128]{4,3,2,1,0:T(8,128)S(1)} async-done(((f32[16,4,3,8,128]{4,3,2,1,0:T(8,128)}), f32[16,4,3,8,128]{4,3,2,1,0:T(8,128)S(1)}, u32[]{:S(2)}, u32[]{:S(2)}) %all-to-all-start) | async-done | bytes 786464 | tf_op jit(solution)/shard_map/all_to_all | solution.py:255
  37.5 6.2 %fine.4 = (f32[8,64,128]{2,1,0:T(8,128)S(1)}, f32[512,128]{1,0:T(8,128)S(1)}, f32[5,64,128]{2,1,0:T(8,128)S(1)}, f32[5,64,128]{2,1,0:T(8,128)S(1)}) custom-call(s32[7]{0:T(128)S(1)} %pad_add_fusion.info, f32[24,64,128]{2,1,0:T(8,128)S(1)} %get-tuple-element.42.cond, f32[18,64,128]{2,1,0:T(8,128)S(1)} %get-tuple-element.43.coil, ...), custom_call_target="tpu_custom_call" | custom-call | flops 14745600 | bytes 3670016 | tf_op jit(solution)/shard_map/fine/pallas_call | solution.py:198
  43.6 9.8 %collective-permute-start.2 = (f32[5,64,128]{2,1,0:T(8,128)S(1)}, f32[5,64,128]{2,1,0:T(8,128)S(1)}, u32[]{:S(2)}, u32[]{:S(2)}) collective-permute-start(f32[5,64,128]{2,1,0:T(8,128)S(1)} %get-tuple-element.46), channel_id=1, source_target_pairs={{0,16},{16,0},{32,48},{48,32},{64,80},{80,64},{96,112},{112,96},{1... | collective-permute-start | bytes 491528 | tf_op jit(solution)/shard_map/ppermute | solution.py:215
  54.5 6.2 %fine.5 = (f32[8,64,128]{2,1,0:T(8,128)S(1)}, f32[512,128]{1,0:T(8,128)S(1)}, f32[5,64,128]{2,1,0:T(8,128)S(1)}, f32[5,64,128]{2,1,0:T(8,128)S(1)}) custom-call(s32[7]{0:T(128)S(1)} %pad_add_fusion.info, f32[24,64,128]{2,1,0:T(8,128)S(1)} %get-tuple-element.42.cond, f32[18,64,128]{2,1,0:T(8,128)S(1)} %get-tuple-element.43.coil, ...), custom_call_target="tpu_custom_call" | custom-call | flops 14745600 | bytes 2818048 | tf_op jit(solution)/shard_map/fine/pallas_call | solution.py:198
  60.6 5.7 %collective-permute-start.4 = (f32[5,64,128]{2,1,0:T(8,128)S(1)}, f32[5,64,128]{2,1,0:T(8,128)S(1)}, u32[]{:S(2)}, u32[]{:S(2)}) collective-permute-start(f32[5,64,128]{2,1,0:T(8,128)S(1)} %get-tuple-element.49), channel_id=1, source_target_pairs={{0,16},{16,0},{32,48},{48,32},{64,80},{80,64},{96,112},{112,96},{1... | collective-permute-start | bytes 491528 | tf_op jit(solution)/shard_map/ppermute | solution.py:215
  67.4 6.2 %fine.6 = (f32[8,64,128]{2,1,0:T(8,128)S(1)}, f32[512,128]{1,0:T(8,128)S(1)}, f32[5,64,128]{2,1,0:T(8,128)S(1)}, f32[5,64,128]{2,1,0:T(8,128)S(1)}) custom-call(s32[7]{0:T(128)S(1)} %pad_add_fusion.info, f32[24,64,128]{2,1,0:T(8,128)S(1)} %get-tuple-element.42.cond, f32[18,64,128]{2,1,0:T(8,128)S(1)} %get-tuple-element.43.coil, ...), custom_call_target="tpu_custom_call" | custom-call | flops 14745600 | bytes 2818048 | tf_op jit(solution)/shard_map/fine/pallas_call | solution.py:198
  73.5 5.7 %collective-permute-start.6 = (f32[5,64,128]{2,1,0:T(8,128)S(1)}, f32[5,64,128]{2,1,0:T(8,128)S(1)}, u32[]{:S(2)}, u32[]{:S(2)}) collective-permute-start(f32[5,64,128]{2,1,0:T(8,128)S(1)} %get-tuple-element.52), channel_id=1, source_target_pairs={{0,16},{16,0},{32,48},{48,32},{64,80},{80,64},{96,112},{112,96},{1... | collective-permute-start | bytes 491528 | tf_op jit(solution)/shard_map/ppermute | solution.py:215
  80.3 6.8 %fine.7 = (f32[8,64,128]{2,1,0:T(8,128)S(1)}, f32[512,128]{1,0:T(8,128)S(1)}, f32[5,64,128]{2,1,0:T(8,128)}, f32[5,64,128]{2,1,0:T(8,128)}) custom-call(s32[7]{0:T(128)S(1)} %pad_add_fusion.info, f32[24,64,128]{2,1,0:T(8,128)S(1)} %get-tuple-element.42.cond, f32[18,64,128]{2,1,0:T(8,128)S(1)} %get-tuple-element.43.coil, ...), custom_call_target="tpu_custom_call" | custom-call | flops 14745600 | bytes 2818048 | tf_op jit(solution)/shard_map/fine/pallas_call | solution.py:198
  88.8 8.1 %all-to-all-start.2 = ((f32[16,4,4,8,128]{4,3,2,1,0:T(8,128)}), f32[16,4,4,8,128]{4,3,2,1,0:T(8,128)}, u32[]{:S(2)}, u32[]{:S(2)}) async-start(f32[16,4,4,8,128]{4,3,2,1,0:T(8,128)} %pad_maximum_fusion), calls=%async_computation.2 | async-start | bytes 2097152 | tf_op jit(solution)/shard_map/all_to_all | solution.py:342
  98.1 7.7 %collective-permute-start.9 = (f32[2,64,128]{2,1,0:T(8,128)S(1)}, f32[2,64,128]{2,1,0:T(8,128)S(1)}, u32[]{:S(2)}, u32[]{:S(2)}) collective-permute-start(f32[2,64,128]{2,1,0:T(8,128)S(1)} %get-tuple-element.56), channel_id=1, source_target_pairs={{0,16},{16,0},{32,48},{48,32},{64,80},{80,64},{96,112},{112,96},{1... | collective-permute-start | bytes 196616 | tf_op jit(solution)/shard_map/ppermute | solution.py:215
  106.7 2.3 coarse.5
  109.0 3.4 %collective-permute-start.11 = (f32[8,64,128]{2,1,0:T(8,128)S(1)}, f32[8,64,128]{2,1,0:T(8,128)S(1)}, u32[]{:S(2)}, u32[]{:S(2)}) collective-permute-start(f32[8,64,128]{2,1,0:T(8,128)S(1)} %coarse.5), channel_id=1, source_target_pairs={{0,1},{1,2},{2,3},{3,4},{4,5},{5,6},{6,7},{7,8},{8,9},{9,10},{10,1... | collective-permute-start | bytes 786440 | tf_op jit(solution)/shard_map/ppermute | solution.py:220
  112.4 14.5 %collective-permute-done.11.right = f32[8,64,128]{2,1,0:T(8,128)S(1)} collective-permute-done((f32[8,64,128]{2,1,0:T(8,128)S(1)}, f32[8,64,128]{2,1,0:T(8,128)S(1)}, u32[]{:S(2)}, u32[]{:S(2)}) %collective-permute-start.11) | collective-permute-done | bytes 262176 | tf_op jit(solution)/shard_map/ppermute | solution.py:220
  127.4 2.1 collective-permute-start.12
  130.5 4.7 %coarse.6 = f32[8,64,128]{2,1,0:T(8,128)S(1)} custom-call(s32[7]{0:T(128)S(1)} %pad_add_fusion.info, f32[24,64,128]{2,1,0:T(8,128)S(1)} %get-tuple-element.42.cond, f32[8,64,128]{2,1,0:T(8,128)S(1)} %get-tuple-element.58.own.left, f32[4,64,128]{2,1,0:T(8,128)S(1)} %collective-permute-done.12.halo_i, f32[4,64,128]{2,1,0:T(8,128)S(1)} %collective-permute-done.13.halo_x), custom_call_target="tpu_custom_call" | custom-call | flops 10485760 | bytes 1572864 | tf_op jit(solution)/shard_map/coarse/pallas_call | solution.py:198
  135.3 2.5 collective-permute-start.14
  137.7 5.8 %collective-permute-done.14.right = f32[8,64,128]{2,1,0:T(8,128)S(1)} collective-permute-done((f32[8,64,128]{2,1,0:T(8,128)S(1)}, f32[8,64,128]{2,1,0:T(8,128)S(1)}, u32[]{:S(2)}, u32[]{:S(2)}) %collective-permute-start.14) | collective-permute-done | bytes 262176 | tf_op jit(solution)/shard_map/ppermute | solution.py:220
  144.1 9.4 %collective-permute-start.15 = (f32[8,64,128]{2,1,0:T(8,128)S(1)}, f32[8,64,128]{2,1,0:T(8,128)S(1)}, u32[]{:S(2)}, u32[]{:S(2)}) collective-permute-start(f32[8,64,128]{2,1,0:T(8,128)S(1)} %get-tuple-element.62), channel_id=1, source_target_pairs={{0,16},{16,0},{32,48},{48,32},{64,80},{80,64},{96,112},{112,96},{1... | collective-permute-start | bytes 786440 | tf_op jit(solution)/shard_map/ppermute | solution.py:215
  154.7 11.8 %coarse.7 = f32[8,64,128]{2,1,0:T(8,128)S(1)} custom-call(s32[7]{0:T(128)S(1)} %pad_add_fusion.info, f32[24,64,128]{2,1,0:T(8,128)S(1)} %get-tuple-element.42.cond, f32[8,64,128]{2,1,0:T(8,128)S(1)} %get-tuple-element.61.own.left, f32[8,64,128]{2,1,0:T(8,128)S(1)} %collective-permute-done.15.halo_i, f32[8,64,128]{2,1,0:T(8,128)S(1)} %collective-permute-done.16.halo_x), custom_call_target="tpu_custom_call" | custom-call | flops 31457280 | bytes 1835008 | tf_op jit(solution)/shard_map/coarse/pallas_call | solution.py:198
  166.5 3.2 %collective-permute-start.17 = (f32[8,64,128]{2,1,0:T(8,128)S(1)}, f32[8,64,128]{2,1,0:T(8,128)S(1)}, u32[]{:S(2)}, u32[]{:S(2)}) collective-permute-start(f32[8,64,128]{2,1,0:T(8,128)S(1)} %coarse.7), channel_id=1, source_target_pairs={{0,4},{1,5},{2,6},{3,7},{4,8},{5,9},{6,10},{7,11},{8,12},{9,13},{1... | collective-permute-start | bytes 786440 | tf_op jit(solution)/shard_map/ppermute | solution.py:220
  169.7 19.3 %collective-permute-start.23 = (f32[3,4,8,128]{3,2,1,0:T(8,128)S(1)}, f32[3,4,8,128]{3,2,1,0:T(8,128)S(1)}, u32[]{:S(2)}, u32[]{:S(2)}) collective-permute-start(f32[3,4,8,128]{3,2,1,0:T(8,128)S(1)} %copy-done.1), channel_id=1, source_target_pairs={{0,0},{1,16},{2,32},{3,48},{4,64},{5,80},{6,96},{7,112},{8,224},{9... | collective-permute-start | bytes 147464 | tf_op jit(solution)/shard_map/ppermute | solution.py:259
  191.3 11.8 %coarse.8 = (f32[8,64,128]{2,1,0:T(8,128)S(1)}, f32[8,64,128]{2,1,0:T(8,128)S(1)}, f32[8,64,128]{2,1,0:T(8,128)S(1)}) custom-call(s32[7]{0:T(128)S(1)} %pad_add_fusion.info, f32[24,64,128]{2,1,0:T(8,128)S(1)} %get-tuple-element.42.cond, f32[8,64,128]{2,1,0:T(8,128)S(1)} %get-tuple-element.64.own.left, f32[8,64,128]{2,1,0:T(8,128)S(1)} %collective-permute-done.18.halo_i, ...), custom_call_target="tpu_custom_call" | custom-call | flops 31457280 | bytes 2359296 | tf_op jit(solution)/shard_map/coarse/pallas_call | solution.py:198
  203.2 11.2 %collective-permute-start.20 = (f32[8,64,128]{2,1,0:T(8,128)S(1)}, f32[8,64,128]{2,1,0:T(8,128)S(1)}, u32[]{:S(2)}, u32[]{:S(2)}) collective-permute-start(f32[8,64,128]{2,1,0:T(8,128)S(1)} %get-tuple-element.68), channel_id=1, source_target_pairs={{0,16},{16,0},{32,48},{48,32},{64,80},{80,64},{96,112},{112,96},{1... | collective-permute-start | bytes 786440 | tf_op jit(solution)/shard_map/ppermute | solution.py:215
  215.3 1.9 copy.21
  217.2 11.8 %coarse.9 = f32[8,64,128]{2,1,0:T(8,128)S(1)} custom-call(s32[7]{0:T(128)S(1)} %pad_add_fusion.info, f32[24,64,128]{2,1,0:T(8,128)S(1)} %get-tuple-element.42.cond, f32[8,64,128]{2,1,0:T(8,128)S(1)} %get-tuple-element.67.own, f32[8,64,128]{2,1,0:T(8,128)S(1)} %collective-permute-done.20.halo_i, f32[8,64,128]{2,1,0:T(8,128)S(1)} %collective-permute-done.21.halo_x), custom_call_target="tpu_custom_call" | custom-call | flops 31457280 | bytes 1835008 | tf_op jit(solution)/shard_map/coarse/pallas_call | solution.py:198
  229.0 1.3 collective-permute-start.22
  230.6 13.3 %collective-permute-done.22.right = f32[8,64,128]{2,1,0:T(8,128)S(1)} collective-permute-done((f32[8,64,128]{2,1,0:T(8,128)S(1)}, f32[8,64,128]{2,1,0:T(8,128)S(1)}, u32[]{:S(2)}, u32[]{:S(2)}) %collective-permute-start.22) | collective-permute-done | bytes 262176 | tf_op jit(solution)/shard_map/ppermute | solution.py:220
  244.0 1.3 final.1
  245.3 19.7 %all-to-all-start.1 = ((f32[16,4,8,128]{3,2,1,0:T(8,128)}), f32[16,4,8,128]{3,2,1,0:T(8,128)S(1)}, u32[]{:S(2)}, u32[]{:S(2)}) async-start(f32[16,4,8,128]{3,2,1,0:T(8,128)} %bitcast.22), calls=%async_computation.1 | async-start | bytes 524288 | tf_op jit(solution)/shard_map/all_to_all | solution.py:338
  266.6 3.8 %collective-permute-start.24 = (f32[4,8,128]{2,1,0:T(8,128)S(1)}, f32[4,8,128]{2,1,0:T(8,128)S(1)}, u32[]{:S(2)}, u32[]{:S(2)}) collective-permute-start(f32[4,8,128]{2,1,0:T(8,128)S(1)} %fusion.4), channel_id=1, source_target_pairs={{0,0},{16,1},{32,2},{48,3},{64,4},{80,5},{96,6},{112,7},{224,8},{2... | collective-permute-start | bytes 49160 | tf_op jit(solution)/shard_map/ppermute | solution.py:346
  270.3 9.8 %collective-permute-done.24 = f32[4,8,128]{2,1,0:T(8,128)S(1)} collective-permute-done((f32[4,8,128]{2,1,0:T(8,128)S(1)}, f32[4,8,128]{2,1,0:T(8,128)S(1)}, u32[]{:S(2)}, u32[]{:S(2)}) %collective-permute-start.24) | collective-permute-done | bytes 16416 | tf_op jit(solution)/shard_map/ppermute | solution.py:346
  (94 shorter events, 33.8 us)
Async XLA Ops:
  11.8 22.2 %all-to-all-start = ((f32[16,4,3,8,128]{4,3,2,1,0:T(8,128)}), f32[16,4,3,8,128]{4,3,2,1,0:T(8,128)S(1)}, u32[]{:S(2)}, u32[]{:S(2)}) async-start(f32[16,4,3,8,128]{4,3,2,1,0:T(8,128)} %constant_dynamic-update-slice_fusion), calls=%async_computation | async-start | bytes 1572864 | tf_op jit(solution)/shard_map/all_to_all | solution.py:255
  18.8 0.7 copy-start.2
  22.0 0.7 copy-start
  34.7 2.1 collective-permute-start
  34.8 2.0 collective-permute-start.1
  43.6 10.8 %collective-permute-start.2 = (f32[5,64,128]{2,1,0:T(8,128)S(1)}, f32[5,64,128]{2,1,0:T(8,128)S(1)}, u32[]{:S(2)}, u32[]{:S(2)}) collective-permute-start(f32[5,64,128]{2,1,0:T(8,128)S(1)} %get-tuple-element.46), channel_id=1, source_target_pairs={{0,16},{16,0},{32,48},{48,32},{64,80},{80,64},{96,112},{112,96},{1... | collective-permute-start | bytes 491528 | tf_op jit(solution)/shard_map/ppermute | solution.py:215
  53.4 1.0 collective-permute-start.3
  60.6 6.7 %collective-permute-start.4 = (f32[5,64,128]{2,1,0:T(8,128)S(1)}, f32[5,64,128]{2,1,0:T(8,128)S(1)}, u32[]{:S(2)}, u32[]{:S(2)}) collective-permute-start(f32[5,64,128]{2,1,0:T(8,128)S(1)} %get-tuple-element.49), channel_id=1, source_target_pairs={{0,16},{16,0},{32,48},{48,32},{64,80},{80,64},{96,112},{112,96},{1... | collective-permute-start | bytes 491528 | tf_op jit(solution)/shard_map/ppermute | solution.py:215
  66.3 1.0 collective-permute-start.5
  73.5 6.7 %collective-permute-start.6 = (f32[5,64,128]{2,1,0:T(8,128)S(1)}, f32[5,64,128]{2,1,0:T(8,128)S(1)}, u32[]{:S(2)}, u32[]{:S(2)}) collective-permute-start(f32[5,64,128]{2,1,0:T(8,128)S(1)} %get-tuple-element.52), channel_id=1, source_target_pairs={{0,16},{16,0},{32,48},{48,32},{64,80},{80,64},{96,112},{112,96},{1... | collective-permute-start | bytes 491528 | tf_op jit(solution)/shard_map/ppermute | solution.py:215
  79.2 1.0 collective-permute-start.7
  87.1 9.8 %collective-permute-start.8 = (f32[8,64,128]{2,1,0:T(8,128)S(1)}, f32[8,64,128]{2,1,0:T(8,128)S(1)}, u32[]{:S(2)}, u32[]{:S(2)}) collective-permute-start(f32[8,64,128]{2,1,0:T(8,128)S(1)} %get-tuple-element.54), channel_id=1, source_target_pairs={{0,1},{1,2},{2,3},{3,4},{4,5},{5,6},{6,7},{7,8},{8,9},{9,10},{10,1... | collective-permute-start | bytes 786440 | tf_op jit(solution)/shard_map/ppermute | solution.py:220
  88.8 126.5 %all-to-all-start.2 = ((f32[16,4,4,8,128]{4,3,2,1,0:T(8,128)}), f32[16,4,4,8,128]{4,3,2,1,0:T(8,128)}, u32[]{:S(2)}, u32[]{:S(2)}) async-start(f32[16,4,4,8,128]{4,3,2,1,0:T(8,128)} %pad_maximum_fusion), calls=%async_computation.2 | async-start | bytes 2097152 | tf_op jit(solution)/shard_map/all_to_all | solution.py:342
  97.4 8.3 %collective-permute-start.10 = (f32[2,64,128]{2,1,0:T(8,128)S(1)}, f32[2,64,128]{2,1,0:T(8,128)S(1)}, u32[]{:S(2)}, u32[]{:S(2)}) collective-permute-start(f32[2,64,128]{2,1,0:T(8,128)S(1)} %get-tuple-element.57), channel_id=1, source_target_pairs={{16,32},{32,16},{48,64},{64,48},{80,96},{96,80},{112,224},{224,112... | collective-permute-start | bytes 196616 | tf_op jit(solution)/shard_map/ppermute | solution.py:215
  98.1 8.6 %collective-permute-start.9 = (f32[2,64,128]{2,1,0:T(8,128)S(1)}, f32[2,64,128]{2,1,0:T(8,128)S(1)}, u32[]{:S(2)}, u32[]{:S(2)}) collective-permute-start(f32[2,64,128]{2,1,0:T(8,128)S(1)} %get-tuple-element.56), channel_id=1, source_target_pairs={{0,16},{16,0},{32,48},{48,32},{64,80},{80,64},{96,112},{112,96},{1... | collective-permute-start | bytes 196616 | tf_op jit(solution)/shard_map/ppermute | solution.py:215
  109.0 17.9 %collective-permute-start.11 = (f32[8,64,128]{2,1,0:T(8,128)S(1)}, f32[8,64,128]{2,1,0:T(8,128)S(1)}, u32[]{:S(2)}, u32[]{:S(2)}) collective-permute-start(f32[8,64,128]{2,1,0:T(8,128)S(1)} %coarse.5), channel_id=1, source_target_pairs={{0,1},{1,2},{2,3},{3,4},{4,5},{5,6},{6,7},{7,8},{8,9},{9,10},{10,1... | collective-permute-start | bytes 786440 | tf_op jit(solution)/shard_map/ppermute | solution.py:220
  127.4 3.1 %collective-permute-start.12 = (f32[4,64,128]{2,1,0:T(8,128)S(1)}, f32[4,64,128]{2,1,0:T(8,128)S(1)}, u32[]{:S(2)}, u32[]{:S(2)}) collective-permute-start(f32[4,64,128]{2,1,0:T(8,128)S(1)} %get-tuple-element.59), channel_id=1, source_target_pairs={{0,16},{16,0},{32,48},{48,32},{64,80},{80,64},{96,112},{112,96},{1... | collective-permute-start | bytes 393224 | tf_op jit(solution)/shard_map/ppermute | solution.py:215
  129.5 1.0 collective-permute-start.13
  135.3 8.3 %collective-permute-start.14 = (f32[8,64,128]{2,1,0:T(8,128)S(1)}, f32[8,64,128]{2,1,0:T(8,128)S(1)}, u32[]{:S(2)}, u32[]{:S(2)}) collective-permute-start(f32[8,64,128]{2,1,0:T(8,128)S(1)} %coarse.6), channel_id=1, source_target_pairs={{0,2},{1,3},{2,4},{3,5},{4,6},{5,7},{6,8},{7,9},{8,10},{9,11},{10,... | collective-permute-start | bytes 786440 | tf_op jit(solution)/shard_map/ppermute | solution.py:220
  144.1 10.6 %collective-permute-start.15 = (f32[8,64,128]{2,1,0:T(8,128)S(1)}, f32[8,64,128]{2,1,0:T(8,128)S(1)}, u32[]{:S(2)}, u32[]{:S(2)}) collective-permute-start(f32[8,64,128]{2,1,0:T(8,128)S(1)} %get-tuple-element.62), channel_id=1, source_target_pairs={{0,16},{16,0},{32,48},{48,32},{64,80},{80,64},{96,112},{112,96},{1... | collective-permute-start | bytes 786440 | tf_op jit(solution)/shard_map/ppermute | solution.py:215
  153.5 1.2 collective-permute-start.16
  154.7 15.0 %copy-start.1 = (f32[3,4,8,128]{3,2,1,0:T(8,128)S(1)}, f32[3,4,8,128]{3,2,1,0:T(8,128)}, u32[]{:S(2)}) copy-start(f32[3,4,8,128]{3,2,1,0:T(8,128)} %param.10) | copy-start | bytes 147460
  166.5 22.6 %collective-permute-start.17 = (f32[8,64,128]{2,1,0:T(8,128)S(1)}, f32[8,64,128]{2,1,0:T(8,128)S(1)}, u32[]{:S(2)}, u32[]{:S(2)}) collective-permute-start(f32[8,64,128]{2,1,0:T(8,128)S(1)} %coarse.7), channel_id=1, source_target_pairs={{0,4},{1,5},{2,6},{3,7},{4,8},{5,9},{6,10},{7,11},{8,12},{9,13},{1... | collective-permute-start | bytes 786440 | tf_op jit(solution)/shard_map/ppermute | solution.py:220
  169.7 45.5 %collective-permute-start.23 = (f32[3,4,8,128]{3,2,1,0:T(8,128)S(1)}, f32[3,4,8,128]{3,2,1,0:T(8,128)S(1)}, u32[]{:S(2)}, u32[]{:S(2)}) collective-permute-start(f32[3,4,8,128]{3,2,1,0:T(8,128)S(1)} %copy-done.1), channel_id=1, source_target_pairs={{0,0},{1,16},{2,32},{3,48},{4,64},{5,80},{6,96},{7,112},{8,224},{9... | collective-permute-start | bytes 147464 | tf_op jit(solution)/shard_map/ppermute | solution.py:259
  189.7 1.6 collective-permute-start.18
  189.8 1.5 collective-permute-start.19
  203.2 14.0 %collective-permute-start.20 = (f32[8,64,128]{2,1,0:T(8,128)S(1)}, f32[8,64,128]{2,1,0:T(8,128)S(1)}, u32[]{:S(2)}, u32[]{:S(2)}) collective-permute-start(f32[8,64,128]{2,1,0:T(8,128)S(1)} %get-tuple-element.68), channel_id=1, source_target_pairs={{0,16},{16,0},{32,48},{48,32},{64,80},{80,64},{96,112},{112,96},{1... | collective-permute-start | bytes 786440 | tf_op jit(solution)/shard_map/ppermute | solution.py:215
  214.4 2.8 %collective-permute-start.21 = (f32[8,64,128]{2,1,0:T(8,128)S(1)}, f32[8,64,128]{2,1,0:T(8,128)S(1)}, u32[]{:S(2)}, u32[]{:S(2)}) collective-permute-start(f32[8,64,128]{2,1,0:T(8,128)S(1)} %get-tuple-element.69), channel_id=1, source_target_pairs={{16,32},{32,16},{48,64},{64,48},{80,96},{96,80},{112,224},{224,112... | collective-permute-start | bytes 786440 | tf_op jit(solution)/shard_map/ppermute | solution.py:215
  229.0 15.0 %collective-permute-start.22 = (f32[8,64,128]{2,1,0:T(8,128)S(1)}, f32[8,64,128]{2,1,0:T(8,128)S(1)}, u32[]{:S(2)}, u32[]{:S(2)}) collective-permute-start(f32[8,64,128]{2,1,0:T(8,128)S(1)} %coarse.9), channel_id=1, source_target_pairs={{0,8},{1,9},{2,10},{3,11},{4,12},{5,13},{6,14},{7,15},{16,24},{17,... | collective-permute-start | bytes 786440 | tf_op jit(solution)/shard_map/ppermute | solution.py:220
  245.3 34.8 %all-to-all-start.1 = ((f32[16,4,8,128]{3,2,1,0:T(8,128)}), f32[16,4,8,128]{3,2,1,0:T(8,128)S(1)}, u32[]{:S(2)}, u32[]{:S(2)}) async-start(f32[16,4,8,128]{3,2,1,0:T(8,128)} %bitcast.22), calls=%async_computation.1 | async-start | bytes 524288 | tf_op jit(solution)/shard_map/all_to_all | solution.py:338
  266.6 13.6 %collective-permute-start.24 = (f32[4,8,128]{2,1,0:T(8,128)S(1)}, f32[4,8,128]{2,1,0:T(8,128)S(1)}, u32[]{:S(2)}, u32[]{:S(2)}) collective-permute-start(f32[4,8,128]{2,1,0:T(8,128)S(1)} %fusion.4), channel_id=1, source_target_pairs={{0,0},{16,1},{32,2},{48,3},{64,4},{80,5},{96,6},{112,7},{224,8},{2... | collective-permute-start | bytes 49160 | tf_op jit(solution)/shard_map/ppermute | solution.py:346

commit v2 on v1

v2 whole, which is shorter than its diff:
```python
import functools

import jax
import jax.numpy as jnp
import numpy as np
from jax import lax
from jax.experimental import pallas as pl
from jax.experimental.pallas import tpu as pltpu
from jax.sharding import PartitionSpec as P


STEPS = 4
SWEEPS = 5
CSWEEPS = 2
TAU = 0.25
LINE = 16
ROWS = 8
NX = 64
CZ = 128
FINE_HALO = 5
S_HALO = 8

CHIP = [c if c < 4 else 11 - c for c in range(8)]
BLOCK_OF = [2 * CHIP[m // 2] + m % 2 for m in range(LINE)]
HOLDER = [BLOCK_OF.index(q) for q in range(LINE)]


def sweep_constants(scale, sweeps):
    upper = 2.0 + 12.0 * scale
    center = (upper + 0.5) / 2.0
    radius = (upper - 0.5) / 2.0
    ratio = center / radius
    weight = 1.0 / ratio
    pairs = []
    for _ in range(sweeps):
        weight_next = 1.0 / (2.0 * ratio - weight)
        pairs.append((weight_next * weight, 2.0 * weight_next / radius))
        weight = weight_next
    return 1.0 / center, pairs


def near_sum(now, row):
    row_id = lax.broadcasted_iota(jnp.int32, (NX, CZ), 0)
    lane_id = lax.broadcasted_iota(jnp.int32, (NX, CZ), 1)
    x = now[row]
    near = now[row - 1] + now[row + 1]
    near = near + jnp.where(row_id == 0, 0.0, pltpu.roll(x, 1, 0))
    near = near + jnp.where(row_id == NX - 1, 0.0, pltpu.roll(x, NX - 1, 0))
    near = near + jnp.where(lane_id == 0, 0.0, pltpu.roll(x, 1, 1))
    near = near + jnp.where(lane_id == CZ - 1, 0.0, pltpu.roll(x, CZ - 1, 1))
    return x, near


def solve(block, height, lo, hi, cond_at, rhs, a, b, scale, sweeps, store):
    inverse, pairs = sweep_constants(scale, sweeps)
    low = jnp.where(block > 0, 1.0, 0.0)
    high = jnp.where(block < LINE - 1, 1.0, 0.0)
    old, now = None, None
    for k, (alpha, beta) in enumerate(pairs):
        own = 1.0 + alpha - 6.0 * scale * beta
        unit = inverse if k == 0 else 1.0
        target = (a, b)[k % 2]
        for row in range(lo + k + 1, hi - k - 1):
            gain = unit * beta * scale
            if row < height:
                gain = gain * low
            elif row >= height + ROWS:
                gain = gain * high
            if k == 0:
                x, near = near_sum(rhs, row)
                new = x * ((inverse * own + beta) - (inverse * beta) * cond_at(row)) + gain * near
            else:
                x, near = near_sum(now, row)
                new = x * (own - beta * cond_at(row)) + gain * near
                if k == 1:
                    new = new + (beta - alpha * inverse) * rhs[row]
                else:
                    new = new + beta * rhs[row] - alpha * old[row]
            if k == sweeps - 1:
                store(row, new)
            else:
                target[row] = new
        old, now = now, target


def write_edges(parity, source, at, height, out_i, out_x):
    top = ROWS - height
    from_i = jnp.where(parity == 0, top, 0)
    out_i[...] = source[pl.ds(at + from_i, height)]
    out_x[...] = source[pl.ds(at + top - from_i, height)]


def places(parity, height):
    far = height + ROWS
    place_i = jnp.where(parity == 0, far, 0)
    return place_i, far - place_i


def pack_kernel(cond, coil, start, out, sems):
    copies = []
    for place, field in enumerate((cond, coil, start)):
        for m in range(LINE):
            copies.append(
                pltpu.make_async_copy(
                    field.at[:, pl.ds(BLOCK_OF[m] * ROWS, ROWS), :], out.at[m, :, place], sems.at[place * LINE + m]
                )
            )
    for copy in copies:
        copy.start()
    for copy in copies:
        copy.wait()


def unpack_kernel(info, packed, cond, coil, start, edge_i, edge_x):
    for row in range(ROWS):
        for place, out in enumerate((cond, coil, start)):
            out[row] = packed[pl.ds(place * ROWS + row, NX, stride=3 * ROWS), :]
    parity = info[1]
    at = 0
    for out, height in ((cond, S_HALO), (coil, FINE_HALO), (start, FINE_HALO)):
        write_edges(parity, out, 0, height, edge_i.at[pl.ds(at, height)], edge_x.at[pl.ds(at, height)])
        at += height


def gather_kernel(info, cond, coil, halo_i, halo_x, cond_all, coil_all):
    at = 0
    for own, target, height in ((cond, cond_all, S_HALO), (coil, coil_all, FINE_HALO)):
        place_i, place_x = places(info[1], height)
        target[pl.ds(height, ROWS)] = own[...]
        target[pl.ds(place_i, height)] = halo_i[pl.ds(at, height)]
        target[pl.ds(place_x, height)] = halo_x[pl.ds(at, height)]
        at += height


def first_kernel(info, cond, coil, own, halo_i, halo_x, state, edge_i, edge_x, cond_all, coil_all, a, b, rhs):
    gather_kernel(info, cond, coil, halo_i, halo_x, cond_all, coil_all)
    fine_kernel(
        S_HALO + FINE_HALO, 0, info, cond_all, coil_all, own, halo_i, halo_x, state, edge_i, edge_x, a, b, rhs
    )


def fine_kernel(halo_at, step, info, cond, coil, own, halo_i, halo_x, state, edge_i, edge_x, a, b, rhs):
    block, parity = info[0], info[1]
    height = FINE_HALO
    total = ROWS + 2 * height
    drive = TAU * info[3 + step].astype(jnp.float32)
    shift = S_HALO - height
    place_i, place_x = places(parity, height)
    for at, size, field, start in (
        (height, ROWS, own, 0),
        (place_i, height, halo_i, halo_at),
        (place_x, height, halo_x, halo_at),
    ):
        for row in range(size):
            rhs[at + row] = cond[at + row + shift] * field[start + row] + drive * coil[at + row]

    def store(row, value):
        state[row - height] = value

    solve(block, height, 0, total, lambda row: cond[row + shift], rhs, a, b, TAU, SWEEPS, store)
    write_edges(parity, state, 0, height, edge_i, edge_x)


def coarse_kernel(power, height, halo_at, info, cond, own, halo_i, halo_x, *rest):
    outs, (a, b, c) = rest[:-3], rest[-3:]
    block, parity = info[0], info[1]
    scale = 4.0 * TAU
    shift = S_HALO - height
    place_i, place_x = places(parity, height)
    for at, size, field, start in (
        (height, ROWS, own, 0),
        (place_i, height, halo_i, halo_at),
        (place_x, height, halo_x, halo_at),
    ):
        for row in range(size):
            a[at + row] = cond[at + row + shift] * field[start + row]
    lo, hi = height - CSWEEPS * power, height + ROWS + CSWEEPS * power
    rhs, result = a, c
    for turn in range(power):
        if turn + 1 < power:

            def store(row, value, result=result):
                result[row] = cond[row + shift] * value

        else:

            def store(row, value):
                outs[0][row - height] = value

        solve(block, height, lo, hi, lambda row: cond[row + shift], rhs, b, None, scale, CSWEEPS, store)
        rhs, result = result, rhs
        lo, hi = lo + CSWEEPS, hi - CSWEEPS
    if len(outs) > 1:
        write_edges(parity, outs[0], 0, ROWS, outs[1], outs[2])


def combine_kernel(height, first, info, left, right, out, edge_i, edge_x):
    value = right[...]
    if first:
        value = value * jnp.where(info[2] == LINE - 1, 0.0, -1.0)
    out[...] = left[...] + value
    write_edges(info[1], out, 0, height, edge_i, edge_x)


def columns_kernel(*refs):
    fields, out = refs[:-1], refs[-1]
    for row in range(ROWS):
        for place, field in enumerate(fields):
            value = field[row]
            for m in range(LINE):
                first = (m * len(fields) + place) * (NX // LINE) * ROWS
                out[pl.ds(first + row, NX // LINE, stride=ROWS), :] = value[m * 4 : m * 4 + 4]


def final_kernel(left, right, out):
    for row in range(ROWS):
        out[pl.ds(row, NX, stride=ROWS), :] = left[row] + right[row]


def lay_out_kernel(blocks, out, sems):
    copies = []
    for m in range(LINE):
        target = out.at[0, :, pl.ds(BLOCK_OF[m] * ROWS, ROWS), :]
        copies.append(pltpu.make_async_copy(blocks.at[m], target, sems.at[m]))
    for copy in copies:
        copy.start()
    for copy in copies:
        copy.wait()


def move(kernel, out, count, from_hbm, to_hbm, *args):
    source = pltpu.HBM if from_hbm else pltpu.VMEM
    return pl.pallas_call(
        kernel,
        out_shape=out,
        in_specs=[pl.BlockSpec(memory_space=source)] * len(args),
        out_specs=pl.BlockSpec(memory_space=pltpu.HBM if to_hbm else pltpu.VMEM),
        scratch_shapes=[pltpu.SemaphoreType.DMA((count,))],
        compiler_params=pltpu.CompilerParams(vmem_limit_bytes=60 << 20),
    )(*args)


def shape(*dims):
    return jax.ShapeDtypeStruct(dims, jnp.float32)


def tile(rows=ROWS):
    return shape(rows, NX, CZ)


def call(kernel, outs, scratch, flops, *args):
    size = sum(int(np.prod(o.shape)) for o in outs) + sum(int(np.prod(a.shape)) for a in args)
    spaces = [pltpu.SMEM if a.dtype == jnp.int32 else pltpu.VMEM for a in args]
    return pl.pallas_call(
        kernel,
        out_shape=outs,
        in_specs=[pl.BlockSpec(memory_space=space) for space in spaces],
        out_specs=[pl.BlockSpec(memory_space=pltpu.VMEM)] * len(outs),
        scratch_shapes=[pltpu.VMEM((rows, NX, CZ), jnp.float32) for rows in scratch],
        cost_estimate=pl.CostEstimate(flops=flops, bytes_accessed=4 * size, transcendentals=0),
        compiler_params=pltpu.CompilerParams(vmem_limit_bytes=24 << 20),
    )(*args)


def swap_halos(edge_i, edge_x):
    inner = [(m, m ^ 1) for m in range(LINE)]
    outer = []
    for q in range(1, LINE - 1, 2):
        outer += [(HOLDER[q], HOLDER[q + 1]), (HOLDER[q + 1], HOLDER[q])]
    halo_x = lax.ppermute(edge_x, "mesh", outer)
    halo_i = lax.ppermute(edge_i, "mesh", inner)
    return halo_i, halo_x


def later(value, distance, shift=0):
    route = [((p - 1) % LINE, (p + distance - 1 + shift) % LINE) for p in range(LINE) if p + distance < LINE]
    return lax.ppermute(value, "tm", route)


def dft_table(sample_times, total, harmonics):
    orders = jnp.arange(1, harmonics + 1, dtype=jnp.int32)
    product = orders[:, None] * sample_times[None, :] % total
    angle = 2.0 * jnp.pi / total * product.astype(jnp.float32)
    return jnp.concatenate([jnp.cos(angle), -jnp.sin(angle)], axis=0)


def z_difference(field):
    inner = field[..., 1:] - field[..., :-1]
    return jnp.concatenate([inner, jnp.zeros_like(field[..., :1])], axis=-1)


def loss_sums(spectrum, total):
    harmonics = total // 2
    real_part = spectrum[:harmonics]
    imag_part = spectrum[harmonics:]
    power = (real_part * real_part + imag_part * imag_part) * (2.0 / total) ** 2
    freq = (jnp.arange(1, harmonics + 1, dtype=jnp.int32).astype(jnp.float32) / harmonics).reshape(-1, 1, 1, 1)
    root = jnp.sqrt(power)
    terms = (freq * power, (freq * freq) * power, freq**1.5 * (root * jnp.sqrt(root)))
    return jnp.stack([jnp.sum(term, axis=0) for term in terms], axis=0)


def by_cell(states):
    count = len(states)
    (packed,) = call(columns_kernel, [shape(LINE * count * 4 * ROWS, CZ)], [], 0, *states)
    packed = lax.all_to_all(packed.reshape(LINE, count, 4, ROWS, CZ), "tm", 0, 0, tiled=True)
    return packed.reshape(LINE * count, 4, ROWS, CZ)


def iteration(slice_start, conductivity, coil_current, switching, loss_coeffs):
    total = STEPS * LINE
    block = jnp.asarray(BLOCK_OF, jnp.int32)[lax.axis_index("mesh")]
    info = jnp.concatenate([jnp.stack([block, block % 2, lax.axis_index("tm")]), switching]).astype(jnp.int32)

    fields = move(
        pack_kernel, shape(LINE, 4, 3, ROWS, CZ), 3 * LINE, True, False, conductivity, coil_current, slice_start[0]
    )
    packed = lax.all_to_all(fields, "mesh", 0, 0, tiled=True)

    packed = packed.reshape(LINE * 4 * 3 * ROWS, CZ)

    edge_rows = S_HALO + 2 * FINE_HALO
    cond, coil, start, edge_i, edge_x = call(
        unpack_kernel, [tile(), tile(), tile(), tile(edge_rows), tile(edge_rows)], [], 0, info, packed
    )
    rows = ROWS + 2 * FINE_HALO
    halo_i, halo_x = first_i, first_x = swap_halos(edge_i, edge_x)
    state, edge_i, edge_x, cond_all, coil_all = call(
        first_kernel,
        [tile(), tile(FINE_HALO), tile(FINE_HALO), tile(ROWS + 2 * S_HALO), tile(rows)],
        [rows] * 3,
        20 * SWEEPS * rows * NX * CZ,
        info,
        cond,
        coil,
        start,
        halo_i,
        halo_x,
    )

    def coarse(power, height, halo_at, value, halo_i, halo_x, edges=0):
        rows = ROWS + 2 * height
        return call(
            functools.partial(coarse_kernel, power, height, halo_at),
            [tile()] + [tile()] * edges,
            [rows] * 3,
            20 * CSWEEPS * power * rows * NX * CZ,
            info,
            cond_all,
            value,
            halo_i,
            halo_x,
        )

    (coarse_start,) = coarse(1, FINE_HALO, S_HALO + FINE_HALO, start, first_i, first_x)
    states = [state]
    for step in range(1, STEPS):
        halo_i, halo_x = swap_halos(edge_i, edge_x)
        if step == STEPS - 1:
            early = by_cell(states)
        state, edge_i, edge_x = call(
            functools.partial(fine_kernel, 0, step),
            [tile(), tile(FINE_HALO), tile(FINE_HALO)],
            [rows] * 3,
            20 * SWEEPS * rows * NX * CZ,
            info,
            cond_all,
            coil_all,
            state,
            halo_i,
            halo_x,
        )
        states.append(state)
    value, other = state, coarse_start
    for power in (1, 2, 4):
        value, edge_i, edge_x = call(
            functools.partial(combine_kernel, 2 * power, power == 1),
            [tile(), tile(2 * power), tile(2 * power)],
            [],
            0,
            info,
            value,
            other,
        )
        halo_i, halo_x = swap_halos(edge_i, edge_x)
        (moved,) = coarse(power, 2 * power, 0, value, halo_i, halo_x)
        other = later(moved, power)
    value, edge_i, edge_x = call(
        functools.partial(combine_kernel, ROWS, False), [tile()] * 3, [], 0, info, value, other
    )
    value, edge_i, edge_x, late = lax.optimization_barrier((value, edge_i, edge_x, states[-1]))
    final = by_cell([late])
    table = dft_table(jnp.arange(total, dtype=jnp.int32), total, total // 2).reshape(total, LINE, STEPS)
    first_steps = table[:, :, : STEPS - 1].reshape(total, -1)
    spectrum = jnp.einsum("kt,txyz->kxyz", first_steps, z_difference(early), precision=lax.Precision.HIGHEST)
    last_step = table[:, :, STEPS - 1]
    spectrum += jnp.einsum("kt,txyz->kxyz", last_step, z_difference(final), precision=lax.Precision.HIGHEST)
    sums = loss_sums(spectrum, total)

    left = later(value, 0, shift=1)
    halo_i, halo_x = swap_halos(edge_i, edge_x)
    moved, edge_i, edge_x = coarse(4, ROWS, 0, value, halo_i, halo_x, edges=2)
    halo_i, halo_x = swap_halos(edge_i, edge_x)
    (moved,) = coarse(4, ROWS, 0, moved, halo_i, halo_x)
    right = later(moved, 8, shift=1)
    right, sums = lax.optimization_barrier((right, sums))
    (out,) = call(final_kernel, [shape(NX * ROWS, CZ)], [], 0, left, right)
    out = lax.all_to_all(out.reshape(LINE, 4, ROWS, CZ), "mesh", 0, 0, tiled=True)
    route = [(m * LINE + t, t * LINE + BLOCK_OF[m]) for m in range(LINE) for t in range(LINE)]
    sums = lax.ppermute(sums, ("mesh", "tm"), route)
    loss_density = jnp.sum(loss_coeffs * sums, axis=0)
    next_start = move(lay_out_kernel, shape(1, 4, LINE * ROWS, CZ), LINE, False, True, out)
    return next_start, loss_density


def solution(mesh):
    placed = (
        P("tm", "mesh", None, None),
        P("mesh", None, None),
        P("mesh", None, None),
        P("tm"),
        P(None, "mesh", "tm", None),
    )
    return jax.shard_map(
        iteration,
        mesh=mesh,
        in_specs=placed,
        out_specs=(P("tm", "mesh", None, None), P("mesh", "tm", None)),
        check_vma=False,
    )
```

time: 283 us -> 230 us (0.81)
  the two profiles are of different devices: /device:TPU:160 before, /device:TPU:168 now
where the time goes in v2:
time: 230 us; the launch traced here: 229 us
  waiting for transfers between devices  106 us (46%)
  starting transfers between devices  77.1 us (34%)
  Pallas kernels  32 us (14%)
  local copies, waits for them, and re-layouts  4.51 us (2%)
  other arithmetic  4.14 us (2%)
  between operations  3.21 us (1%)
    ppermute x5, waiting for transfers between devices, later(): return lax.ppermute(value, 'tm', route)  56.1 us
    ppermute x9, waiting for transfers between devices, swap_halos(): halo_x = lax.ppermute(edge_x, 'mesh', outer)  30.5 us
    pallas_call x18, Pallas kernels, call(): pl.pallas_call(kernel, out_shape=outs, in_specs=[pl.BlockSpec(memory_spac...  27.8 us
    ppermute x9, starting transfers between devices, swap_halos(): halo_x = lax.ppermute(edge_x, 'mesh', outer)  25 us
    all_to_all x2, starting transfers between devices, by_cell(): lax.all_to_all(packed.reshape(LINE, count, 4, ROWS, CZ), 'tm', 0, 0, tile...  17.3 us
    ppermute x1, waiting for transfers between devices, iteration(): sums = lax.ppermute(sums, ('mesh', 'tm'), route)  13.2 us
    ppermute x5, starting transfers between devices, later(): return lax.ppermute(value, 'tm', route)  10.4 us
    all_to_all x1, starting transfers between devices, iteration(): lax.all_to_all(out.reshape(LINE, 4, ROWS, CZ), 'mesh', 0, 0, tiled=True)  9.01 us
  transfers between devices with their start and end apart: 28, of which 13 were waited for; matrix products, arithmetic and copies ran while one was open for 4% of the time, Pallas kernels for 8%

profile of v2, /device:TPU:168, one launch (start us, length us, event | category | flops | bytes accessed | tf_op | source)
XLA Modules:
  0.0 229.1 jit_solution(5804935592916357539)
XLA Ops:
  0.6 2.4 %shard_map.77 = f32[16,4,3,8,128]{4,3,2,1,0:T(8,128)} custom-call(f32[4,128,128]{2,1,0:T(8,128)} %cond.1, f32[4,128,128]{2,1,0:T(8,128)} %coil.1, f32[4,128,128]{2,1,0:T(8,128)} %bitcast.31), custom_call_target="tpu_custom_call" | custom-call | tf_op jit(solution)/shard_map/pallas_call | solution.py:233
  3.0 7.4 %all-to-all-start = ((f32[16,4,3,8,128]{4,3,2,1,0:T(8,128)}), f32[16,4,3,8,128]{4,3,2,1,0:T(8,128)S(1)}, u32[]{:S(2)}, u32[]{:S(2)}) async-start(f32[16,4,3,8,128]{4,3,2,1,0:T(8,128)} %shard_map.77), calls=%async_computation | async-start | bytes 1572864 | tf_op jit(solution)/shard_map/all_to_all | solution.py:318
  15.0 6.2 %all-to-all-done = f32[16,4,3,8,128]{4,3,2,1,0:T(8,128)S(1)} async-done(((f32[16,4,3,8,128]{4,3,2,1,0:T(8,128)}), f32[16,4,3,8,128]{4,3,2,1,0:T(8,128)S(1)}, u32[]{:S(2)}, u32[]{:S(2)}) %all-to-all-start) | async-done | bytes 786464 | tf_op jit(solution)/shard_map/all_to_all | solution.py:318
  23.0 5.5 %collective-permute-start.1 = (f32[18,64,128]{2,1,0:T(8,128)S(1)}, f32[18,64,128]{2,1,0:T(8,128)S(1)}, u32[]{:S(2)}, u32[]{:S(2)}) collective-permute-start(f32[18,64,128]{2,1,0:T(8,128)S(1)} %get-tuple-element.44), channel_id=1, source_target_pairs={{16,32},{32,16},{48,64},{64,48},{80,96},{96,80},{112,224},{224,112... | collective-permute-start | bytes 1769480 | tf_op jit(solution)/shard_map/ppermute | solution.py:270
  28.6 7.5 %collective-permute-done.1.halo_x = f32[18,64,128]{2,1,0:T(8,128)S(1)} collective-permute-done((f32[18,64,128]{2,1,0:T(8,128)S(1)}, f32[18,64,128]{2,1,0:T(8,128)S(1)}, u32[]{:S(2)}, u32[]{:S(2)}) %collective-permute-start.1) | collective-permute-done | bytes 589856 | tf_op jit(solution)/shard_map/ppermute | solution.py:270
  36.1 2.1 shard_map.79
  38.3 3.6 %collective-permute-start.3 = (f32[5,64,128]{2,1,0:T(8,128)S(1)}, f32[5,64,128]{2,1,0:T(8,128)S(1)}, u32[]{:S(2)}, u32[]{:S(2)}) collective-permute-start(f32[5,64,128]{2,1,0:T(8,128)S(1)} %get-tuple-element.49), channel_id=1, source_target_pairs={{16,32},{32,16},{48,64},{64,48},{80,96},{96,80},{112,224},{224,112... | collective-permute-start | bytes 491528 | tf_op jit(solution)/shard_map/ppermute | solution.py:270
  42.0 3.0 %collective-permute-done.3.halo_x = f32[5,64,128]{2,1,0:T(8,128)S(1)} collective-permute-done((f32[5,64,128]{2,1,0:T(8,128)S(1)}, f32[5,64,128]{2,1,0:T(8,128)S(1)}, u32[]{:S(2)}, u32[]{:S(2)}) %collective-permute-start.3) | collective-permute-done | bytes 163872 | tf_op jit(solution)/shard_map/ppermute | solution.py:270
  47.5 3.2 %collective-permute-start.5 = (f32[5,64,128]{2,1,0:T(8,128)S(1)}, f32[5,64,128]{2,1,0:T(8,128)S(1)}, u32[]{:S(2)}, u32[]{:S(2)}) collective-permute-start(f32[5,64,128]{2,1,0:T(8,128)S(1)} %get-tuple-element.52), channel_id=1, source_target_pairs={{16,32},{32,16},{48,64},{64,48},{80,96},{96,80},{112,224},{224,112... | collective-permute-start | bytes 491528 | tf_op jit(solution)/shard_map/ppermute | solution.py:270
  50.7 3.4 %collective-permute-done.5.halo_x = f32[5,64,128]{2,1,0:T(8,128)S(1)} collective-permute-done((f32[5,64,128]{2,1,0:T(8,128)S(1)}, f32[5,64,128]{2,1,0:T(8,128)S(1)}, u32[]{:S(2)}, u32[]{:S(2)}) %collective-permute-start.5) | collective-permute-done | bytes 163872 | tf_op jit(solution)/shard_map/ppermute | solution.py:270
  54.2 2.8 %shard_map.81 = (f32[8,64,128]{2,1,0:T(8,128)S(1)}, f32[5,64,128]{2,1,0:T(8,128)}, f32[5,64,128]{2,1,0:T(8,128)}) custom-call(s32[7]{0:T(128)S(1)} %pad_add_fusion.info, f32[24,64,128]{2,1,0:T(8,128)S(1)} %get-tuple-element.45.cond, f32[18,64,128]{2,1,0:T(8,128)S(1)} %get-tuple-element.46.coil, f32[8,64,128]{2,1,0:T(8,128)S(1)} %get-tuple-element.50.own.refs_1_, ...), custom_call_target="tpu_custom_call" | custom-call | flops 14745600 | bytes 2555932 | tf_op jit(solution)/shard_map/pallas_call | solution.py:254
  57.2 2.9 %collective-permute-start.7 = (f32[5,64,128]{2,1,0:T(8,128)}, f32[5,64,128]{2,1,0:T(8,128)S(1)}, u32[]{:S(2)}, u32[]{:S(2)}) collective-permute-start(f32[5,64,128]{2,1,0:T(8,128)} %get-tuple-element.55), channel_id=1, source_target_pairs={{16,32},{32,16},{48,64},{64,48},{80,96},{96,80},{112,224},{224,112... | collective-permute-start | bytes 491528 | tf_op jit(solution)/shard_map/ppermute | solution.py:270
  61.2 6.8 %all-to-all-start.1 = ((f32[16,3,4,8,128]{4,3,2,1,0:T(8,128)}), f32[16,3,4,8,128]{4,3,2,1,0:T(8,128)}, u32[]{:S(2)}, u32[]{:S(2)}) async-start(f32[16,3,4,8,128]{4,3,2,1,0:T(8,128)} %bitcast.6), calls=%async_computation.1 | async-start | bytes 1572864 | tf_op jit(solution)/shard_map/all_to_all | solution.py:306
  69.1 2.7 %shard_map.82 = (f32[8,64,128]{2,1,0:T(8,128)S(1)}, f32[5,64,128]{2,1,0:T(8,128)}, f32[5,64,128]{2,1,0:T(8,128)}) custom-call(s32[7]{0:T(128)S(1)} %pad_add_fusion.info, f32[24,64,128]{2,1,0:T(8,128)S(1)} %get-tuple-element.45.cond, f32[18,64,128]{2,1,0:T(8,128)S(1)} %get-tuple-element.46.coil, f32[8,64,128]{2,1,0:T(8,128)S(1)} %get-tuple-element.53.own.refs_2_, ...), custom_call_target="tpu_custom_call" | custom-call | flops 14745600 | bytes 2555932 | tf_op jit(solution)/shard_map/pallas_call | solution.py:254
  76.1 3.6 %collective-permute-done.9.halo_x = f32[2,64,128]{2,1,0:T(8,128)S(1)} collective-permute-done((f32[2,64,128]{2,1,0:T(8,128)S(1)}, f32[2,64,128]{2,1,0:T(8,128)S(1)}, u32[]{:S(2)}, u32[]{:S(2)}) %collective-permute-start.9) | collective-permute-done | bytes 65568 | tf_op jit(solution)/shard_map/ppermute | solution.py:270
  80.7 3.4 %collective-permute-start.10 = (f32[8,64,128]{2,1,0:T(8,128)S(1)}, f32[8,64,128]{2,1,0:T(8,128)S(1)}, u32[]{:S(2)}, u32[]{:S(2)}) collective-permute-start(f32[8,64,128]{2,1,0:T(8,128)S(1)} %shard_map.85), channel_id=1, source_target_pairs={{15,0},{0,1},{1,2},{2,3},{3,4},{4,5},{5,6},{6,7},{7,8},{8,9},{9,10... | collective-permute-start | bytes 786440 | tf_op jit(solution)/shard_map/ppermute | solution.py:277
  84.1 9.9 %collective-permute-done.10.right = f32[8,64,128]{2,1,0:T(8,128)S(1)} collective-permute-done((f32[8,64,128]{2,1,0:T(8,128)S(1)}, f32[8,64,128]{2,1,0:T(8,128)S(1)}, u32[]{:S(2)}, u32[]{:S(2)}) %collective-permute-start.10) | collective-permute-done | bytes 262176 | tf_op jit(solution)/shard_map/ppermute | solution.py:277
  97.2 4.3 %collective-permute-done.12.halo_x = f32[4,64,128]{2,1,0:T(8,128)S(1)} collective-permute-done((f32[4,64,128]{2,1,0:T(8,128)S(1)}, f32[4,64,128]{2,1,0:T(8,128)S(1)}, u32[]{:S(2)}, u32[]{:S(2)}) %collective-permute-start.12) | collective-permute-done | bytes 131104 | tf_op jit(solution)/shard_map/ppermute | solution.py:270
  103.1 2.7 %collective-permute-start.13 = (f32[8,64,128]{2,1,0:T(8,128)S(1)}, f32[8,64,128]{2,1,0:T(8,128)S(1)}, u32[]{:S(2)}, u32[]{:S(2)}) collective-permute-start(f32[8,64,128]{2,1,0:T(8,128)S(1)} %shard_map.87), channel_id=1, source_target_pairs={{15,1},{0,2},{1,3},{2,4},{3,5},{4,6},{5,7},{6,8},{7,9},{8,10},{9,1... | collective-permute-start | bytes 786440 | tf_op jit(solution)/shard_map/ppermute | solution.py:277
  105.8 7.9 %collective-permute-done.13.right = f32[8,64,128]{2,1,0:T(8,128)S(1)} collective-permute-done((f32[8,64,128]{2,1,0:T(8,128)S(1)}, f32[8,64,128]{2,1,0:T(8,128)S(1)}, u32[]{:S(2)}, u32[]{:S(2)}) %collective-permute-start.13) | collective-permute-done | bytes 262176 | tf_op jit(solution)/shard_map/ppermute | solution.py:277
  116.5 5.5 %collective-permute-done.15.halo_x = f32[8,64,128]{2,1,0:T(8,128)S(1)} collective-permute-done((f32[8,64,128]{2,1,0:T(8,128)S(1)}, f32[8,64,128]{2,1,0:T(8,128)S(1)}, u32[]{:S(2)}, u32[]{:S(2)}) %collective-permute-start.15) | collective-permute-done | bytes 262176 | tf_op jit(solution)/shard_map/ppermute | solution.py:270
  122.1 3.0 %shard_map.89 = f32[8,64,128]{2,1,0:T(8,128)S(1)} custom-call(s32[7]{0:T(128)S(1)} %pad_add_fusion.info, f32[24,64,128]{2,1,0:T(8,128)S(1)} %get-tuple-element.45.cond, f32[8,64,128]{2,1,0:T(8,128)S(1)} %get-tuple-element.63.own.left, f32[8,64,128]{2,1,0:T(8,128)S(1)} %collective-permute-done.14.halo_i, f32[8,64,128]{2,1,0:T(8,128)S(1)} %collective-permute-done.15.halo_x), custom_call_target="tpu_custom_call" | custom-call | flops 31457280 | bytes 1835036 | tf_op jit(solution)/shard_map/pallas_call | solution.py:254
  125.1 3.0 %collective-permute-start.16 = (f32[8,64,128]{2,1,0:T(8,128)S(1)}, f32[8,64,128]{2,1,0:T(8,128)S(1)}, u32[]{:S(2)}, u32[]{:S(2)}) collective-permute-start(f32[8,64,128]{2,1,0:T(8,128)S(1)} %shard_map.89), channel_id=1, source_target_pairs={{15,3},{0,4},{1,5},{2,6},{3,7},{4,8},{5,9},{6,10},{7,11},{8,12},{9... | collective-permute-start | bytes 786440 | tf_op jit(solution)/shard_map/ppermute | solution.py:277
  128.2 14.4 %collective-permute-done.16.right = f32[8,64,128]{2,1,0:T(8,128)S(1)} collective-permute-done((f32[8,64,128]{2,1,0:T(8,128)S(1)}, f32[8,64,128]{2,1,0:T(8,128)S(1)}, u32[]{:S(2)}, u32[]{:S(2)}) %collective-permute-start.16) | collective-permute-done | bytes 262176 | tf_op jit(solution)/shard_map/ppermute | solution.py:277
  146.1 10.5 %all-to-all-start.2 = ((f32[16,1,4,8,128]{4,3,2,1,0:T(8,128)}), f32[16,1,4,8,128]{4,3,2,1,0:T(8,128)S(1)}, u32[]{:S(2)}, u32[]{:S(2)}) async-start(f32[16,1,4,8,128]{4,3,2,1,0:T(8,128)} %bitcast.12), calls=%async_computation.2 | async-start | bytes 524288 | tf_op jit(solution)/shard_map/all_to_all | solution.py:306
  160.0 3.0 %shard_map.91 = (f32[8,64,128]{2,1,0:T(8,128)S(1)}, f32[8,64,128]{2,1,0:T(8,128)S(1)}, f32[8,64,128]{2,1,0:T(8,128)S(1)}) custom-call(s32[7]{0:T(128)S(1)} %pad_add_fusion.info, f32[24,64,128]{2,1,0:T(8,128)S(1)} %get-tuple-element.45.cond, f32[8,64,128]{2,1,0:T(8,128)S(1)} %get-tuple-element.69.own, f32[8,64,128]{2,1,0:T(8,128)S(1)} %collective-permute-done.18.halo_i, ...), custom_call_target="tpu_custom_call" | custom-call | flops 31457280 | bytes 2359324 | tf_op jit(solution)/shard_map/pallas_call | solution.py:254
  164.5 2.1 collective-permute-start.21
  169.1 3.1 %collective-permute-done.21.halo_x = f32[8,64,128]{2,1,0:T(8,128)S(1)} collective-permute-done((f32[8,64,128]{2,1,0:T(8,128)S(1)}, f32[8,64,128]{2,1,0:T(8,128)S(1)}, u32[]{:S(2)}, u32[]{:S(2)}) %collective-permute-start.21) | collective-permute-done | bytes 262176 | tf_op jit(solution)/shard_map/ppermute | solution.py:270
  172.2 3.0 %shard_map.92 = f32[8,64,128]{2,1,0:T(8,128)S(1)} custom-call(s32[7]{0:T(128)S(1)} %pad_add_fusion.info, f32[24,64,128]{2,1,0:T(8,128)S(1)} %get-tuple-element.45.cond, f32[8,64,128]{2,1,0:T(8,128)S(1)} %get-tuple-element.72.own, f32[8,64,128]{2,1,0:T(8,128)S(1)} %collective-permute-done.20.halo_i, f32[8,64,128]{2,1,0:T(8,128)S(1)} %collective-permute-done.21.halo_x), custom_call_target="tpu_custom_call" | custom-call | flops 31457280 | bytes 1835036 | tf_op jit(solution)/shard_map/pallas_call | solution.py:254
  177.1 23.9 %collective-permute-done.22.right = f32[8,64,128]{2,1,0:T(8,128)S(1)} collective-permute-done((f32[8,64,128]{2,1,0:T(8,128)S(1)}, f32[8,64,128]{2,1,0:T(8,128)S(1)}, u32[]{:S(2)}, u32[]{:S(2)}) %collective-permute-start.22) | collective-permute-done | bytes 262176 | tf_op jit(solution)/shard_map/ppermute | solution.py:277
  201.7 9.0 %all-to-all-start.3 = ((f32[16,4,8,128]{3,2,1,0:T(8,128)}), f32[16,4,8,128]{3,2,1,0:T(8,128)S(1)}, u32[]{:S(2)}, u32[]{:S(2)}) async-start(f32[16,4,8,128]{3,2,1,0:T(8,128)} %bitcast.17), calls=%async_computation.3 | async-start | bytes 524288 | tf_op jit(solution)/shard_map/all_to_all | solution.py:408
  212.6 13.2 %collective-permute-done.23 = f32[3,4,8,128]{3,2,1,0:T(8,128)S(1)} collective-permute-done((f32[3,4,8,128]{3,2,1,0:T(8,128)S(1)}, f32[3,4,8,128]{3,2,1,0:T(8,128)S(1)}, u32[]{:S(2)}, u32[]{:S(2)}) %collective-permute-start.23) | collective-permute-done | bytes 49184 | tf_op jit(solution)/shard_map/ppermute | solution.py:410
  (73 shorter events, 40.8 us)
Async XLA Ops:
  3.0 18.2 %all-to-all-start = ((f32[16,4,3,8,128]{4,3,2,1,0:T(8,128)}), f32[16,4,3,8,128]{4,3,2,1,0:T(8,128)S(1)}, u32[]{:S(2)}, u32[]{:S(2)}) async-start(f32[16,4,3,8,128]{4,3,2,1,0:T(8,128)} %shard_map.77), calls=%async_computation | async-start | bytes 1572864 | tf_op jit(solution)/shard_map/all_to_all | solution.py:318
  13.6 0.7 copy-start.3
  22.0 6.6 %collective-permute-start = (f32[18,64,128]{2,1,0:T(8,128)S(1)}, f32[18,64,128]{2,1,0:T(8,128)S(1)}, u32[]{:S(2)}, u32[]{:S(2)}) collective-permute-start(f32[18,64,128]{2,1,0:T(8,128)S(1)} %get-tuple-element.43), channel_id=1, source_target_pairs={{0,16},{16,0},{32,48},{48,32},{64,80},{80,64},{96,112},{112,96},{1... | collective-permute-start | bytes 1769480 | tf_op jit(solution)/shard_map/ppermute | solution.py:271
  23.0 13.1 %collective-permute-start.1 = (f32[18,64,128]{2,1,0:T(8,128)S(1)}, f32[18,64,128]{2,1,0:T(8,128)S(1)}, u32[]{:S(2)}, u32[]{:S(2)}) collective-permute-start(f32[18,64,128]{2,1,0:T(8,128)S(1)} %get-tuple-element.44), channel_id=1, source_target_pairs={{16,32},{32,16},{48,64},{64,48},{80,96},{96,80},{112,224},{224,112... | collective-permute-start | bytes 1769480 | tf_op jit(solution)/shard_map/ppermute | solution.py:270
  38.2 3.7 %collective-permute-start.2 = (f32[5,64,128]{2,1,0:T(8,128)S(1)}, f32[5,64,128]{2,1,0:T(8,128)S(1)}, u32[]{:S(2)}, u32[]{:S(2)}) collective-permute-start(f32[5,64,128]{2,1,0:T(8,128)S(1)} %get-tuple-element.48), channel_id=1, source_target_pairs={{0,16},{16,0},{32,48},{48,32},{64,80},{80,64},{96,112},{112,96},{1... | collective-permute-start | bytes 491528 | tf_op jit(solution)/shard_map/ppermute | solution.py:271
  38.3 6.6 %collective-permute-start.3 = (f32[5,64,128]{2,1,0:T(8,128)S(1)}, f32[5,64,128]{2,1,0:T(8,128)S(1)}, u32[]{:S(2)}, u32[]{:S(2)}) collective-permute-start(f32[5,64,128]{2,1,0:T(8,128)S(1)} %get-tuple-element.49), channel_id=1, source_target_pairs={{16,32},{32,16},{48,64},{64,48},{80,96},{96,80},{112,224},{224,112... | collective-permute-start | bytes 491528 | tf_op jit(solution)/shard_map/ppermute | solution.py:270
  47.0 3.7 %collective-permute-start.4 = (f32[5,64,128]{2,1,0:T(8,128)S(1)}, f32[5,64,128]{2,1,0:T(8,128)S(1)}, u32[]{:S(2)}, u32[]{:S(2)}) collective-permute-start(f32[5,64,128]{2,1,0:T(8,128)S(1)} %get-tuple-element.51), channel_id=1, source_target_pairs={{0,16},{16,0},{32,48},{48,32},{64,80},{80,64},{96,112},{112,96},{1... | collective-permute-start | bytes 491528 | tf_op jit(solution)/shard_map/ppermute | solution.py:271
  47.5 6.6 %collective-permute-start.5 = (f32[5,64,128]{2,1,0:T(8,128)S(1)}, f32[5,64,128]{2,1,0:T(8,128)S(1)}, u32[]{:S(2)}, u32[]{:S(2)}) collective-permute-start(f32[5,64,128]{2,1,0:T(8,128)S(1)} %get-tuple-element.52), channel_id=1, source_target_pairs={{16,32},{32,16},{48,64},{64,48},{80,96},{96,80},{112,224},{224,112... | collective-permute-start | bytes 491528 | tf_op jit(solution)/shard_map/ppermute | solution.py:270
  56.9 12.2 %collective-permute-start.6 = (f32[5,64,128]{2,1,0:T(8,128)}, f32[5,64,128]{2,1,0:T(8,128)S(1)}, u32[]{:S(2)}, u32[]{:S(2)}) collective-permute-start(f32[5,64,128]{2,1,0:T(8,128)} %get-tuple-element.54), channel_id=1, source_target_pairs={{0,16},{16,0},{32,48},{48,32},{64,80},{80,64},{96,112},{112,96},{1... | collective-permute-start | bytes 491528 | tf_op jit(solution)/shard_map/ppermute | solution.py:271
  57.2 11.9 %collective-permute-start.7 = (f32[5,64,128]{2,1,0:T(8,128)}, f32[5,64,128]{2,1,0:T(8,128)S(1)}, u32[]{:S(2)}, u32[]{:S(2)}) collective-permute-start(f32[5,64,128]{2,1,0:T(8,128)} %get-tuple-element.55), channel_id=1, source_target_pairs={{16,32},{32,16},{48,64},{64,48},{80,96},{96,80},{112,224},{224,112... | collective-permute-start | bytes 491528 | tf_op jit(solution)/shard_map/ppermute | solution.py:270
  61.2 84.9 %all-to-all-start.1 = ((f32[16,3,4,8,128]{4,3,2,1,0:T(8,128)}), f32[16,3,4,8,128]{4,3,2,1,0:T(8,128)}, u32[]{:S(2)}, u32[]{:S(2)}) async-start(f32[16,3,4,8,128]{4,3,2,1,0:T(8,128)} %bitcast.6), calls=%async_computation.1 | async-start | bytes 1572864 | tf_op jit(solution)/shard_map/all_to_all | solution.py:306
  72.4 3.6 %collective-permute-start.8 = (f32[2,64,128]{2,1,0:T(8,128)S(1)}, f32[2,64,128]{2,1,0:T(8,128)S(1)}, u32[]{:S(2)}, u32[]{:S(2)}) collective-permute-start(f32[2,64,128]{2,1,0:T(8,128)S(1)} %get-tuple-element.58), channel_id=1, source_target_pairs={{0,16},{16,0},{32,48},{48,32},{64,80},{80,64},{96,112},{112,96},{1... | collective-permute-start | bytes 196616 | tf_op jit(solution)/shard_map/ppermute | solution.py:271
  74.1 5.6 %collective-permute-start.9 = (f32[2,64,128]{2,1,0:T(8,128)S(1)}, f32[2,64,128]{2,1,0:T(8,128)S(1)}, u32[]{:S(2)}, u32[]{:S(2)}) collective-permute-start(f32[2,64,128]{2,1,0:T(8,128)S(1)} %get-tuple-element.59), channel_id=1, source_target_pairs={{16,32},{32,16},{48,64},{64,48},{80,96},{96,80},{112,224},{224,112... | collective-permute-start | bytes 196616 | tf_op jit(solution)/shard_map/ppermute | solution.py:270
  80.7 13.3 %collective-permute-start.10 = (f32[8,64,128]{2,1,0:T(8,128)S(1)}, f32[8,64,128]{2,1,0:T(8,128)S(1)}, u32[]{:S(2)}, u32[]{:S(2)}) collective-permute-start(f32[8,64,128]{2,1,0:T(8,128)S(1)} %shard_map.85), channel_id=1, source_target_pairs={{15,0},{0,1},{1,2},{2,3},{3,4},{4,5},{5,6},{6,7},{7,8},{8,9},{9,10... | collective-permute-start | bytes 786440 | tf_op jit(solution)/shard_map/ppermute | solution.py:277
  94.6 2.6 %collective-permute-start.11 = (f32[4,64,128]{2,1,0:T(8,128)S(1)}, f32[4,64,128]{2,1,0:T(8,128)S(1)}, u32[]{:S(2)}, u32[]{:S(2)}) collective-permute-start(f32[4,64,128]{2,1,0:T(8,128)S(1)} %get-tuple-element.61), channel_id=1, source_target_pairs={{0,16},{16,0},{32,48},{48,32},{64,80},{80,64},{96,112},{112,96},{1... | collective-permute-start | bytes 393224 | tf_op jit(solution)/shard_map/ppermute | solution.py:271
  95.3 6.3 %collective-permute-start.12 = (f32[4,64,128]{2,1,0:T(8,128)S(1)}, f32[4,64,128]{2,1,0:T(8,128)S(1)}, u32[]{:S(2)}, u32[]{:S(2)}) collective-permute-start(f32[4,64,128]{2,1,0:T(8,128)S(1)} %get-tuple-element.62), channel_id=1, source_target_pairs={{16,32},{32,16},{48,64},{64,48},{80,96},{96,80},{112,224},{224,112... | collective-permute-start | bytes 393224 | tf_op jit(solution)/shard_map/ppermute | solution.py:270
  103.1 10.6 %collective-permute-start.13 = (f32[8,64,128]{2,1,0:T(8,128)S(1)}, f32[8,64,128]{2,1,0:T(8,128)S(1)}, u32[]{:S(2)}, u32[]{:S(2)}) collective-permute-start(f32[8,64,128]{2,1,0:T(8,128)S(1)} %shard_map.87), channel_id=1, source_target_pairs={{15,1},{0,2},{1,3},{2,4},{3,5},{4,6},{5,7},{6,8},{7,9},{8,10},{9,1... | collective-permute-start | bytes 786440 | tf_op jit(solution)/shard_map/ppermute | solution.py:277
  114.3 2.3 collective-permute-start.14
  114.4 7.7 %collective-permute-start.15 = (f32[8,64,128]{2,1,0:T(8,128)S(1)}, f32[8,64,128]{2,1,0:T(8,128)S(1)}, u32[]{:S(2)}, u32[]{:S(2)}) collective-permute-start(f32[8,64,128]{2,1,0:T(8,128)S(1)} %get-tuple-element.65), channel_id=1, source_target_pairs={{16,32},{32,16},{48,64},{64,48},{80,96},{96,80},{112,224},{224,112... | collective-permute-start | bytes 786440 | tf_op jit(solution)/shard_map/ppermute | solution.py:270
  125.1 17.5 %collective-permute-start.16 = (f32[8,64,128]{2,1,0:T(8,128)S(1)}, f32[8,64,128]{2,1,0:T(8,128)S(1)}, u32[]{:S(2)}, u32[]{:S(2)}) collective-permute-start(f32[8,64,128]{2,1,0:T(8,128)S(1)} %shard_map.89), channel_id=1, source_target_pairs={{15,3},{0,4},{1,5},{2,6},{3,7},{4,8},{5,9},{6,10},{7,11},{8,12},{9... | collective-permute-start | bytes 786440 | tf_op jit(solution)/shard_map/ppermute | solution.py:277
  144.0 16.1 %collective-permute-start.18 = (f32[8,64,128]{2,1,0:T(8,128)S(1)}, f32[8,64,128]{2,1,0:T(8,128)S(1)}, u32[]{:S(2)}, u32[]{:S(2)}) collective-permute-start(f32[8,64,128]{2,1,0:T(8,128)S(1)} %get-tuple-element.70), channel_id=1, source_target_pairs={{0,16},{16,0},{32,48},{48,32},{64,80},{80,64},{96,112},{112,96},{1... | collective-permute-start | bytes 786440 | tf_op jit(solution)/shard_map/ppermute | solution.py:271
  144.1 15.9 %collective-permute-start.19 = (f32[8,64,128]{2,1,0:T(8,128)S(1)}, f32[8,64,128]{2,1,0:T(8,128)S(1)}, u32[]{:S(2)}, u32[]{:S(2)}) collective-permute-start(f32[8,64,128]{2,1,0:T(8,128)S(1)} %get-tuple-element.71), channel_id=1, source_target_pairs={{16,32},{32,16},{48,64},{64,48},{80,96},{96,80},{112,224},{224,112... | collective-permute-start | bytes 786440 | tf_op jit(solution)/shard_map/ppermute | solution.py:270
  146.0 54.9 %collective-permute-start.17 = (f32[8,64,128]{2,1,0:T(8,128)S(1)}, f32[8,64,128]{2,1,0:T(8,128)S(1)}, u32[]{:S(2)}, u32[]{:S(2)}) collective-permute-start(f32[8,64,128]{2,1,0:T(8,128)S(1)} %get-tuple-element.69.own), channel_id=1, source_target_pairs={{15,0},{0,1},{1,2},{2,3},{3,4},{4,5},{5,6},{6,7},{7,8},{8,9},{9,10... | collective-permute-start | bytes 786440 | tf_op jit(solution)/shard_map/ppermute | solution.py:277
  146.1 20.5 %all-to-all-start.2 = ((f32[16,1,4,8,128]{4,3,2,1,0:T(8,128)}), f32[16,1,4,8,128]{4,3,2,1,0:T(8,128)S(1)}, u32[]{:S(2)}, u32[]{:S(2)}) async-start(f32[16,1,4,8,128]{4,3,2,1,0:T(8,128)} %bitcast.12), calls=%async_computation.2 | async-start | bytes 524288 | tf_op jit(solution)/shard_map/all_to_all | solution.py:306
  163.0 6.1 %collective-permute-start.20 = (f32[8,64,128]{2,1,0:T(8,128)S(1)}, f32[8,64,128]{2,1,0:T(8,128)S(1)}, u32[]{:S(2)}, u32[]{:S(2)}) collective-permute-start(f32[8,64,128]{2,1,0:T(8,128)S(1)} %get-tuple-element.73), channel_id=1, source_target_pairs={{0,16},{16,0},{32,48},{48,32},{64,80},{80,64},{96,112},{112,96},{1... | collective-permute-start | bytes 786440 | tf_op jit(solution)/shard_map/ppermute | solution.py:271
  164.5 7.7 %collective-permute-start.21 = (f32[8,64,128]{2,1,0:T(8,128)S(1)}, f32[8,64,128]{2,1,0:T(8,128)S(1)}, u32[]{:S(2)}, u32[]{:S(2)}) collective-permute-start(f32[8,64,128]{2,1,0:T(8,128)S(1)} %get-tuple-element.74), channel_id=1, source_target_pairs={{16,32},{32,16},{48,64},{64,48},{80,96},{96,80},{112,224},{224,112... | collective-permute-start | bytes 786440 | tf_op jit(solution)/shard_map/ppermute | solution.py:270
  166.9 1.1 copy-start
  175.1 25.8 %collective-permute-start.22 = (f32[8,64,128]{2,1,0:T(8,128)S(1)}, f32[8,64,128]{2,1,0:T(8,128)S(1)}, u32[]{:S(2)}, u32[]{:S(2)}) collective-permute-start(f32[8,64,128]{2,1,0:T(8,128)S(1)} %shard_map.92), channel_id=1, source_target_pairs={{15,8},{0,9},{1,10},{2,11},{3,12},{4,13},{5,14},{6,15},{31,24},{16... | collective-permute-start | bytes 786440 | tf_op jit(solution)/shard_map/ppermute | solution.py:277
  201.7 24.1 %copy-start.2 = (f32[3,4,8,128]{3,2,1,0:T(8,128)S(1)}, f32[3,4,8,128]{3,2,1,0:T(8,128)}, u32[]{:S(2)}) copy-start(f32[3,4,8,128]{3,2,1,0:T(8,128)} %param.10) | copy-start | bytes 147460
  201.7 24.7 %all-to-all-start.3 = ((f32[16,4,8,128]{3,2,1,0:T(8,128)}), f32[16,4,8,128]{3,2,1,0:T(8,128)S(1)}, u32[]{:S(2)}, u32[]{:S(2)}) async-start(f32[16,4,8,128]{3,2,1,0:T(8,128)} %bitcast.17), calls=%async_computation.3 | async-start | bytes 524288 | tf_op jit(solution)/shard_map/all_to_all | solution.py:408
  210.7 15.1 %collective-permute-start.23 = (f32[3,4,8,128]{3,2,1,0:T(8,128)S(1)}, f32[3,4,8,128]{3,2,1,0:T(8,128)S(1)}, u32[]{:S(2)}, u32[]{:S(2)}) collective-permute-start(f32[3,4,8,128]{3,2,1,0:T(8,128)S(1)} %pad_maximum_fusion), channel_id=1, source_target_pairs={{0,0},{1,16},{2,32},{3,48},{4,64},{5,80},{6,96},{7,112},{8,128},{9... | collective-permute-start | bytes 147464 | tf_op jit(solution)/shard_map/ppermute | solution.py:410
  226.4 0.7 copy-start.1
  (1 other events, 0.7 us)

commit v3 on v2

--- a/solution.py
+++ b/solution.py
@@ -19,6 +19,7 @@
 CZ = 128
 FINE_HALO = 5
 S_HALO = 8
+DISTANCES = (8, 4, 2, 1)
 
 CHIP = [c if c < 4 else 11 - c for c in range(8)]
 BLOCK_OF = [2 * CHIP[m // 2] + m % 2 for m in range(LINE)]
@@ -194,11 +195,18 @@
         write_edges(parity, outs[0], 0, ROWS, outs[1], outs[2])
 
 
-def combine_kernel(height, first, info, left, right, out, edge_i, edge_x):
-    value = right[...]
-    if first:
-        value = value * jnp.where(info[2] == LINE - 1, 0.0, -1.0)
-    out[...] = left[...] + value
+def reaches(info, distance, moved):
+    position = lax.rem(info[2] + 1 + moved, LINE)
+    return jnp.where(position + distance < LINE, 1.0, 0.0)
+
+
+def jump_kernel(height, info, fine_end, coarse_start, out, edge_i, edge_x):
+    out[...] = fine_end[...] - jnp.where(info[2] == LINE - 1, 0.0, 1.0) * coarse_start[...]
+    write_edges(info[1], out, 0, height, edge_i, edge_x)
+
+
+def combine_kernel(height, distance, moved, info, arrived, product, out, edge_i, edge_x):
+    out[...] = arrived[...] + reaches(info, distance, moved) * product[...]
     write_edges(info[1], out, 0, height, edge_i, edge_x)
 
 
@@ -212,29 +220,24 @@
                 out[pl.ds(first + row, NX // LINE, stride=ROWS), :] = value[m * 4 : m * 4 + 4]
 
 
-def final_kernel(left, right, out):
+def final_kernel(distance, moved, info, arrived, product, out):
+    factor = reaches(info, distance, moved)
     for row in range(ROWS):
-        out[pl.ds(row, NX, stride=ROWS), :] = left[row] + right[row]
-
-
-def lay_out_kernel(blocks, out, sems):
-    copies = []
+        out[pl.ds(row, NX, stride=ROWS), :] = arrived[row] + factor * product[row]
+
+
+def lay_out_kernel(blocks, out):
     for m in range(LINE):
-        target = out.at[0, :, pl.ds(BLOCK_OF[m] * ROWS, ROWS), :]
-        copies.append(pltpu.make_async_copy(blocks.at[m], target, sems.at[m]))
-    for copy in copies:
-        copy.start()
-    for copy in copies:
-        copy.wait()
-
-
-def move(kernel, out, count, from_hbm, to_hbm, *args):
-    source = pltpu.HBM if from_hbm else pltpu.VMEM
+        for x in range(NX // LINE):
+            out[0, x, pl.ds(BLOCK_OF[m] * ROWS, ROWS), :] = blocks[m, x]
+
+
+def gathered_copies(kernel, out, count, *args):
     return pl.pallas_call(
         kernel,
         out_shape=out,
-        in_specs=[pl.BlockSpec(memory_space=source)] * len(args),
-        out_specs=pl.BlockSpec(memory_space=pltpu.HBM if to_hbm else pltpu.VMEM),
+        in_specs=[pl.BlockSpec(memory_space=pltpu.HBM)] * len(args),
+        out_specs=pl.BlockSpec(memory_space=pltpu.VMEM),
         scratch_shapes=[pltpu.SemaphoreType.DMA((count,))],
         compiler_params=pltpu.CompilerParams(vmem_limit_bytes=60 << 20),
     )(*args)
@@ -272,9 +275,8 @@
     return halo_i, halo_x
 
 
-def later(value, distance, shift=0):
-    route = [((p - 1) % LINE, (p + distance - 1 + shift) % LINE) for p in range(LINE) if p + distance < LINE]
-    return lax.ppermute(value, "tm", route)
+def earlier(value, distance):
+    return lax.ppermute(value, "tm", [(n, (n - distance) % LINE) for n in range(LINE)])
 
 
 def dft_table(sample_times, total, harmonics):
@@ -312,8 +314,8 @@
     block = jnp.asarray(BLOCK_OF, jnp.int32)[lax.axis_index("mesh")]
     info = jnp.concatenate([jnp.stack([block, block % 2, lax.axis_index("tm")]), switching]).astype(jnp.int32)
 
-    fields = move(
-        pack_kernel, shape(LINE, 4, 3, ROWS, CZ), 3 * LINE, True, False, conductivity, coil_current, slice_start[0]
+    fields = gathered_copies(
+        pack_kernel, shape(LINE, 4, 3, ROWS, CZ), 3 * LINE, conductivity, coil_current, slice_start[0]
     )
     packed = lax.all_to_all(fields, "mesh", 0, 0, tiled=True)
 
@@ -371,24 +373,35 @@
             halo_x,
         )
         states.append(state)
-    value, other = state, coarse_start
-    for power in (1, 2, 4):
-        value, edge_i, edge_x = call(
-            functools.partial(combine_kernel, 2 * power, power == 1),
-            [tile(), tile(2 * power), tile(2 * power)],
-            [],
-            0,
-            info,
-            value,
-            other,
-        )
+    value, edge_i, edge_x = call(functools.partial(jump_kernel, ROWS), [tile()] * 3, [], 0, info, state, coarse_start)
+    moved = 0
+    for level, distance in enumerate(DISTANCES):
         halo_i, halo_x = swap_halos(edge_i, edge_x)
-        (moved,) = coarse(power, 2 * power, 0, value, halo_i, halo_x)
-        other = later(moved, power)
-    value, edge_i, edge_x = call(
-        functools.partial(combine_kernel, ROWS, False), [tile()] * 3, [], 0, info, value, other
-    )
-    value, edge_i, edge_x, late = lax.optimization_barrier((value, edge_i, edge_x, states[-1]))
+        arrived = earlier(value, distance)
+        height = min(2 * distance, ROWS)
+        product, power = value, distance
+        if distance == 8:
+            product, edge_i, edge_x = coarse(4, ROWS, 0, value, halo_i, halo_x, edges=2)
+            halo_i, halo_x = swap_halos(edge_i, edge_x)
+            power = 4
+        (product,) = coarse(power, height, 0, product, halo_i, halo_x)
+        if level + 1 < len(DISTANCES):
+            next_height = min(2 * DISTANCES[level + 1], ROWS)
+            value, edge_i, edge_x = call(
+                functools.partial(combine_kernel, next_height, distance, moved),
+                [tile(), tile(next_height), tile(next_height)],
+                [],
+                0,
+                info,
+                arrived,
+                product,
+            )
+            if DISTANCES[level + 1] == 4:
+                value, edge_i, edge_x, late, early = lax.optimization_barrier(
+                    (value, edge_i, edge_x, states[-1], early)
+                )
+        moved += distance
+
     final = by_cell([late])
     table = dft_table(jnp.arange(total, dtype=jnp.int32), total, total // 2).reshape(total, LINE, STEPS)
     first_steps = table[:, :, : STEPS - 1].reshape(total, -1)
@@ -397,19 +410,21 @@
     spectrum += jnp.einsum("kt,txyz->kxyz", last_step, z_difference(final), precision=lax.Precision.HIGHEST)
     sums = loss_sums(spectrum, total)
 
-    left = later(value, 0, shift=1)
-    halo_i, halo_x = swap_halos(edge_i, edge_x)
-    moved, edge_i, edge_x = coarse(4, ROWS, 0, value, halo_i, halo_x, edges=2)
-    halo_i, halo_x = swap_halos(edge_i, edge_x)
-    (moved,) = coarse(4, ROWS, 0, moved, halo_i, halo_x)
-    right = later(moved, 8, shift=1)
-    right, sums = lax.optimization_barrier((right, sums))
-    (out,) = call(final_kernel, [shape(NX * ROWS, CZ)], [], 0, left, right)
+    arrived, sums = lax.optimization_barrier((arrived, sums))
+    (out,) = call(
+        functools.partial(final_kernel, DISTANCES[-1], moved - DISTANCES[-1]),
+        [shape(NX * ROWS, CZ)],
+        [],
+        0,
+        info,
+        arrived,
+        product,
+    )
     out = lax.all_to_all(out.reshape(LINE, 4, ROWS, CZ), "mesh", 0, 0, tiled=True)
     route = [(m * LINE + t, t * LINE + BLOCK_OF[m]) for m in range(LINE) for t in range(LINE)]
     sums = lax.ppermute(sums, ("mesh", "tm"), route)
     loss_density = jnp.sum(loss_coeffs * sums, axis=0)
-    next_start = move(lay_out_kernel, shape(1, 4, LINE * ROWS, CZ), LINE, False, True, out)
+    (next_start,) = call(lay_out_kernel, [shape(1, 4, LINE * ROWS, CZ)], [], 0, out)
     return next_start, loss_density
 
 

time: 230 us -> 180 us (0.78)
  the two profiles are of different devices: /device:TPU:168 before, /device:TPU:20 now
where the time goes in v3:
time: 180 us; the launch traced here: 179 us
  starting transfers between devices  94.6 us (53%)
  waiting for transfers between devices  41.3 us (23%)
  Pallas kernels  31.5 us (18%)
  local copies, waits for them, and re-layouts  3.67 us (2%)
  between operations  3.05 us (2%)
  other arithmetic  2.66 us (1%)
  matrix products  2.12 us (1%)
    ppermute x9, starting transfers between devices, swap_halos(): halo_x = lax.ppermute(edge_x, 'mesh', outer)  43.9 us
    pallas_call x19, Pallas kernels, call(): pl.pallas_call(kernel, out_shape=outs, in_specs=[pl.BlockSpec(memory_spac...  29.1 us
    ppermute x9, waiting for transfers between devices, swap_halos(): halo_x = lax.ppermute(edge_x, 'mesh', outer)  22.3 us
    ppermute x4, starting transfers between devices, earlier(): lax.ppermute(value, 'tm', [(n, (n - distance) % LINE) for n in range(LINE)])  15.7 us
    all_to_all x2, starting transfers between devices, by_cell(): lax.all_to_all(packed.reshape(LINE, count, 4, ROWS, CZ), 'tm', 0, 0, tile...  15.1 us
    ppermute x1, waiting for transfers between devices, iteration(): sums = lax.ppermute(sums, ('mesh', 'tm'), route)  11.3 us
    all_to_all x1, starting transfers between devices, iteration(): lax.all_to_all(out.reshape(LINE, 4, ROWS, CZ), 'mesh', 0, 0, tiled=True)  9.04 us
    all_to_all x1, starting transfers between devices, iteration(): packed = lax.all_to_all(fields, 'mesh', 0, 0, tiled=True)  7.24 us
  transfers between devices with their start and end apart: 27, of which 10 were waited for; matrix products, arithmetic and copies ran while one was open for 4% of the time, Pallas kernels for 10%

profile of v3, /device:TPU:20, one launch (start us, length us, event | category | flops | bytes accessed | tf_op | source)
XLA Modules:
  0.0 178.9 jit_solution(14555983883761040796)
XLA Ops:
  0.6 2.4 %shard_map.77 = f32[16,4,3,8,128]{4,3,2,1,0:T(8,128)} custom-call(f32[4,128,128]{2,1,0:T(8,128)} %cond.1, f32[4,128,128]{2,1,0:T(8,128)} %coil.1, f32[4,128,128]{2,1,0:T(8,128)} %bitcast.31), custom_call_target="tpu_custom_call" | custom-call | tf_op jit(solution)/shard_map/pallas_call | solution.py:236
  3.1 7.2 %all-to-all-start = ((f32[16,4,3,8,128]{4,3,2,1,0:T(8,128)}), f32[16,4,3,8,128]{4,3,2,1,0:T(8,128)S(1)}, u32[]{:S(2)}, u32[]{:S(2)}) async-start(f32[16,4,3,8,128]{4,3,2,1,0:T(8,128)} %shard_map.77), calls=%async_computation | async-start | bytes 1572864 | tf_op jit(solution)/shard_map/all_to_all | solution.py:320
  14.9 6.1 %all-to-all-done = f32[16,4,3,8,128]{4,3,2,1,0:T(8,128)S(1)} async-done(((f32[16,4,3,8,128]{4,3,2,1,0:T(8,128)}), f32[16,4,3,8,128]{4,3,2,1,0:T(8,128)S(1)}, u32[]{:S(2)}, u32[]{:S(2)}) %all-to-all-start) | async-done | bytes 786464 | tf_op jit(solution)/shard_map/all_to_all | solution.py:320
  22.0 3.0 %collective-permute-start.1 = (f32[18,64,128]{2,1,0:T(8,128)S(1)}, f32[18,64,128]{2,1,0:T(8,128)S(1)}, u32[]{:S(2)}, u32[]{:S(2)}) collective-permute-start(f32[18,64,128]{2,1,0:T(8,128)S(1)} %get-tuple-element.45), channel_id=1, source_target_pairs={{16,32},{32,16},{48,64},{64,48},{80,96},{96,80},{112,224},{224,112... | collective-permute-start | bytes 1769480 | tf_op jit(solution)/shard_map/ppermute | solution.py:273
  24.9 8.2 %collective-permute-done.1.halo_x = f32[18,64,128]{2,1,0:T(8,128)S(1)} collective-permute-done((f32[18,64,128]{2,1,0:T(8,128)S(1)}, f32[18,64,128]{2,1,0:T(8,128)S(1)}, u32[]{:S(2)}, u32[]{:S(2)}) %collective-permute-start.1) | collective-permute-done | bytes 589856 | tf_op jit(solution)/shard_map/ppermute | solution.py:273
  33.1 2.1 %shard_map.79 = (f32[8,64,128]{2,1,0:T(8,128)S(1)}, f32[5,64,128]{2,1,0:T(8,128)S(1)}, f32[5,64,128]{2,1,0:T(8,128)S(1)}, f32[24,64,128]{2,1,0:T(8,128)S(1)}, f32[18,64,128]{2,1,0:T(8,128)S(1)}) custom-call(s32[7]{0:T(128)S(1)} %pad_add_fusion.info, f32[8,64,128]{2,1,0:T(8,128)S(1)} %get-tuple-element.41.cond, f32[8,64,128]{2,1,0:T(8,128)S(1)} %get-tuple-element.42.coil, ...), custom_call_target="tpu_custom_call" | custom-call | flops 14745600 | bytes 3932188 | tf_op jit(solution)/shard_map/pallas_call | solution.py:257
  35.8 4.4 %collective-permute-start.3 = (f32[5,64,128]{2,1,0:T(8,128)S(1)}, f32[5,64,128]{2,1,0:T(8,128)S(1)}, u32[]{:S(2)}, u32[]{:S(2)}) collective-permute-start(f32[5,64,128]{2,1,0:T(8,128)S(1)} %get-tuple-element.50), channel_id=1, source_target_pairs={{16,32},{32,16},{48,64},{64,48},{80,96},{96,80},{112,224},{224,112... | collective-permute-start | bytes 491528 | tf_op jit(solution)/shard_map/ppermute | solution.py:273
  40.2 3.0 %collective-permute-done.3.halo_x = f32[5,64,128]{2,1,0:T(8,128)S(1)} collective-permute-done((f32[5,64,128]{2,1,0:T(8,128)S(1)}, f32[5,64,128]{2,1,0:T(8,128)S(1)}, u32[]{:S(2)}, u32[]{:S(2)}) %collective-permute-start.3) | collective-permute-done | bytes 163872 | tf_op jit(solution)/shard_map/ppermute | solution.py:273
  43.2 2.1 %shard_map.80 = (f32[8,64,128]{2,1,0:T(8,128)S(1)}, f32[5,64,128]{2,1,0:T(8,128)S(1)}, f32[5,64,128]{2,1,0:T(8,128)S(1)}) custom-call(s32[7]{0:T(128)S(1)} %pad_add_fusion.info, f32[24,64,128]{2,1,0:T(8,128)S(1)} %get-tuple-element.46.cond, f32[18,64,128]{2,1,0:T(8,128)S(1)} %get-tuple-element.47.coil, f32[8,64,128]{2,1,0:T(8,128)S(1)} %get-tuple-element.48.own.refs_0_, ...), custom_call_target="tpu_custom_call" | custom-call | flops 14745600 | bytes 2555932 | tf_op jit(solution)/shard_map/pallas_call | solution.py:257
  45.4 5.1 %collective-permute-start.5 = (f32[5,64,128]{2,1,0:T(8,128)S(1)}, f32[5,64,128]{2,1,0:T(8,128)S(1)}, u32[]{:S(2)}, u32[]{:S(2)}) collective-permute-start(f32[5,64,128]{2,1,0:T(8,128)S(1)} %get-tuple-element.53), channel_id=1, source_target_pairs={{16,32},{32,16},{48,64},{64,48},{80,96},{96,80},{112,224},{224,112... | collective-permute-start | bytes 491528 | tf_op jit(solution)/shard_map/ppermute | solution.py:273
  50.5 3.0 %collective-permute-done.5.halo_x = f32[5,64,128]{2,1,0:T(8,128)S(1)} collective-permute-done((f32[5,64,128]{2,1,0:T(8,128)S(1)}, f32[5,64,128]{2,1,0:T(8,128)S(1)}, u32[]{:S(2)}, u32[]{:S(2)}) %collective-permute-start.5) | collective-permute-done | bytes 163872 | tf_op jit(solution)/shard_map/ppermute | solution.py:273
  53.5 2.1 %shard_map.81 = (f32[8,64,128]{2,1,0:T(8,128)S(1)}, f32[5,64,128]{2,1,0:T(8,128)S(1)}, f32[5,64,128]{2,1,0:T(8,128)S(1)}) custom-call(s32[7]{0:T(128)S(1)} %pad_add_fusion.info, f32[24,64,128]{2,1,0:T(8,128)S(1)} %get-tuple-element.46.cond, f32[18,64,128]{2,1,0:T(8,128)S(1)} %get-tuple-element.47.coil, f32[8,64,128]{2,1,0:T(8,128)S(1)} %get-tuple-element.51.own.refs_1_, ...), custom_call_target="tpu_custom_call" | custom-call | flops 14745600 | bytes 2555932 | tf_op jit(solution)/shard_map/pallas_call | solution.py:257
  56.7 9.2 %all-to-all-start.1 = ((f32[16,3,4,8,128]{4,3,2,1,0:T(8,128)}), f32[16,3,4,8,128]{4,3,2,1,0:T(8,128)}, u32[]{:S(2)}, u32[]{:S(2)}) async-start(f32[16,3,4,8,128]{4,3,2,1,0:T(8,128)} %bitcast.5), calls=%async_computation.1 | async-start | bytes 1572864 | tf_op jit(solution)/shard_map/all_to_all | solution.py:308
  66.0 5.1 %collective-permute-start.7 = (f32[5,64,128]{2,1,0:T(8,128)S(1)}, f32[5,64,128]{2,1,0:T(8,128)S(1)}, u32[]{:S(2)}, u32[]{:S(2)}) collective-permute-start(f32[5,64,128]{2,1,0:T(8,128)S(1)} %get-tuple-element.56), channel_id=1, source_target_pairs={{16,32},{32,16},{48,64},{64,48},{80,96},{96,80},{112,224},{224,112... | collective-permute-start | bytes 491528 | tf_op jit(solution)/shard_map/ppermute | solution.py:273
  74.2 2.8 %shard_map.82 = (f32[8,64,128]{2,1,0:T(8,128)S(1)}, f32[5,64,128]{2,1,0:T(8,128)}, f32[5,64,128]{2,1,0:T(8,128)}) custom-call(s32[7]{0:T(128)S(1)} %pad_add_fusion.info, f32[24,64,128]{2,1,0:T(8,128)S(1)} %get-tuple-element.46.cond, f32[18,64,128]{2,1,0:T(8,128)S(1)} %get-tuple-element.47.coil, f32[8,64,128]{2,1,0:T(8,128)S(1)} %get-tuple-element.54.own.refs_2_, ...), custom_call_target="tpu_custom_call" | custom-call | flops 14745600 | bytes 2555932 | tf_op jit(solution)/shard_map/pallas_call | solution.py:257
  77.7 5.1 %collective-permute-start.10 = (f32[8,64,128]{2,1,0:T(8,128)S(1)}, f32[8,64,128]{2,1,0:T(8,128)S(1)}, u32[]{:S(2)}, u32[]{:S(2)}) collective-permute-start(f32[8,64,128]{2,1,0:T(8,128)S(1)} %get-tuple-element.60), channel_id=1, source_target_pairs={{16,32},{32,16},{48,64},{64,48},{80,96},{96,80},{112,224},{224,112... | collective-permute-start | bytes 786440 | tf_op jit(solution)/shard_map/ppermute | solution.py:273
  82.9 6.0 %collective-permute-start.8 = (f32[8,64,128]{2,1,0:T(8,128)S(1)}, f32[8,64,128]{2,1,0:T(8,128)S(1)}, u32[]{:S(2)}, u32[]{:S(2)}) collective-permute-start(f32[8,64,128]{2,1,0:T(8,128)S(1)} %get-tuple-element.58.own), channel_id=1, source_target_pairs={{0,8},{1,9},{2,10},{3,11},{4,12},{5,13},{6,14},{7,15},{8,0},{9,1},... | collective-permute-start | bytes 786440 | tf_op jit(solution)/shard_map/ppermute | solution.py:279
  88.8 3.1 %shard_map.85 = (f32[8,64,128]{2,1,0:T(8,128)S(1)}, f32[8,64,128]{2,1,0:T(8,128)S(1)}, f32[8,64,128]{2,1,0:T(8,128)S(1)}) custom-call(s32[7]{0:T(128)S(1)} %pad_add_fusion.info, f32[24,64,128]{2,1,0:T(8,128)S(1)} %get-tuple-element.46.cond, f32[8,64,128]{2,1,0:T(8,128)S(1)} %get-tuple-element.58.own, f32[8,64,128]{2,1,0:T(8,128)S(1)} %collective-permute-done.9.halo_i, ...), custom_call_target="tpu_custom_call" | custom-call | flops 31457280 | bytes 2359324 | tf_op jit(solution)/shard_map/pallas_call | solution.py:257
  92.1 6.5 %collective-permute-start.12 = (f32[8,64,128]{2,1,0:T(8,128)S(1)}, f32[8,64,128]{2,1,0:T(8,128)S(1)}, u32[]{:S(2)}, u32[]{:S(2)}) collective-permute-start(f32[8,64,128]{2,1,0:T(8,128)S(1)} %get-tuple-element.63), channel_id=1, source_target_pairs={{16,32},{32,16},{48,64},{64,48},{80,96},{96,80},{112,224},{224,112... | collective-permute-start | bytes 786440 | tf_op jit(solution)/shard_map/ppermute | solution.py:273
  98.8 3.8 %collective-permute-done.12.halo_x = f32[8,64,128]{2,1,0:T(8,128)S(1)} collective-permute-done((f32[8,64,128]{2,1,0:T(8,128)S(1)}, f32[8,64,128]{2,1,0:T(8,128)S(1)}, u32[]{:S(2)}, u32[]{:S(2)}) %collective-permute-start.12) | collective-permute-done | bytes 262176 | tf_op jit(solution)/shard_map/ppermute | solution.py:273
  102.6 3.1 %shard_map.86.product = f32[8,64,128]{2,1,0:T(8,128)S(1)} custom-call(s32[7]{0:T(128)S(1)} %pad_add_fusion.info, f32[24,64,128]{2,1,0:T(8,128)S(1)} %get-tuple-element.46.cond, f32[8,64,128]{2,1,0:T(8,128)S(1)} %get-tuple-element.61.own, f32[8,64,128]{2,1,0:T(8,128)S(1)} %collective-permute-done.11.halo_i, f32[8,64,128]{2,1,0:T(8,128)S(1)} %collective-permute-done.12.halo_x), custom_call_target="tpu_custom_call" | custom-call | flops 31457280 | bytes 1835036 | tf_op jit(solution)/shard_map/pallas_call | solution.py:257
  106.5 5.1 %collective-permute-start.15 = (f32[8,64,128]{2,1,0:T(8,128)S(1)}, f32[8,64,128]{2,1,0:T(8,128)S(1)}, u32[]{:S(2)}, u32[]{:S(2)}) collective-permute-start(f32[8,64,128]{2,1,0:T(8,128)S(1)} %get-tuple-element.69), channel_id=1, source_target_pairs={{16,32},{32,16},{48,64},{64,48},{80,96},{96,80},{112,224},{224,112... | collective-permute-start | bytes 786440 | tf_op jit(solution)/shard_map/ppermute | solution.py:273
  111.6 2.9 %collective-permute-start.13 = (f32[8,64,128]{2,1,0:T(8,128)S(1)}, f32[8,64,128]{2,1,0:T(8,128)S(1)}, u32[]{:S(2)}, u32[]{:S(2)}) collective-permute-start(f32[8,64,128]{2,1,0:T(8,128)S(1)} %get-tuple-element.67.own), channel_id=1, source_target_pairs={{0,12},{1,13},{2,14},{3,15},{4,0},{5,1},{6,2},{7,3},{8,4},{9,5},{1... | collective-permute-start | bytes 786440 | tf_op jit(solution)/shard_map/ppermute | solution.py:279
  115.3 5.9 %all-to-all-start.2 = ((f32[16,1,4,8,128]{4,3,2,1,0:T(8,128)}), f32[16,1,4,8,128]{4,3,2,1,0:T(8,128)S(1)}, u32[]{:S(2)}, u32[]{:S(2)}) async-start(f32[16,1,4,8,128]{4,3,2,1,0:T(8,128)} %bitcast.12), calls=%async_computation.2 | async-start | bytes 524288 | tf_op jit(solution)/shard_map/all_to_all | solution.py:308
  122.9 3.1 %shard_map.89.product = f32[8,64,128]{2,1,0:T(8,128)S(1)} custom-call(s32[7]{0:T(128)S(1)} %pad_add_fusion.info, f32[24,64,128]{2,1,0:T(8,128)S(1)} %get-tuple-element.46.cond, f32[8,64,128]{2,1,0:T(8,128)S(1)} %get-tuple-element.67.own, f32[8,64,128]{2,1,0:T(8,128)S(1)} %collective-permute-done.14.halo_i, f32[8,64,128]{2,1,0:T(8,128)S(1)} %collective-permute-done.15.halo_x), custom_call_target="tpu_custom_call" | custom-call | flops 31457280 | bytes 1835036 | tf_op jit(solution)/shard_map/pallas_call | solution.py:257
  126.8 3.4 %collective-permute-start.18 = (f32[4,64,128]{2,1,0:T(8,128)S(1)}, f32[4,64,128]{2,1,0:T(8,128)S(1)}, u32[]{:S(2)}, u32[]{:S(2)}) collective-permute-start(f32[4,64,128]{2,1,0:T(8,128)S(1)} %get-tuple-element.72), channel_id=1, source_target_pairs={{16,32},{32,16},{48,64},{64,48},{80,96},{96,80},{112,224},{224,112... | collective-permute-start | bytes 393224 | tf_op jit(solution)/shard_map/ppermute | solution.py:273
  130.5 2.2 %collective-permute-start.16 = (f32[8,64,128]{2,1,0:T(8,128)S(1)}, f32[8,64,128]{2,1,0:T(8,128)S(1)}, u32[]{:S(2)}, u32[]{:S(2)}) collective-permute-start(f32[8,64,128]{2,1,0:T(8,128)S(1)} %get-tuple-element.70.own), channel_id=1, source_target_pairs={{0,14},{1,15},{2,0},{3,1},{4,2},{5,3},{6,4},{7,5},{8,6},{9,7},{10,... | collective-permute-start | bytes 786440 | tf_op jit(solution)/shard_map/ppermute | solution.py:279
  139.2 4.7 %collective-permute-start.19 = (f32[8,64,128]{2,1,0:T(8,128)S(1)}, f32[8,64,128]{2,1,0:T(8,128)S(1)}, u32[]{:S(2)}, u32[]{:S(2)}) collective-permute-start(f32[8,64,128]{2,1,0:T(8,128)S(1)} %get-tuple-element.73.own), channel_id=1, source_target_pairs={{0,15},{1,0},{2,1},{3,2},{4,3},{5,4},{6,5},{7,6},{8,7},{9,8},{10,9... | collective-permute-start | bytes 786440 | tf_op jit(solution)/shard_map/ppermute | solution.py:279
  144.6 6.0 %collective-permute-start.21 = (f32[2,64,128]{2,1,0:T(8,128)S(1)}, f32[2,64,128]{2,1,0:T(8,128)S(1)}, u32[]{:S(2)}, u32[]{:S(2)}) collective-permute-start(f32[2,64,128]{2,1,0:T(8,128)S(1)} %get-tuple-element.78), channel_id=1, source_target_pairs={{16,32},{32,16},{48,64},{64,48},{80,96},{96,80},{112,224},{224,112... | collective-permute-start | bytes 196616 | tf_op jit(solution)/shard_map/ppermute | solution.py:273
  154.9 9.0 %all-to-all-start.3 = ((f32[16,4,8,128]{3,2,1,0:T(8,128)}), f32[16,4,8,128]{3,2,1,0:T(8,128)S(1)}, u32[]{:S(2)}, u32[]{:S(2)}) async-start(f32[16,4,8,128]{3,2,1,0:T(8,128)} %bitcast.17), calls=%async_computation.3 | async-start | bytes 524288 | tf_op jit(solution)/shard_map/all_to_all | solution.py:423
  163.9 2.3 %collective-permute-start.22 = (f32[3,4,8,128]{3,2,1,0:T(8,128)S(1)}, f32[3,4,8,128]{3,2,1,0:T(8,128)S(1)}, u32[]{:S(2)}, u32[]{:S(2)}) collective-permute-start(f32[3,4,8,128]{3,2,1,0:T(8,128)S(1)} %pad_maximum_fusion), channel_id=1, source_target_pairs={{0,0},{1,16},{2,32},{3,48},{4,64},{5,80},{6,96},{7,112},{8,128},{9... | collective-permute-start | bytes 147464 | tf_op jit(solution)/shard_map/ppermute | solution.py:425
  166.3 11.3 %collective-permute-done.22 = f32[3,4,8,128]{3,2,1,0:T(8,128)S(1)} collective-permute-done((f32[3,4,8,128]{3,2,1,0:T(8,128)S(1)}, f32[3,4,8,128]{3,2,1,0:T(8,128)S(1)}, u32[]{:S(2)}, u32[]{:S(2)}) %collective-permute-start.22) | collective-permute-done | bytes 49184 | tf_op jit(solution)/shard_map/ppermute | solution.py:425
  (67 shorter events, 26.3 us)
Async XLA Ops:
  3.1 17.9 %all-to-all-start = ((f32[16,4,3,8,128]{4,3,2,1,0:T(8,128)}), f32[16,4,3,8,128]{4,3,2,1,0:T(8,128)S(1)}, u32[]{:S(2)}, u32[]{:S(2)}) async-start(f32[16,4,3,8,128]{4,3,2,1,0:T(8,128)} %shard_map.77), calls=%async_computation | async-start | bytes 1572864 | tf_op jit(solution)/shard_map/all_to_all | solution.py:320
  10.3 0.7 copy-start.2
  13.5 0.7 copy-start.1
  21.8 3.2 %collective-permute-start = (f32[18,64,128]{2,1,0:T(8,128)S(1)}, f32[18,64,128]{2,1,0:T(8,128)S(1)}, u32[]{:S(2)}, u32[]{:S(2)}) collective-permute-start(f32[18,64,128]{2,1,0:T(8,128)S(1)} %get-tuple-element.44), channel_id=1, source_target_pairs={{0,16},{16,0},{32,48},{48,32},{64,80},{80,64},{96,112},{112,96},{1... | collective-permute-start | bytes 1769480 | tf_op jit(solution)/shard_map/ppermute | solution.py:274
  22.0 11.2 %collective-permute-start.1 = (f32[18,64,128]{2,1,0:T(8,128)S(1)}, f32[18,64,128]{2,1,0:T(8,128)S(1)}, u32[]{:S(2)}, u32[]{:S(2)}) collective-permute-start(f32[18,64,128]{2,1,0:T(8,128)S(1)} %get-tuple-element.45), channel_id=1, source_target_pairs={{16,32},{32,16},{48,64},{64,48},{80,96},{96,80},{112,224},{224,112... | collective-permute-start | bytes 1769480 | tf_op jit(solution)/shard_map/ppermute | solution.py:273
  35.3 4.9 %collective-permute-start.2 = (f32[5,64,128]{2,1,0:T(8,128)S(1)}, f32[5,64,128]{2,1,0:T(8,128)S(1)}, u32[]{:S(2)}, u32[]{:S(2)}) collective-permute-start(f32[5,64,128]{2,1,0:T(8,128)S(1)} %get-tuple-element.49), channel_id=1, source_target_pairs={{0,16},{16,0},{32,48},{48,32},{64,80},{80,64},{96,112},{112,96},{1... | collective-permute-start | bytes 491528 | tf_op jit(solution)/shard_map/ppermute | solution.py:274
  35.8 7.4 %collective-permute-start.3 = (f32[5,64,128]{2,1,0:T(8,128)S(1)}, f32[5,64,128]{2,1,0:T(8,128)S(1)}, u32[]{:S(2)}, u32[]{:S(2)}) collective-permute-start(f32[5,64,128]{2,1,0:T(8,128)S(1)} %get-tuple-element.50), channel_id=1, source_target_pairs={{16,32},{32,16},{48,64},{64,48},{80,96},{96,80},{112,224},{224,112... | collective-permute-start | bytes 491528 | tf_op jit(solution)/shard_map/ppermute | solution.py:273
  45.3 5.3 %collective-permute-start.4 = (f32[5,64,128]{2,1,0:T(8,128)S(1)}, f32[5,64,128]{2,1,0:T(8,128)S(1)}, u32[]{:S(2)}, u32[]{:S(2)}) collective-permute-start(f32[5,64,128]{2,1,0:T(8,128)S(1)} %get-tuple-element.52), channel_id=1, source_target_pairs={{0,16},{16,0},{32,48},{48,32},{64,80},{80,64},{96,112},{112,96},{1... | collective-permute-start | bytes 491528 | tf_op jit(solution)/shard_map/ppermute | solution.py:274
  45.4 8.1 %collective-permute-start.5 = (f32[5,64,128]{2,1,0:T(8,128)S(1)}, f32[5,64,128]{2,1,0:T(8,128)S(1)}, u32[]{:S(2)}, u32[]{:S(2)}) collective-permute-start(f32[5,64,128]{2,1,0:T(8,128)S(1)} %get-tuple-element.53), channel_id=1, source_target_pairs={{16,32},{32,16},{48,64},{64,48},{80,96},{96,80},{112,224},{224,112... | collective-permute-start | bytes 491528 | tf_op jit(solution)/shard_map/ppermute | solution.py:273
  56.7 49.6 %all-to-all-start.1 = ((f32[16,3,4,8,128]{4,3,2,1,0:T(8,128)}), f32[16,3,4,8,128]{4,3,2,1,0:T(8,128)}, u32[]{:S(2)}, u32[]{:S(2)}) async-start(f32[16,3,4,8,128]{4,3,2,1,0:T(8,128)} %bitcast.5), calls=%async_computation.1 | async-start | bytes 1572864 | tf_op jit(solution)/shard_map/all_to_all | solution.py:308
  65.9 6.3 %collective-permute-start.6 = (f32[5,64,128]{2,1,0:T(8,128)S(1)}, f32[5,64,128]{2,1,0:T(8,128)S(1)}, u32[]{:S(2)}, u32[]{:S(2)}) collective-permute-start(f32[5,64,128]{2,1,0:T(8,128)S(1)} %get-tuple-element.55), channel_id=1, source_target_pairs={{0,16},{16,0},{32,48},{48,32},{64,80},{80,64},{96,112},{112,96},{1... | collective-permute-start | bytes 491528 | tf_op jit(solution)/shard_map/ppermute | solution.py:274
  66.0 8.1 %collective-permute-start.7 = (f32[5,64,128]{2,1,0:T(8,128)S(1)}, f32[5,64,128]{2,1,0:T(8,128)S(1)}, u32[]{:S(2)}, u32[]{:S(2)}) collective-permute-start(f32[5,64,128]{2,1,0:T(8,128)S(1)} %get-tuple-element.56), channel_id=1, source_target_pairs={{16,32},{32,16},{48,64},{64,48},{80,96},{96,80},{112,224},{224,112... | collective-permute-start | bytes 491528 | tf_op jit(solution)/shard_map/ppermute | solution.py:273
  77.6 11.2 %collective-permute-start.9 = (f32[8,64,128]{2,1,0:T(8,128)S(1)}, f32[8,64,128]{2,1,0:T(8,128)S(1)}, u32[]{:S(2)}, u32[]{:S(2)}) collective-permute-start(f32[8,64,128]{2,1,0:T(8,128)S(1)} %get-tuple-element.59), channel_id=1, source_target_pairs={{0,16},{16,0},{32,48},{48,32},{64,80},{80,64},{96,112},{112,96},{1... | collective-permute-start | bytes 786440 | tf_op jit(solution)/shard_map/ppermute | solution.py:274
  77.7 11.1 %collective-permute-start.10 = (f32[8,64,128]{2,1,0:T(8,128)S(1)}, f32[8,64,128]{2,1,0:T(8,128)S(1)}, u32[]{:S(2)}, u32[]{:S(2)}) collective-permute-start(f32[8,64,128]{2,1,0:T(8,128)S(1)} %get-tuple-element.60), channel_id=1, source_target_pairs={{16,32},{32,16},{48,64},{64,48},{80,96},{96,80},{112,224},{224,112... | collective-permute-start | bytes 786440 | tf_op jit(solution)/shard_map/ppermute | solution.py:273
  82.9 22.9 %collective-permute-start.8 = (f32[8,64,128]{2,1,0:T(8,128)S(1)}, f32[8,64,128]{2,1,0:T(8,128)S(1)}, u32[]{:S(2)}, u32[]{:S(2)}) collective-permute-start(f32[8,64,128]{2,1,0:T(8,128)S(1)} %get-tuple-element.58.own), channel_id=1, source_target_pairs={{0,8},{1,9},{2,10},{3,11},{4,12},{5,13},{6,14},{7,15},{8,0},{9,1},... | collective-permute-start | bytes 786440 | tf_op jit(solution)/shard_map/ppermute | solution.py:279
  92.0 6.8 %collective-permute-start.11 = (f32[8,64,128]{2,1,0:T(8,128)S(1)}, f32[8,64,128]{2,1,0:T(8,128)S(1)}, u32[]{:S(2)}, u32[]{:S(2)}) collective-permute-start(f32[8,64,128]{2,1,0:T(8,128)S(1)} %get-tuple-element.62), channel_id=1, source_target_pairs={{0,16},{16,0},{32,48},{48,32},{64,80},{80,64},{96,112},{112,96},{1... | collective-permute-start | bytes 786440 | tf_op jit(solution)/shard_map/ppermute | solution.py:274
  92.1 10.5 %collective-permute-start.12 = (f32[8,64,128]{2,1,0:T(8,128)S(1)}, f32[8,64,128]{2,1,0:T(8,128)S(1)}, u32[]{:S(2)}, u32[]{:S(2)}) collective-permute-start(f32[8,64,128]{2,1,0:T(8,128)S(1)} %get-tuple-element.63), channel_id=1, source_target_pairs={{16,32},{32,16},{48,64},{64,48},{80,96},{96,80},{112,224},{224,112... | collective-permute-start | bytes 786440 | tf_op jit(solution)/shard_map/ppermute | solution.py:273
  106.3 16.6 %collective-permute-start.14 = (f32[8,64,128]{2,1,0:T(8,128)S(1)}, f32[8,64,128]{2,1,0:T(8,128)S(1)}, u32[]{:S(2)}, u32[]{:S(2)}) collective-permute-start(f32[8,64,128]{2,1,0:T(8,128)S(1)} %get-tuple-element.68), channel_id=1, source_target_pairs={{0,16},{16,0},{32,48},{48,32},{64,80},{80,64},{96,112},{112,96},{1... | collective-permute-start | bytes 786440 | tf_op jit(solution)/shard_map/ppermute | solution.py:274
  106.5 16.5 %collective-permute-start.15 = (f32[8,64,128]{2,1,0:T(8,128)S(1)}, f32[8,64,128]{2,1,0:T(8,128)S(1)}, u32[]{:S(2)}, u32[]{:S(2)}) collective-permute-start(f32[8,64,128]{2,1,0:T(8,128)S(1)} %get-tuple-element.69), channel_id=1, source_target_pairs={{16,32},{32,16},{48,64},{64,48},{80,96},{96,80},{112,224},{224,112... | collective-permute-start | bytes 786440 | tf_op jit(solution)/shard_map/ppermute | solution.py:273
  111.6 14.5 %collective-permute-start.13 = (f32[8,64,128]{2,1,0:T(8,128)S(1)}, f32[8,64,128]{2,1,0:T(8,128)S(1)}, u32[]{:S(2)}, u32[]{:S(2)}) collective-permute-start(f32[8,64,128]{2,1,0:T(8,128)S(1)} %get-tuple-element.67.own), channel_id=1, source_target_pairs={{0,12},{1,13},{2,14},{3,15},{4,0},{5,1},{6,2},{7,3},{8,4},{9,5},{1... | collective-permute-start | bytes 786440 | tf_op jit(solution)/shard_map/ppermute | solution.py:279
  115.3 19.2 %all-to-all-start.2 = ((f32[16,1,4,8,128]{4,3,2,1,0:T(8,128)}), f32[16,1,4,8,128]{4,3,2,1,0:T(8,128)S(1)}, u32[]{:S(2)}, u32[]{:S(2)}) async-start(f32[16,1,4,8,128]{4,3,2,1,0:T(8,128)} %bitcast.12), calls=%async_computation.2 | async-start | bytes 524288 | tf_op jit(solution)/shard_map/all_to_all | solution.py:308
  126.7 5.9 %collective-permute-start.17 = (f32[4,64,128]{2,1,0:T(8,128)S(1)}, f32[4,64,128]{2,1,0:T(8,128)S(1)}, u32[]{:S(2)}, u32[]{:S(2)}) collective-permute-start(f32[4,64,128]{2,1,0:T(8,128)S(1)} %get-tuple-element.71), channel_id=1, source_target_pairs={{0,16},{16,0},{32,48},{48,32},{64,80},{80,64},{96,112},{112,96},{1... | collective-permute-start | bytes 393224 | tf_op jit(solution)/shard_map/ppermute | solution.py:274
  126.8 6.3 %collective-permute-start.18 = (f32[4,64,128]{2,1,0:T(8,128)S(1)}, f32[4,64,128]{2,1,0:T(8,128)S(1)}, u32[]{:S(2)}, u32[]{:S(2)}) collective-permute-start(f32[4,64,128]{2,1,0:T(8,128)S(1)} %get-tuple-element.72), channel_id=1, source_target_pairs={{16,32},{32,16},{48,64},{64,48},{80,96},{96,80},{112,224},{224,112... | collective-permute-start | bytes 393224 | tf_op jit(solution)/shard_map/ppermute | solution.py:273
  130.5 8.2 %collective-permute-start.16 = (f32[8,64,128]{2,1,0:T(8,128)S(1)}, f32[8,64,128]{2,1,0:T(8,128)S(1)}, u32[]{:S(2)}, u32[]{:S(2)}) collective-permute-start(f32[8,64,128]{2,1,0:T(8,128)S(1)} %get-tuple-element.70.own), channel_id=1, source_target_pairs={{0,14},{1,15},{2,0},{3,1},{4,2},{5,3},{6,4},{7,5},{8,6},{9,7},{10,... | collective-permute-start | bytes 786440 | tf_op jit(solution)/shard_map/ppermute | solution.py:279
  139.2 14.4 %collective-permute-start.19 = (f32[8,64,128]{2,1,0:T(8,128)S(1)}, f32[8,64,128]{2,1,0:T(8,128)S(1)}, u32[]{:S(2)}, u32[]{:S(2)}) collective-permute-start(f32[8,64,128]{2,1,0:T(8,128)S(1)} %get-tuple-element.73.own), channel_id=1, source_target_pairs={{0,15},{1,0},{2,1},{3,2},{4,3},{5,4},{6,5},{7,6},{8,7},{9,8},{10,9... | collective-permute-start | bytes 786440 | tf_op jit(solution)/shard_map/ppermute | solution.py:279
  144.5 6.2 %collective-permute-start.20 = (f32[2,64,128]{2,1,0:T(8,128)S(1)}, f32[2,64,128]{2,1,0:T(8,128)S(1)}, u32[]{:S(2)}, u32[]{:S(2)}) collective-permute-start(f32[2,64,128]{2,1,0:T(8,128)S(1)} %get-tuple-element.77), channel_id=1, source_target_pairs={{0,16},{16,0},{32,48},{48,32},{64,80},{80,64},{96,112},{112,96},{1... | collective-permute-start | bytes 196616 | tf_op jit(solution)/shard_map/ppermute | solution.py:274
  144.6 8.0 %collective-permute-start.21 = (f32[2,64,128]{2,1,0:T(8,128)S(1)}, f32[2,64,128]{2,1,0:T(8,128)S(1)}, u32[]{:S(2)}, u32[]{:S(2)}) collective-permute-start(f32[2,64,128]{2,1,0:T(8,128)S(1)} %get-tuple-element.78), channel_id=1, source_target_pairs={{16,32},{32,16},{48,64},{64,48},{80,96},{96,80},{112,224},{224,112... | collective-permute-start | bytes 196616 | tf_op jit(solution)/shard_map/ppermute | solution.py:273
  154.9 22.7 %copy-start = (f32[3,4,8,128]{3,2,1,0:T(8,128)S(1)}, f32[3,4,8,128]{3,2,1,0:T(8,128)}, u32[]{:S(2)}) copy-start(f32[3,4,8,128]{3,2,1,0:T(8,128)} %param.10) | copy-start | bytes 147460
  154.9 23.3 %all-to-all-start.3 = ((f32[16,4,8,128]{3,2,1,0:T(8,128)}), f32[16,4,8,128]{3,2,1,0:T(8,128)S(1)}, u32[]{:S(2)}, u32[]{:S(2)}) async-start(f32[16,4,8,128]{3,2,1,0:T(8,128)} %bitcast.17), calls=%async_computation.3 | async-start | bytes 524288 | tf_op jit(solution)/shard_map/all_to_all | solution.py:423
  163.9 13.7 %collective-permute-start.22 = (f32[3,4,8,128]{3,2,1,0:T(8,128)S(1)}, f32[3,4,8,128]{3,2,1,0:T(8,128)S(1)}, u32[]{:S(2)}, u32[]{:S(2)}) collective-permute-start(f32[3,4,8,128]{3,2,1,0:T(8,128)S(1)} %pad_maximum_fusion), channel_id=1, source_target_pairs={{0,0},{1,16},{2,32},{3,48},{4,64},{5,80},{6,96},{7,112},{8,128},{9... | collective-permute-start | bytes 147464 | tf_op jit(solution)/shard_map/ppermute | solution.py:425

commit v4 on v3

--- a/solution.py
+++ b/solution.py
@@ -19,7 +19,7 @@
 CZ = 128
 FINE_HALO = 5
 S_HALO = 8
-DISTANCES = (8, 4, 2, 1)
+DISTANCES = (1, 2, 4, 8)
 
 CHIP = [c if c < 4 else 11 - c for c in range(8)]
 BLOCK_OF = [2 * CHIP[m // 2] + m % 2 for m in range(LINE)]
@@ -159,10 +159,20 @@
         state[row - height] = value
 
     solve(block, height, 0, total, lambda row: cond[row + shift], rhs, a, b, TAU, SWEEPS, store)
-    write_edges(parity, state, 0, height, edge_i, edge_x)
-
-
-def coarse_kernel(power, height, halo_at, info, cond, own, halo_i, halo_x, *rest):
+    if edge_i is not None:
+        write_edges(parity, state, 0, height, edge_i, edge_x)
+
+
+def last_kernel(info, cond, coil, own, halo_i, halo_x, coarse_start, state, value, edge_i, edge_x, a, b, rhs):
+    fine_kernel(0, STEPS - 1, info, cond, coil, own, halo_i, halo_x, state, None, None, a, b, rhs)
+    value[...] = state[...] - jnp.where(info[2] == LINE - 1, 0.0, 1.0) * coarse_start[...]
+    write_edges(info[1], value, 0, 2 * DISTANCES[0], edge_i, edge_x)
+
+
+def coarse_kernel(power, height, halo_at, edge_height, mix, info, cond, own, halo_i, halo_x, *rest):
+    if mix:
+        arrived, rest = rest[0], rest[1:]
+        factor = reaches(info, *mix)
     outs, (a, b, c) = rest[:-3], rest[-3:]
     block, parity = info[0], info[1]
     scale = 4.0 * TAU
@@ -186,13 +196,15 @@
         else:
 
             def store(row, value):
+                if mix:
+                    value = arrived[row - height] + factor * value
                 outs[0][row - height] = value
 
         solve(block, height, lo, hi, lambda row: cond[row + shift], rhs, b, None, scale, CSWEEPS, store)
         rhs, result = result, rhs
         lo, hi = lo + CSWEEPS, hi - CSWEEPS
     if len(outs) > 1:
-        write_edges(parity, outs[0], 0, ROWS, outs[1], outs[2])
+        write_edges(parity, outs[0], 0, edge_height, outs[1], outs[2])
 
 
 def reaches(info, distance, moved):
@@ -200,23 +212,18 @@
     return jnp.where(position + distance < LINE, 1.0, 0.0)
 
 
-def jump_kernel(height, info, fine_end, coarse_start, out, edge_i, edge_x):
-    out[...] = fine_end[...] - jnp.where(info[2] == LINE - 1, 0.0, 1.0) * coarse_start[...]
-    write_edges(info[1], out, 0, height, edge_i, edge_x)
-
-
 def combine_kernel(height, distance, moved, info, arrived, product, out, edge_i, edge_x):
     out[...] = arrived[...] + reaches(info, distance, moved) * product[...]
     write_edges(info[1], out, 0, height, edge_i, edge_x)
 
 
-def columns_kernel(*refs):
-    fields, out = refs[:-1], refs[-1]
+def columns_kernel(count, *refs):
+    fields, out = refs[:count], refs[-1]
     for row in range(ROWS):
         for place, field in enumerate(fields):
             value = field[row]
             for m in range(LINE):
-                first = (m * len(fields) + place) * (NX // LINE) * ROWS
+                first = (m * count + place) * (NX // LINE) * ROWS
                 out[pl.ds(first + row, NX // LINE, stride=ROWS), :] = value[m * 4 : m * 4 + 4]
 
 
@@ -302,9 +309,10 @@
     return jnp.stack([jnp.sum(term, axis=0) for term in terms], axis=0)
 
 
-def by_cell(states):
+def by_cell(states, after=None):
     count = len(states)
-    (packed,) = call(columns_kernel, [shape(LINE * count * 4 * ROWS, CZ)], [], 0, *states)
+    extra = () if after is None else (after,)
+    (packed,) = call(functools.partial(columns_kernel, count), [shape(LINE * count * 4 * ROWS, CZ)], [], 0, *states, *extra)
     packed = lax.all_to_all(packed.reshape(LINE, count, 4, ROWS, CZ), "tm", 0, 0, tiled=True)
     return packed.reshape(LINE * count, 4, ROWS, CZ)
 
@@ -340,11 +348,11 @@
         halo_x,
     )
 
-    def coarse(power, height, halo_at, value, halo_i, halo_x, edges=0):
+    def coarse(power, height, halo_at, value, halo_i, halo_x, edge_height=0, mix=(), others=()):
         rows = ROWS + 2 * height
         return call(
-            functools.partial(coarse_kernel, power, height, halo_at),
-            [tile()] + [tile()] * edges,
+            functools.partial(coarse_kernel, power, height, halo_at, edge_height, mix),
+            [tile()] + [tile(edge_height)] * (2 if edge_height else 0),
             [rows] * 3,
             20 * CSWEEPS * power * rows * NX * CZ,
             info,
@@ -352,17 +360,19 @@
             value,
             halo_i,
             halo_x,
+            *others,
         )
 
     (coarse_start,) = coarse(1, FINE_HALO, S_HALO + FINE_HALO, start, first_i, first_x)
     states = [state]
     for step in range(1, STEPS):
         halo_i, halo_x = swap_halos(edge_i, edge_x)
-        if step == STEPS - 1:
+        last = step == STEPS - 1
+        if last:
             early = by_cell(states)
-        state, edge_i, edge_x = call(
-            functools.partial(fine_kernel, 0, step),
-            [tile(), tile(FINE_HALO), tile(FINE_HALO)],
+        results = call(
+            last_kernel if last else functools.partial(fine_kernel, 0, step),
+            [tile(), tile()] + [tile(2 * DISTANCES[0])] * 2 if last else [tile(), tile(FINE_HALO), tile(FINE_HALO)],
             [rows] * 3,
             20 * SWEEPS * rows * NX * CZ,
             info,
@@ -371,17 +381,24 @@
             state,
             halo_i,
             halo_x,
+            *((coarse_start,) if last else ()),
         )
-        states.append(state)
-    value, edge_i, edge_x = call(functools.partial(jump_kernel, ROWS), [tile()] * 3, [], 0, info, state, coarse_start)
+        if last:
+            state, value, edge_i, edge_x = results
+        else:
+            state, edge_i, edge_x = results
+            states.append(state)
+
     moved = 0
     for level, distance in enumerate(DISTANCES):
         halo_i, halo_x = swap_halos(edge_i, edge_x)
         arrived = earlier(value, distance)
         height = min(2 * distance, ROWS)
         product, power = value, distance
+        if distance == 2:
+            final = by_cell([state], early[:1, 0])
         if distance == 8:
-            product, edge_i, edge_x = coarse(4, ROWS, 0, value, halo_i, halo_x, edges=2)
+            product, edge_i, edge_x = coarse(4, ROWS, 0, value, halo_i, halo_x, ROWS)
             halo_i, halo_x = swap_halos(edge_i, edge_x)
             power = 4
         (product,) = coarse(power, height, 0, product, halo_i, halo_x)
@@ -396,13 +413,8 @@
                 arrived,
                 product,
             )
-            if DISTANCES[level + 1] == 4:
-                value, edge_i, edge_x, late, early = lax.optimization_barrier(
-                    (value, edge_i, edge_x, states[-1], early)
-                )
         moved += distance
 
-    final = by_cell([late])
     table = dft_table(jnp.arange(total, dtype=jnp.int32), total, total // 2).reshape(total, LINE, STEPS)
     first_steps = table[:, :, : STEPS - 1].reshape(total, -1)
     spectrum = jnp.einsum("kt,txyz->kxyz", first_steps, z_difference(early), precision=lax.Precision.HIGHEST)
@@ -410,7 +422,8 @@
     spectrum += jnp.einsum("kt,txyz->kxyz", last_step, z_difference(final), precision=lax.Precision.HIGHEST)
     sums = loss_sums(spectrum, total)
 
-    arrived, sums = lax.optimization_barrier((arrived, sums))
+    route = [(m * LINE + t, t * LINE + BLOCK_OF[m]) for m in range(LINE) for t in range(LINE)]
+    sums = lax.ppermute(sums, ("mesh", "tm"), route)
     (out,) = call(
         functools.partial(final_kernel, DISTANCES[-1], moved - DISTANCES[-1]),
         [shape(NX * ROWS, CZ)],
@@ -421,8 +434,6 @@
         product,
     )
     out = lax.all_to_all(out.reshape(LINE, 4, ROWS, CZ), "mesh", 0, 0, tiled=True)
-    route = [(m * LINE + t, t * LINE + BLOCK_OF[m]) for m in range(LINE) for t in range(LINE)]
-    sums = lax.ppermute(sums, ("mesh", "tm"), route)
     loss_density = jnp.sum(loss_coeffs * sums, axis=0)
     (next_start,) = call(lay_out_kernel, [shape(1, 4, LINE * ROWS, CZ)], [], 0, out)
     return next_start, loss_density

time: 180 us -> 187 us (1.039)
  the two profiles are of different devices: /device:TPU:20 before, /device:TPU:28 now
where the time goes in v4:
time: 187 us; the launch traced here: 186 us
  starting transfers between devices  77.2 us (41%)
  waiting for transfers between devices  66.1 us (35%)
  Pallas kernels  30.2 us (16%)
  other arithmetic  4.12 us (2%)
  local copies, waits for them, and re-layouts  3.21 us (2%)
  between operations  3.04 us (2%)
  matrix products  2.11 us (1%)
    ppermute x9, waiting for transfers between devices, swap_halos(): halo_x = lax.ppermute(edge_x, 'mesh', outer)  40.4 us
    ppermute x9, starting transfers between devices, swap_halos(): halo_x = lax.ppermute(edge_x, 'mesh', outer)  30.6 us
    pallas_call x18, Pallas kernels, call(): pl.pallas_call(kernel, out_shape=outs, in_specs=[pl.BlockSpec(memory_spac...  27.8 us
    all_to_all x2, starting transfers between devices, by_cell(): lax.all_to_all(packed.reshape(LINE, count, 4, ROWS, CZ), 'tm', 0, 0, tile...  16.2 us
    ppermute x4, starting transfers between devices, earlier(): lax.ppermute(value, 'tm', [(n, (n - distance) % LINE) for n in range(LINE)])  11.9 us
    ppermute x1, waiting for transfers between devices, iteration(): sums = lax.ppermute(sums, ('mesh', 'tm'), route)  10.7 us
    all_to_all x1, starting transfers between devices, iteration(): packed = lax.all_to_all(fields, 'mesh', 0, 0, tiled=True)  7.13 us
    all_to_all x1, starting transfers between devices, iteration(): lax.all_to_all(out.reshape(LINE, 4, ROWS, CZ), 'mesh', 0, 0, tiled=True)  6.93 us
  transfers between devices with their start and end apart: 27, of which 12 were waited for; matrix products, arithmetic and copies ran while one was open for 4% of the time, Pallas kernels for 11%

profile of v4, /device:TPU:28, one launch (start us, length us, event | category | flops | bytes accessed | tf_op | source)
XLA Modules:
  0.0 186.0 jit_solution(14532813597507357425)
XLA Ops:
  0.6 2.4 %shard_map.77 = f32[16,4,3,8,128]{4,3,2,1,0:T(8,128)} custom-call(f32[4,128,128]{2,1,0:T(8,128)} %cond.1, f32[4,128,128]{2,1,0:T(8,128)} %coil.1, f32[4,128,128]{2,1,0:T(8,128)} %bitcast.33), custom_call_target="tpu_custom_call" | custom-call | tf_op jit(solution)/shard_map/pallas_call | solution.py:243
  3.1 7.1 %all-to-all-start = ((f32[16,4,3,8,128]{4,3,2,1,0:T(8,128)}), f32[16,4,3,8,128]{4,3,2,1,0:T(8,128)S(1)}, u32[]{:S(2)}, u32[]{:S(2)}) async-start(f32[16,4,3,8,128]{4,3,2,1,0:T(8,128)} %shard_map.77), calls=%async_computation | async-start | bytes 1572864 | tf_op jit(solution)/shard_map/all_to_all | solution.py:328
  14.8 6.0 %all-to-all-done = f32[16,4,3,8,128]{4,3,2,1,0:T(8,128)S(1)} async-done(((f32[16,4,3,8,128]{4,3,2,1,0:T(8,128)}), f32[16,4,3,8,128]{4,3,2,1,0:T(8,128)S(1)}, u32[]{:S(2)}, u32[]{:S(2)}) %all-to-all-start) | async-done | bytes 786464 | tf_op jit(solution)/shard_map/all_to_all | solution.py:328
  22.0 4.6 %collective-permute-start.1 = (f32[18,64,128]{2,1,0:T(8,128)S(1)}, f32[18,64,128]{2,1,0:T(8,128)S(1)}, u32[]{:S(2)}, u32[]{:S(2)}) collective-permute-start(f32[18,64,128]{2,1,0:T(8,128)S(1)} %get-tuple-element.38), channel_id=1, source_target_pairs={{16,32},{32,16},{48,64},{64,48},{80,96},{96,80},{112,224},{224,112... | collective-permute-start | bytes 1769480 | tf_op jit(solution)/shard_map/ppermute | solution.py:280
  26.6 8.1 %collective-permute-done.1.halo_x = f32[18,64,128]{2,1,0:T(8,128)S(1)} collective-permute-done((f32[18,64,128]{2,1,0:T(8,128)S(1)}, f32[18,64,128]{2,1,0:T(8,128)S(1)}, u32[]{:S(2)}, u32[]{:S(2)}) %collective-permute-start.1) | collective-permute-done | bytes 589856 | tf_op jit(solution)/shard_map/ppermute | solution.py:280
  34.7 2.1 %shard_map.79 = (f32[8,64,128]{2,1,0:T(8,128)S(1)}, f32[5,64,128]{2,1,0:T(8,128)S(1)}, f32[5,64,128]{2,1,0:T(8,128)S(1)}, f32[24,64,128]{2,1,0:T(8,128)S(1)}, f32[18,64,128]{2,1,0:T(8,128)S(1)}) custom-call(s32[7]{0:T(128)S(1)} %pad_add_fusion.info, f32[8,64,128]{2,1,0:T(8,128)S(1)} %get-tuple-element.34.cond, f32[8,64,128]{2,1,0:T(8,128)S(1)} %get-tuple-element.35.coil, ...), custom_call_target="tpu_custom_call" | custom-call | flops 14745600 | bytes 3932188 | tf_op jit(solution)/shard_map/pallas_call | solution.py:264
  36.9 4.6 %collective-permute-start.3 = (f32[5,64,128]{2,1,0:T(8,128)S(1)}, f32[5,64,128]{2,1,0:T(8,128)S(1)}, u32[]{:S(2)}, u32[]{:S(2)}) collective-permute-start(f32[5,64,128]{2,1,0:T(8,128)S(1)} %get-tuple-element.43), channel_id=1, source_target_pairs={{16,32},{32,16},{48,64},{64,48},{80,96},{96,80},{112,224},{224,112... | collective-permute-start | bytes 491528 | tf_op jit(solution)/shard_map/ppermute | solution.py:280
  41.6 3.5 %collective-permute-done.3.halo_x = f32[5,64,128]{2,1,0:T(8,128)S(1)} collective-permute-done((f32[5,64,128]{2,1,0:T(8,128)S(1)}, f32[5,64,128]{2,1,0:T(8,128)S(1)}, u32[]{:S(2)}, u32[]{:S(2)}) %collective-permute-start.3) | collective-permute-done | bytes 163872 | tf_op jit(solution)/shard_map/ppermute | solution.py:280
  45.1 2.1 %shard_map.80 = (f32[8,64,128]{2,1,0:T(8,128)S(1)}, f32[5,64,128]{2,1,0:T(8,128)S(1)}, f32[5,64,128]{2,1,0:T(8,128)S(1)}) custom-call(s32[7]{0:T(128)S(1)} %pad_add_fusion.info, f32[24,64,128]{2,1,0:T(8,128)S(1)} %get-tuple-element.39.cond, f32[18,64,128]{2,1,0:T(8,128)S(1)} %get-tuple-element.40.coil, f32[8,64,128]{2,1,0:T(8,128)S(1)} %get-tuple-element.41.own.refs_0_, ...), custom_call_target="tpu_custom_call" | custom-call | flops 14745600 | bytes 2555932 | tf_op jit(solution)/shard_map/pallas_call | solution.py:264
  47.3 4.6 %collective-permute-start.5 = (f32[5,64,128]{2,1,0:T(8,128)S(1)}, f32[5,64,128]{2,1,0:T(8,128)S(1)}, u32[]{:S(2)}, u32[]{:S(2)}) collective-permute-start(f32[5,64,128]{2,1,0:T(8,128)S(1)} %get-tuple-element.46), channel_id=1, source_target_pairs={{16,32},{32,16},{48,64},{64,48},{80,96},{96,80},{112,224},{224,112... | collective-permute-start | bytes 491528 | tf_op jit(solution)/shard_map/ppermute | solution.py:280
  51.9 3.5 %collective-permute-done.5.halo_x = f32[5,64,128]{2,1,0:T(8,128)S(1)} collective-permute-done((f32[5,64,128]{2,1,0:T(8,128)S(1)}, f32[5,64,128]{2,1,0:T(8,128)S(1)}, u32[]{:S(2)}, u32[]{:S(2)}) %collective-permute-start.5) | collective-permute-done | bytes 163872 | tf_op jit(solution)/shard_map/ppermute | solution.py:280
  55.4 2.1 %shard_map.81 = (f32[8,64,128]{2,1,0:T(8,128)S(1)}, f32[5,64,128]{2,1,0:T(8,128)S(1)}, f32[5,64,128]{2,1,0:T(8,128)S(1)}) custom-call(s32[7]{0:T(128)S(1)} %pad_add_fusion.info, f32[24,64,128]{2,1,0:T(8,128)S(1)} %get-tuple-element.39.cond, f32[18,64,128]{2,1,0:T(8,128)S(1)} %get-tuple-element.40.coil, f32[8,64,128]{2,1,0:T(8,128)S(1)} %get-tuple-element.44.own.refs_1_, ...), custom_call_target="tpu_custom_call" | custom-call | flops 14745600 | bytes 2555932 | tf_op jit(solution)/shard_map/pallas_call | solution.py:264
  58.6 9.2 %all-to-all-start.2 = ((f32[16,3,4,8,128]{4,3,2,1,0:T(8,128)}), f32[16,3,4,8,128]{4,3,2,1,0:T(8,128)}, u32[]{:S(2)}, u32[]{:S(2)}) async-start(f32[16,3,4,8,128]{4,3,2,1,0:T(8,128)} %bitcast.7), calls=%async_computation.2 | async-start | bytes 1572864 | tf_op jit(solution)/shard_map/all_to_all | solution.py:316
  67.9 3.8 %collective-permute-start.7 = (f32[5,64,128]{2,1,0:T(8,128)S(1)}, f32[5,64,128]{2,1,0:T(8,128)S(1)}, u32[]{:S(2)}, u32[]{:S(2)}) collective-permute-start(f32[5,64,128]{2,1,0:T(8,128)S(1)} %get-tuple-element.49), channel_id=1, source_target_pairs={{16,32},{32,16},{48,64},{64,48},{80,96},{96,80},{112,224},{224,112... | collective-permute-start | bytes 491528 | tf_op jit(solution)/shard_map/ppermute | solution.py:280
  72.8 3.3 %collective-permute-done.7.halo_x = f32[5,64,128]{2,1,0:T(8,128)S(1)} collective-permute-done((f32[5,64,128]{2,1,0:T(8,128)S(1)}, f32[5,64,128]{2,1,0:T(8,128)S(1)}, u32[]{:S(2)}, u32[]{:S(2)}) %collective-permute-start.7) | collective-permute-done | bytes 163872 | tf_op jit(solution)/shard_map/ppermute | solution.py:280
  78.1 4.0 %collective-permute-start.8 = (f32[8,64,128]{2,1,0:T(8,128)S(1)}, f32[8,64,128]{2,1,0:T(8,128)S(1)}, u32[]{:S(2)}, u32[]{:S(2)}) collective-permute-start(f32[8,64,128]{2,1,0:T(8,128)S(1)} %get-tuple-element.50.own), channel_id=1, source_target_pairs={{0,15},{1,0},{2,1},{3,2},{4,3},{5,4},{6,5},{7,6},{8,7},{9,8},{10,9... | collective-permute-start | bytes 786440 | tf_op jit(solution)/shard_map/ppermute | solution.py:286
  82.1 5.0 %collective-permute-start.10 = (f32[2,64,128]{2,1,0:T(8,128)S(1)}, f32[2,64,128]{2,1,0:T(8,128)S(1)}, u32[]{:S(2)}, u32[]{:S(2)}) collective-permute-start(f32[2,64,128]{2,1,0:T(8,128)S(1)} %get-tuple-element.52), channel_id=1, source_target_pairs={{16,32},{32,16},{48,64},{64,48},{80,96},{96,80},{112,224},{224,112... | collective-permute-start | bytes 196616 | tf_op jit(solution)/shard_map/ppermute | solution.py:280
  87.1 9.3 %collective-permute-done.10.halo_x = f32[2,64,128]{2,1,0:T(8,128)S(1)} collective-permute-done((f32[2,64,128]{2,1,0:T(8,128)S(1)}, f32[2,64,128]{2,1,0:T(8,128)S(1)}, u32[]{:S(2)}, u32[]{:S(2)}) %collective-permute-start.10) | collective-permute-done | bytes 65568 | tf_op jit(solution)/shard_map/ppermute | solution.py:280
  100.6 5.9 %collective-permute-done.13.halo_x = f32[4,64,128]{2,1,0:T(8,128)S(1)} collective-permute-done((f32[4,64,128]{2,1,0:T(8,128)S(1)}, f32[4,64,128]{2,1,0:T(8,128)S(1)}, u32[]{:S(2)}, u32[]{:S(2)}) %collective-permute-start.13) | collective-permute-done | bytes 131104 | tf_op jit(solution)/shard_map/ppermute | solution.py:280
  110.7 2.4 %collective-permute-start.14 = (f32[8,64,128]{2,1,0:T(8,128)S(1)}, f32[8,64,128]{2,1,0:T(8,128)S(1)}, u32[]{:S(2)}, u32[]{:S(2)}) collective-permute-start(f32[8,64,128]{2,1,0:T(8,128)S(1)} %get-tuple-element.56.own), channel_id=1, source_target_pairs={{0,12},{1,13},{2,14},{3,15},{4,0},{5,1},{6,2},{7,3},{8,4},{9,5},{1... | collective-permute-start | bytes 786440 | tf_op jit(solution)/shard_map/ppermute | solution.py:286
  113.1 4.8 %collective-permute-done.16.halo_x = f32[8,64,128]{2,1,0:T(8,128)S(1)} collective-permute-done((f32[8,64,128]{2,1,0:T(8,128)S(1)}, f32[8,64,128]{2,1,0:T(8,128)S(1)}, u32[]{:S(2)}, u32[]{:S(2)}) %collective-permute-start.16) | collective-permute-done | bytes 262176 | tf_op jit(solution)/shard_map/ppermute | solution.py:280
  117.9 3.1 %shard_map.88.product = f32[8,64,128]{2,1,0:T(8,128)S(1)} custom-call(s32[7]{0:T(128)S(1)} %pad_add_fusion.info, f32[24,64,128]{2,1,0:T(8,128)S(1)} %get-tuple-element.39.cond, f32[8,64,128]{2,1,0:T(8,128)S(1)} %get-tuple-element.56.own, f32[8,64,128]{2,1,0:T(8,128)S(1)} %collective-permute-done.15.halo_i, f32[8,64,128]{2,1,0:T(8,128)S(1)} %collective-permute-done.16.halo_x), custom_call_target="tpu_custom_call" | custom-call | flops 31457280 | bytes 1835036 | tf_op jit(solution)/shard_map/pallas_call | solution.py:264
  121.0 5.0 %collective-permute-done.14.arrived = f32[8,64,128]{2,1,0:T(8,128)S(1)} collective-permute-done((f32[8,64,128]{2,1,0:T(8,128)S(1)}, f32[8,64,128]{2,1,0:T(8,128)S(1)}, u32[]{:S(2)}, u32[]{:S(2)}) %collective-permute-start.14) | collective-permute-done | bytes 262176 | tf_op jit(solution)/shard_map/ppermute | solution.py:286
  129.1 4.8 %collective-permute-start.17 = (f32[8,64,128]{2,1,0:T(8,128)S(1)}, f32[8,64,128]{2,1,0:T(8,128)S(1)}, u32[]{:S(2)}, u32[]{:S(2)}) collective-permute-start(f32[8,64,128]{2,1,0:T(8,128)S(1)} %get-tuple-element.59.own), channel_id=1, source_target_pairs={{0,8},{1,9},{2,10},{3,11},{4,12},{5,13},{6,14},{7,15},{8,0},{9,1},... | collective-permute-start | bytes 786440 | tf_op jit(solution)/shard_map/ppermute | solution.py:286
  133.8 2.1 %collective-permute-done.19.halo_x = f32[8,64,128]{2,1,0:T(8,128)S(1)} collective-permute-done((f32[8,64,128]{2,1,0:T(8,128)S(1)}, f32[8,64,128]{2,1,0:T(8,128)S(1)}, u32[]{:S(2)}, u32[]{:S(2)}) %collective-permute-start.19) | collective-permute-done | bytes 262176 | tf_op jit(solution)/shard_map/ppermute | solution.py:280
  136.0 3.1 %shard_map.90 = (f32[8,64,128]{2,1,0:T(8,128)S(1)}, f32[8,64,128]{2,1,0:T(8,128)S(1)}, f32[8,64,128]{2,1,0:T(8,128)S(1)}) custom-call(s32[7]{0:T(128)S(1)} %pad_add_fusion.info, f32[24,64,128]{2,1,0:T(8,128)S(1)} %get-tuple-element.39.cond, f32[8,64,128]{2,1,0:T(8,128)S(1)} %get-tuple-element.59.own, f32[8,64,128]{2,1,0:T(8,128)S(1)} %collective-permute-done.18.halo_i, ...), custom_call_target="tpu_custom_call" | custom-call | flops 31457280 | bytes 2359324 | tf_op jit(solution)/shard_map/pallas_call | solution.py:264
  142.7 7.0 %all-to-all-start.3 = ((f32[16,1,4,8,128]{4,3,2,1,0:T(8,128)}), f32[16,1,4,8,128]{4,3,2,1,0:T(8,128)S(1)}, u32[]{:S(2)}, u32[]{:S(2)}) async-start(f32[16,1,4,8,128]{4,3,2,1,0:T(8,128)} %bitcast.14), calls=%async_computation.3 | async-start | bytes 524288 | tf_op jit(solution)/shard_map/all_to_all | solution.py:316
  149.9 3.1 %shard_map.91.product = f32[8,64,128]{2,1,0:T(8,128)S(1)} custom-call(s32[7]{0:T(128)S(1)} %pad_add_fusion.info, f32[24,64,128]{2,1,0:T(8,128)S(1)} %get-tuple-element.39.cond, f32[8,64,128]{2,1,0:T(8,128)S(1)} %get-tuple-element.62.own, f32[8,64,128]{2,1,0:T(8,128)S(1)} %collective-permute-done.20.halo_i, f32[8,64,128]{2,1,0:T(8,128)S(1)} %collective-permute-done.21.halo_x), custom_call_target="tpu_custom_call" | custom-call | flops 31457280 | bytes 1835036 | tf_op jit(solution)/shard_map/pallas_call | solution.py:264
  156.6 3.9 %all-to-all-done.3 = f32[16,1,4,8,128]{4,3,2,1,0:T(8,128)S(1)} async-done(((f32[16,1,4,8,128]{4,3,2,1,0:T(8,128)}), f32[16,1,4,8,128]{4,3,2,1,0:T(8,128)S(1)}, u32[]{:S(2)}, u32[]{:S(2)}) %all-to-all-start.3) | async-done | bytes 262176 | tf_op jit(solution)/shard_map/all_to_all | solution.py:316
  160.5 6.9 %all-to-all-start.1 = ((f32[16,4,8,128]{3,2,1,0:T(8,128)}), f32[16,4,8,128]{3,2,1,0:T(8,128)S(1)}, u32[]{:S(2)}, u32[]{:S(2)}) async-start(f32[16,4,8,128]{3,2,1,0:T(8,128)} %bitcast.5), calls=%async_computation.1 | async-start | bytes 524288 | tf_op jit(solution)/shard_map/all_to_all | solution.py:436
  170.5 3.5 %collective-permute-start.22 = (f32[3,4,8,128]{3,2,1,0:T(8,128)S(1)}, f32[3,4,8,128]{3,2,1,0:T(8,128)S(1)}, u32[]{:S(2)}, u32[]{:S(2)}) collective-permute-start(f32[3,4,8,128]{3,2,1,0:T(8,128)S(1)} %pad_maximum_fusion), channel_id=1, source_target_pairs={{0,0},{1,16},{2,32},{3,48},{4,64},{5,80},{6,96},{7,112},{8,128},{9... | collective-permute-start | bytes 147464 | tf_op jit(solution)/shard_map/ppermute | solution.py:426
  174.7 10.7 %collective-permute-done.22 = f32[3,4,8,128]{3,2,1,0:T(8,128)S(1)} collective-permute-done((f32[3,4,8,128]{3,2,1,0:T(8,128)S(1)}, f32[3,4,8,128]{3,2,1,0:T(8,128)S(1)}, u32[]{:S(2)}, u32[]{:S(2)}) %collective-permute-start.22) | collective-permute-done | bytes 49184 | tf_op jit(solution)/shard_map/ppermute | solution.py:426
  (67 shorter events, 31.2 us)
Async XLA Ops:
  3.1 17.7 %all-to-all-start = ((f32[16,4,3,8,128]{4,3,2,1,0:T(8,128)}), f32[16,4,3,8,128]{4,3,2,1,0:T(8,128)S(1)}, u32[]{:S(2)}, u32[]{:S(2)}) async-start(f32[16,4,3,8,128]{4,3,2,1,0:T(8,128)} %shard_map.77), calls=%async_computation | async-start | bytes 1572864 | tf_op jit(solution)/shard_map/all_to_all | solution.py:328
  10.2 0.7 copy-start.2
  13.4 0.7 copy-start.1
  21.5 5.1 %collective-permute-start = (f32[18,64,128]{2,1,0:T(8,128)S(1)}, f32[18,64,128]{2,1,0:T(8,128)S(1)}, u32[]{:S(2)}, u32[]{:S(2)}) collective-permute-start(f32[18,64,128]{2,1,0:T(8,128)S(1)} %get-tuple-element.37), channel_id=1, source_target_pairs={{0,16},{16,0},{32,48},{48,32},{64,80},{80,64},{96,112},{112,96},{1... | collective-permute-start | bytes 1769480 | tf_op jit(solution)/shard_map/ppermute | solution.py:281
  22.0 12.7 %collective-permute-start.1 = (f32[18,64,128]{2,1,0:T(8,128)S(1)}, f32[18,64,128]{2,1,0:T(8,128)S(1)}, u32[]{:S(2)}, u32[]{:S(2)}) collective-permute-start(f32[18,64,128]{2,1,0:T(8,128)S(1)} %get-tuple-element.38), channel_id=1, source_target_pairs={{16,32},{32,16},{48,64},{64,48},{80,96},{96,80},{112,224},{224,112... | collective-permute-start | bytes 1769480 | tf_op jit(solution)/shard_map/ppermute | solution.py:280
  36.8 4.7 %collective-permute-start.2 = (f32[5,64,128]{2,1,0:T(8,128)S(1)}, f32[5,64,128]{2,1,0:T(8,128)S(1)}, u32[]{:S(2)}, u32[]{:S(2)}) collective-permute-start(f32[5,64,128]{2,1,0:T(8,128)S(1)} %get-tuple-element.42), channel_id=1, source_target_pairs={{0,16},{16,0},{32,48},{48,32},{64,80},{80,64},{96,112},{112,96},{1... | collective-permute-start | bytes 491528 | tf_op jit(solution)/shard_map/ppermute | solution.py:281
  36.9 8.1 %collective-permute-start.3 = (f32[5,64,128]{2,1,0:T(8,128)S(1)}, f32[5,64,128]{2,1,0:T(8,128)S(1)}, u32[]{:S(2)}, u32[]{:S(2)}) collective-permute-start(f32[5,64,128]{2,1,0:T(8,128)S(1)} %get-tuple-element.43), channel_id=1, source_target_pairs={{16,32},{32,16},{48,64},{64,48},{80,96},{96,80},{112,224},{224,112... | collective-permute-start | bytes 491528 | tf_op jit(solution)/shard_map/ppermute | solution.py:280
  47.2 4.7 %collective-permute-start.4 = (f32[5,64,128]{2,1,0:T(8,128)S(1)}, f32[5,64,128]{2,1,0:T(8,128)S(1)}, u32[]{:S(2)}, u32[]{:S(2)}) collective-permute-start(f32[5,64,128]{2,1,0:T(8,128)S(1)} %get-tuple-element.45), channel_id=1, source_target_pairs={{0,16},{16,0},{32,48},{48,32},{64,80},{80,64},{96,112},{112,96},{1... | collective-permute-start | bytes 491528 | tf_op jit(solution)/shard_map/ppermute | solution.py:281
  47.3 8.1 %collective-permute-start.5 = (f32[5,64,128]{2,1,0:T(8,128)S(1)}, f32[5,64,128]{2,1,0:T(8,128)S(1)}, u32[]{:S(2)}, u32[]{:S(2)}) collective-permute-start(f32[5,64,128]{2,1,0:T(8,128)S(1)} %get-tuple-element.46), channel_id=1, source_target_pairs={{16,32},{32,16},{48,64},{64,48},{80,96},{96,80},{112,224},{224,112... | collective-permute-start | bytes 491528 | tf_op jit(solution)/shard_map/ppermute | solution.py:280
  58.6 82.6 %all-to-all-start.2 = ((f32[16,3,4,8,128]{4,3,2,1,0:T(8,128)}), f32[16,3,4,8,128]{4,3,2,1,0:T(8,128)}, u32[]{:S(2)}, u32[]{:S(2)}) async-start(f32[16,3,4,8,128]{4,3,2,1,0:T(8,128)} %bitcast.7), calls=%async_computation.2 | async-start | bytes 1572864 | tf_op jit(solution)/shard_map/all_to_all | solution.py:316
  67.8 5.0 %collective-permute-start.6 = (f32[5,64,128]{2,1,0:T(8,128)S(1)}, f32[5,64,128]{2,1,0:T(8,128)S(1)}, u32[]{:S(2)}, u32[]{:S(2)}) collective-permute-start(f32[5,64,128]{2,1,0:T(8,128)S(1)} %get-tuple-element.48), channel_id=1, source_target_pairs={{0,16},{16,0},{32,48},{48,32},{64,80},{80,64},{96,112},{112,96},{1... | collective-permute-start | bytes 491528 | tf_op jit(solution)/shard_map/ppermute | solution.py:281
  67.9 8.1 %collective-permute-start.7 = (f32[5,64,128]{2,1,0:T(8,128)S(1)}, f32[5,64,128]{2,1,0:T(8,128)S(1)}, u32[]{:S(2)}, u32[]{:S(2)}) collective-permute-start(f32[5,64,128]{2,1,0:T(8,128)S(1)} %get-tuple-element.49), channel_id=1, source_target_pairs={{16,32},{32,16},{48,64},{64,48},{80,96},{96,80},{112,224},{224,112... | collective-permute-start | bytes 491528 | tf_op jit(solution)/shard_map/ppermute | solution.py:280
  78.1 19.3 %collective-permute-start.8 = (f32[8,64,128]{2,1,0:T(8,128)S(1)}, f32[8,64,128]{2,1,0:T(8,128)S(1)}, u32[]{:S(2)}, u32[]{:S(2)}) collective-permute-start(f32[8,64,128]{2,1,0:T(8,128)S(1)} %get-tuple-element.50.own), channel_id=1, source_target_pairs={{0,15},{1,0},{2,1},{3,2},{4,3},{5,4},{6,5},{7,6},{8,7},{9,8},{10,9... | collective-permute-start | bytes 786440 | tf_op jit(solution)/shard_map/ppermute | solution.py:286
  82.1 5.0 %collective-permute-start.9 = (f32[2,64,128]{2,1,0:T(8,128)S(1)}, f32[2,64,128]{2,1,0:T(8,128)S(1)}, u32[]{:S(2)}, u32[]{:S(2)}) collective-permute-start(f32[2,64,128]{2,1,0:T(8,128)S(1)} %get-tuple-element.51), channel_id=1, source_target_pairs={{0,16},{16,0},{32,48},{48,32},{64,80},{80,64},{96,112},{112,96},{1... | collective-permute-start | bytes 196616 | tf_op jit(solution)/shard_map/ppermute | solution.py:281
  82.1 14.3 %collective-permute-start.10 = (f32[2,64,128]{2,1,0:T(8,128)S(1)}, f32[2,64,128]{2,1,0:T(8,128)S(1)}, u32[]{:S(2)}, u32[]{:S(2)}) collective-permute-start(f32[2,64,128]{2,1,0:T(8,128)S(1)} %get-tuple-element.52), channel_id=1, source_target_pairs={{16,32},{32,16},{48,64},{64,48},{80,96},{96,80},{112,224},{224,112... | collective-permute-start | bytes 196616 | tf_op jit(solution)/shard_map/ppermute | solution.py:280
  98.0 10.0 %collective-permute-start.11 = (f32[8,64,128]{2,1,0:T(8,128)S(1)}, f32[8,64,128]{2,1,0:T(8,128)S(1)}, u32[]{:S(2)}, u32[]{:S(2)}) collective-permute-start(f32[8,64,128]{2,1,0:T(8,128)S(1)} %get-tuple-element.53.own), channel_id=1, source_target_pairs={{0,14},{1,15},{2,0},{3,1},{4,2},{5,3},{6,4},{7,5},{8,6},{9,7},{10,... | collective-permute-start | bytes 786440 | tf_op jit(solution)/shard_map/ppermute | solution.py:286
  98.7 1.9 %collective-permute-start.12 = (f32[4,64,128]{2,1,0:T(8,128)S(1)}, f32[4,64,128]{2,1,0:T(8,128)S(1)}, u32[]{:S(2)}, u32[]{:S(2)}) collective-permute-start(f32[4,64,128]{2,1,0:T(8,128)S(1)} %get-tuple-element.54), channel_id=1, source_target_pairs={{0,16},{16,0},{32,48},{48,32},{64,80},{80,64},{96,112},{112,96},{1... | collective-permute-start | bytes 393224 | tf_op jit(solution)/shard_map/ppermute | solution.py:281
  98.7 7.8 %collective-permute-start.13 = (f32[4,64,128]{2,1,0:T(8,128)S(1)}, f32[4,64,128]{2,1,0:T(8,128)S(1)}, u32[]{:S(2)}, u32[]{:S(2)}) collective-permute-start(f32[4,64,128]{2,1,0:T(8,128)S(1)} %get-tuple-element.55), channel_id=1, source_target_pairs={{16,32},{32,16},{48,64},{64,48},{80,96},{96,80},{112,224},{224,112... | collective-permute-start | bytes 393224 | tf_op jit(solution)/shard_map/ppermute | solution.py:280
  108.6 4.5 %collective-permute-start.15 = (f32[8,64,128]{2,1,0:T(8,128)S(1)}, f32[8,64,128]{2,1,0:T(8,128)S(1)}, u32[]{:S(2)}, u32[]{:S(2)}) collective-permute-start(f32[8,64,128]{2,1,0:T(8,128)S(1)} %get-tuple-element.57), channel_id=1, source_target_pairs={{0,16},{16,0},{32,48},{48,32},{64,80},{80,64},{96,112},{112,96},{1... | collective-permute-start | bytes 786440 | tf_op jit(solution)/shard_map/ppermute | solution.py:281
  108.7 9.2 %collective-permute-start.16 = (f32[8,64,128]{2,1,0:T(8,128)S(1)}, f32[8,64,128]{2,1,0:T(8,128)S(1)}, u32[]{:S(2)}, u32[]{:S(2)}) collective-permute-start(f32[8,64,128]{2,1,0:T(8,128)S(1)} %get-tuple-element.58), channel_id=1, source_target_pairs={{16,32},{32,16},{48,64},{64,48},{80,96},{96,80},{112,224},{224,112... | collective-permute-start | bytes 786440 | tf_op jit(solution)/shard_map/ppermute | solution.py:280
  110.7 15.4 %collective-permute-start.14 = (f32[8,64,128]{2,1,0:T(8,128)S(1)}, f32[8,64,128]{2,1,0:T(8,128)S(1)}, u32[]{:S(2)}, u32[]{:S(2)}) collective-permute-start(f32[8,64,128]{2,1,0:T(8,128)S(1)} %get-tuple-element.56.own), channel_id=1, source_target_pairs={{0,12},{1,13},{2,14},{3,15},{4,0},{5,1},{6,2},{7,3},{8,4},{9,5},{1... | collective-permute-start | bytes 786440 | tf_op jit(solution)/shard_map/ppermute | solution.py:286
  126.7 7.2 %collective-permute-start.18 = (f32[8,64,128]{2,1,0:T(8,128)S(1)}, f32[8,64,128]{2,1,0:T(8,128)S(1)}, u32[]{:S(2)}, u32[]{:S(2)}) collective-permute-start(f32[8,64,128]{2,1,0:T(8,128)S(1)} %get-tuple-element.60), channel_id=1, source_target_pairs={{0,16},{16,0},{32,48},{48,32},{64,80},{80,64},{96,112},{112,96},{1... | collective-permute-start | bytes 786440 | tf_op jit(solution)/shard_map/ppermute | solution.py:281
  126.8 9.2 %collective-permute-start.19 = (f32[8,64,128]{2,1,0:T(8,128)S(1)}, f32[8,64,128]{2,1,0:T(8,128)S(1)}, u32[]{:S(2)}, u32[]{:S(2)}) collective-permute-start(f32[8,64,128]{2,1,0:T(8,128)S(1)} %get-tuple-element.61), channel_id=1, source_target_pairs={{16,32},{32,16},{48,64},{64,48},{80,96},{96,80},{112,224},{224,112... | collective-permute-start | bytes 786440 | tf_op jit(solution)/shard_map/ppermute | solution.py:280
  129.1 24.0 %collective-permute-start.17 = (f32[8,64,128]{2,1,0:T(8,128)S(1)}, f32[8,64,128]{2,1,0:T(8,128)S(1)}, u32[]{:S(2)}, u32[]{:S(2)}) collective-permute-start(f32[8,64,128]{2,1,0:T(8,128)S(1)} %get-tuple-element.59.own), channel_id=1, source_target_pairs={{0,8},{1,9},{2,10},{3,11},{4,12},{5,13},{6,14},{7,15},{8,0},{9,1},... | collective-permute-start | bytes 786440 | tf_op jit(solution)/shard_map/ppermute | solution.py:286
  139.1 10.8 %collective-permute-start.20 = (f32[8,64,128]{2,1,0:T(8,128)S(1)}, f32[8,64,128]{2,1,0:T(8,128)S(1)}, u32[]{:S(2)}, u32[]{:S(2)}) collective-permute-start(f32[8,64,128]{2,1,0:T(8,128)S(1)} %get-tuple-element.63), channel_id=1, source_target_pairs={{0,16},{16,0},{32,48},{48,32},{64,80},{80,64},{96,112},{112,96},{1... | collective-permute-start | bytes 786440 | tf_op jit(solution)/shard_map/ppermute | solution.py:281
  139.2 10.7 %collective-permute-start.21 = (f32[8,64,128]{2,1,0:T(8,128)S(1)}, f32[8,64,128]{2,1,0:T(8,128)S(1)}, u32[]{:S(2)}, u32[]{:S(2)}) collective-permute-start(f32[8,64,128]{2,1,0:T(8,128)S(1)} %get-tuple-element.64), channel_id=1, source_target_pairs={{16,32},{32,16},{48,64},{64,48},{80,96},{96,80},{112,224},{224,112... | collective-permute-start | bytes 786440 | tf_op jit(solution)/shard_map/ppermute | solution.py:280
  142.7 17.8 %all-to-all-start.3 = ((f32[16,1,4,8,128]{4,3,2,1,0:T(8,128)}), f32[16,1,4,8,128]{4,3,2,1,0:T(8,128)S(1)}, u32[]{:S(2)}, u32[]{:S(2)}) async-start(f32[16,1,4,8,128]{4,3,2,1,0:T(8,128)} %bitcast.14), calls=%async_computation.3 | async-start | bytes 524288 | tf_op jit(solution)/shard_map/all_to_all | solution.py:316
  160.5 13.5 %all-to-all-start.1 = ((f32[16,4,8,128]{3,2,1,0:T(8,128)}), f32[16,4,8,128]{3,2,1,0:T(8,128)S(1)}, u32[]{:S(2)}, u32[]{:S(2)}) async-start(f32[16,4,8,128]{3,2,1,0:T(8,128)} %bitcast.5), calls=%async_computation.1 | async-start | bytes 524288 | tf_op jit(solution)/shard_map/all_to_all | solution.py:436
  170.5 14.9 %copy-start = (f32[3,4,8,128]{3,2,1,0:T(8,128)S(1)}, f32[3,4,8,128]{3,2,1,0:T(8,128)}, u32[]{:S(2)}) copy-start(f32[3,4,8,128]{3,2,1,0:T(8,128)} %param.10) | copy-start | bytes 147460
  170.5 14.9 %collective-permute-start.22 = (f32[3,4,8,128]{3,2,1,0:T(8,128)S(1)}, f32[3,4,8,128]{3,2,1,0:T(8,128)S(1)}, u32[]{:S(2)}, u32[]{:S(2)}) collective-permute-start(f32[3,4,8,128]{3,2,1,0:T(8,128)S(1)} %pad_maximum_fusion), channel_id=1, source_target_pairs={{0,0},{1,16},{2,32},{3,48},{4,64},{5,80},{6,96},{7,112},{8,128},{9... | collective-permute-start | bytes 147464 | tf_op jit(solution)/shard_map/ppermute | solution.py:426
